TPU v7x, 256 devices: a whole 4x4x8 slice. The times are simulated.
256 devices in a mesh: tm: 32 (over x, z), space: 8 (over y, core).
Axes of the slice: x: 4, y: 4, z: 8, core: 2. Of those that a mesh axis runs over, the one named last changes fastest.
Arguments:
- density: float32 [128, 512, 512], P('tm', 'space'), may hold values from 0.2 to 2
- flux_x: float32 [128, 512, 512], P('tm', 'space'), may hold values from -5 to 5
- flux_y: float32 [128, 512, 512], P('tm', 'space'), may hold values from -5 to 5
- source: float32 [128, 512, 512], P('tm', 'space'), may hold values from -0.3 to 0.3
Outputs:
- new_density: float32 [128, 512, 512], P('tm', 'space')
- new_flux_x: float32 [128, 512, 512], P('tm', 'space')
- new_flux_y: float32 [128, 512, 512], P('tm', 'space')
- potential: float32 [128, 512, 512], P('tm', 'space')
All inputs are finite; a program needn't handle non-finite values.
Results may differ from a plain program's by a relative error of at most 0.0003.
Values sent between devices are 32-bit elements; how exact they have to be, the bound alone decides.
No kernel may reach another device: no remote copies, remote signals or barrier semaphores. Data moves between devices by JAX's collectives and lax.ppermute only.
A program may use at most 128 MiB of HBM per device.

v0:
```python
import jax
import jax.numpy as jnp
from jax import lax
from jax.sharding import PartitionSpec as P

ITERS = 3
NEWTON = 10


TAU_STEP = 1.0
SLOW_LOOP = 2.25


def shifted_2(block, axis, distance):
    devices = range(lax.axis_size(axis))
    route = [((i - distance) % len(devices), i) for i in devices]
    return lax.ppermute(block, axis, route)


def cosine_matrix(points):
    frequency = jnp.arange(points, dtype=jnp.float32)[:, None]
    sample = jnp.arange(points, dtype=jnp.float32)[None, :]
    scaling = jnp.where(frequency == 0, jnp.sqrt(1.0 / points), jnp.sqrt(2.0 / points))
    return scaling * jnp.cos(jnp.pi * (sample + 0.5) * frequency / points)


def neumann_spectrum(points):
    half_angle = jnp.pi * jnp.arange(points, dtype=jnp.float32) / (2.0 * points)
    sine = jnp.sin(half_angle)
    return 4.0 * sine * sine


def flux_divergence(values):
    points = values.shape[-1]
    inside = jnp.where(jnp.arange(points) < points - 1, values, 0.0)
    before = jnp.concatenate([jnp.zeros_like(values[..., :1]), values[..., :-1]], axis=-1)
    return inside - before


def minus_gradient(values):
    following = jnp.concatenate([values[..., 1:], values[..., -1:]], axis=-1)
    return values - following


def kinetic_prox(mass_in, along_x, along_y):
    target = 0.5 * TAU_STEP * (along_x * along_x + along_y * along_y)
    newton_root = jnp.maximum(mass_in, 0.0) + jnp.cbrt(target)
    for newton_step in range(NEWTON):
        shifted = newton_root + TAU_STEP
        residue = (newton_root - mass_in) * shifted * shifted - target
        derivative = shifted * shifted + 2.0 * (newton_root - mass_in) * shifted
        newton_root = jnp.maximum(newton_root - residue / derivative, 0.0)
    factor = newton_root / (newton_root + TAU_STEP)
    return (newton_root, factor * along_x, factor * along_y)


def neighbour(values, offset):
    return shifted_2(values, "tm", offset)


def local(density, flux_x, flux_y, source):
    highest = lax.Precision.HIGHEST
    steps_local, row_count, grid_width = density.shape
    slab_count = lax.axis_size("tm")
    loop_length = steps_local * slab_count
    screen = SLOW_LOOP / float(loop_length * loop_length)
    cosine = cosine_matrix(grid_width)
    spectrum = neumann_spectrum(grid_width)
    first_row = lax.axis_index("space") * row_count
    mode_spectrum = lax.dynamic_slice_in_dim(spectrum, first_row, row_count)
    excess = screen + mode_spectrum[:, None] + spectrum[None, :]
    half_root = 0.5 * jnp.sqrt(excess)
    log_rate = -2.0 * jnp.log(half_root + jnp.sqrt(half_root * half_root + 1.0))
    decay_rate = jnp.exp(log_rate)
    log_block = steps_local * log_rate
    block_decay = jnp.exp(log_block)
    loop_gain = -1.0 / jnp.expm1(slab_count * log_block)
    moments = jnp.arange(steps_local, dtype=jnp.float32)[:, None, None]
    rising = jnp.exp((moments + 1.0) * log_rate[None])
    falling = jnp.exp((steps_local - moments) * log_rate[None])

    def cyclic_carry(slab_ends, direction):
        combined = neighbour(slab_ends, direction)
        factor = block_decay
        distance = 1
        while distance < slab_count:
            combined = combined + factor * neighbour(combined, direction * distance)
            factor = factor * factor
            distance = distance * 2
        return combined * loop_gain

    def recurrence_step(running, element):
        running = decay_rate * running + element
        return (running, running)

    potential = jnp.zeros_like(density)
    adjoint_t = jnp.zeros_like(density)
    adjoint_x = jnp.zeros_like(density)
    adjoint_y = jnp.zeros_like(density)
    for iteration in range(ITERS):
        next_mass, next_x, next_y = kinetic_prox(
            density - TAU_STEP * adjoint_t,
            flux_x - TAU_STEP * adjoint_x,
            flux_y - TAU_STEP * adjoint_y,
        )
        bar_mass = 2.0 * next_mass - density
        bar_x = 2.0 * next_x - flux_x
        bar_y = 2.0 * next_y - flux_y
        earlier = shifted_2(bar_mass[steps_local - 1 :], "tm", 1)
        time_change = bar_mass - jnp.concatenate([earlier, bar_mass[:-1]], axis=0)
        part_y = time_change + flux_divergence(bar_y) - source
        stacked = jnp.stack([part_y, bar_x])
        spectral = jnp.einsum("ftij,kj->ftki", stacked, cosine, precision=highest)
        in_modes = lax.all_to_all(spectral, "space", split_axis=2, concat_axis=3, tiled=True)
        mixed_rhs = in_modes[0] + flux_divergence(in_modes[1])
        forcing = jnp.einsum("tai,ki->tak", mixed_rhs, cosine, precision=highest)
        forward_end, forward_partial = lax.scan(
            recurrence_step, jnp.zeros_like(decay_rate), forcing
        )
        incoming = cyclic_carry(forward_end, 1)
        forward_full = forward_partial + rising * incoming
        backward_start, backward_partial = lax.scan(
            recurrence_step, jnp.zeros_like(decay_rate), forward_full, reverse=True
        )
        from_next = cyclic_carry(backward_start, -1)
        backward_full = backward_partial + falling * from_next
        update_modes = decay_rate * backward_full
        later_values = jnp.concatenate([backward_full[1:], from_next[None]], axis=0)
        time_modes = decay_rate * (backward_full - later_values)
        spatial = jnp.einsum(
            "ftak,ki->ftai", jnp.stack([update_modes, time_modes]), cosine, precision=highest
        )
        back_stack = jnp.stack([spatial[0], spatial[1], minus_gradient(spatial[0])])
        row_fields = lax.all_to_all(back_stack, "space", split_axis=3, concat_axis=2, tiled=True)
        physical = jnp.einsum("ftki,kj->ftij", row_fields, cosine, precision=highest)
        update = physical[0]
        time_back = physical[1]
        gradient_rows = physical[2]
        potential = potential + update
        adjoint_t = adjoint_t + time_back
        adjoint_x = adjoint_x + gradient_rows
        adjoint_y = adjoint_y + minus_gradient(update)
        density, flux_x, flux_y = (next_mass, next_x, next_y)
    return (density, flux_x, flux_y, potential)


def solution(mesh):
    return jax.shard_map(
        local,
        mesh=mesh,
        in_specs=(
            P("tm", "space", None),
            P("tm", "space", None),
            P("tm", "space", None),
            P("tm", "space", None),
        ),
        out_specs=(
            P("tm", "space", None),
            P("tm", "space", None),
            P("tm", "space", None),
            P("tm", "space", None),
        ),
        check_vma=False,
    )
```

profile of v0, /device:TPU:1, one launch (start us, length us, event | category | flops | bytes accessed | tf_op | source)
XLA Modules:
  0.0 727.2 jit_solution(7713709002069273788)
XLA Ops:
  7.5 9.3 %collective-permute-done = f32[1,64,512]{2,1,0:T(8,128)S(1)} collective-permute-done((f32[1,64,512]{2,1,0:T(8,128)S(1)}, f32[1,64,512]{2,1,0:T(8,128)S(1)}, u32[]{:S(2)}, u32[]{:S(2)}) %collective-permute-start) | collective-permute-done | bytes 131104 | tf_op jit(solution)/shard_map/ppermute | solution.py:17
  17.2 5.5 convolution_bitcast_fusion.2
  28.5 6.3 all-to-all-start
  34.9 14.8 %all-to-all-done = f32[8,1,32768]{2,1,0:T(1,128)S(1)} async-done(((f32[8,1,32768]{2,1,0:T(1,128)}), f32[8,1,32768]{2,1,0:T(1,128)S(1)}, u32[]{:S(2)}, u32[]{:S(2)}) %all-to-all-start) | async-done | bytes 1048608 | tf_op jit(solution)/shard_map/all_to_all | solution.py:114
  51.1 4.3 reduce
  64.6 5.8 fusion.49
  71.5 7.1 collective-permute-done.1
  78.8 7.1 collective-permute-done.2
  86.2 9.0 %collective-permute-done.3 = f32[64,512]{1,0:T(8,128)S(1)} collective-permute-done((f32[64,512]{1,0:T(8,128)S(1)}, f32[64,512]{1,0:T(8,128)S(1)}, u32[]{:S(2)}, u32[]{:S(2)}) %collective-permute-start.3) | collective-permute-done | bytes 131104 | tf_op jit(solution)/shard_map/ppermute | solution.py:17
  95.5 10.3 %collective-permute-done.4 = f32[64,512]{1,0:T(8,128)S(1)} collective-permute-done((f32[64,512]{1,0:T(8,128)S(1)}, f32[64,512]{1,0:T(8,128)S(1)}, u32[]{:S(2)}, u32[]{:S(2)}) %collective-permute-start.4) | collective-permute-done | bytes 131104 | tf_op jit(solution)/shard_map/ppermute | solution.py:17
  106.0 5.0 collective-permute-done.5
  111.4 5.4 collective-permute-done.6
  129.3 4.9 collective-permute-done.9
  134.4 7.8 %collective-permute-done.10 = f32[64,512]{1,0:T(8,128)S(1)} collective-permute-done((f32[64,512]{1,0:T(8,128)S(1)}, f32[64,512]{1,0:T(8,128)S(1)}, u32[]{:S(2)}, u32[]{:S(2)}) %collective-permute-start.10) | collective-permute-done | bytes 131104 | tf_op jit(solution)/shard_map/ppermute | solution.py:17
  146.9 5.3 collective-permute-done.12
  152.9 5.5 fusion.16
  162.0 4.6 reshape.126
  166.5 39.0 %all_to_all.99 = f32[8,1,49152]{2,1,0:T(1,128)} all-to-all(f32[8,1,49152]{2,1,0:T(1,128)S(1)} %reshape.126), channel_id=1, replica_groups=mesh['tm'=32,'space'=8] {'space'}, dimensions={0} | all-to-all | bytes 3145728 | tf_op jit(solution)/shard_map/all_to_all | solution.py:134
  205.6 5.7 reduce.1
  215.1 5.3 copy.56
  224.6 7.7 %fusion.41 = f32[3,4,64,512]{3,2,1,0:T(8,128)S(1)} fusion(f32[3,4,512,64]{2,3,1,0:T(8,128)} %all_to_all.78, f32[512]{0:T(512)S(1)} %get-tuple-element.678, f32[512]{0:T(512)S(1)} %get-tuple-element.679), kind=kOutput, calls=%fused_computation.66 | convolution fusion | flops 2416705536 | bytes 3149824 | tf_op jit(solution)/shard_map/ftki,kj->ftij/dot_general | solution.py:135
  241.4 11.4 %collective-permute-done.13 = f32[1,64,512]{2,1,0:T(8,128)S(1)} collective-permute-done((f32[1,64,512]{2,1,0:T(8,128)S(1)}, f32[1,64,512]{2,1,0:T(8,128)S(1)}, u32[]{:S(2)}, u32[]{:S(2)}) %collective-permute-start.13) | collective-permute-done | bytes 131104 | tf_op jit(solution)/shard_map/ppermute | solution.py:17
  253.1 5.5 convolution_bitcast_fusion.1
  264.4 6.0 all-to-all-start.2
  270.5 15.0 %all-to-all-done.2 = f32[8,1,32768]{2,1,0:T(1,128)} async-done(((f32[8,1,32768]{2,1,0:T(1,128)}), f32[8,1,32768]{2,1,0:T(1,128)}, u32[]{:S(2)}, u32[]{:S(2)}) %all-to-all-start.2) | async-done | bytes 1048608 | tf_op jit(solution)/shard_map/all_to_all | solution.py:114
  285.5 4.3 reduce.2
  299.0 5.8 fusion.47
  305.9 7.1 collective-permute-done.14
  313.4 7.1 collective-permute-done.15
  320.8 9.1 %collective-permute-done.16 = f32[64,512]{1,0:T(8,128)S(1)} collective-permute-done((f32[64,512]{1,0:T(8,128)S(1)}, f32[64,512]{1,0:T(8,128)S(1)}, u32[]{:S(2)}, u32[]{:S(2)}) %collective-permute-start.16) | collective-permute-done | bytes 131104 | tf_op jit(solution)/shard_map/ppermute | solution.py:17
  330.2 11.3 %collective-permute-done.17 = f32[64,512]{1,0:T(8,128)S(1)} collective-permute-done((f32[64,512]{1,0:T(8,128)S(1)}, f32[64,512]{1,0:T(8,128)S(1)}, u32[]{:S(2)}, u32[]{:S(2)}) %collective-permute-start.17) | collective-permute-done | bytes 131104 | tf_op jit(solution)/shard_map/ppermute | solution.py:17
  341.7 5.0 collective-permute-done.18
  347.1 5.3 collective-permute-done.19
  364.8 4.9 collective-permute-done.22
  370.0 7.7 %collective-permute-done.23 = f32[64,512]{1,0:T(8,128)S(1)} collective-permute-done((f32[64,512]{1,0:T(8,128)S(1)}, f32[64,512]{1,0:T(8,128)S(1)}, u32[]{:S(2)}, u32[]{:S(2)}) %collective-permute-start.23) | collective-permute-done | bytes 131104 | tf_op jit(solution)/shard_map/ppermute | solution.py:17
  388.3 5.5 fusion.23
  397.4 4.6 reshape.130
  401.9 35.4 %all_to_all.100 = f32[8,1,49152]{2,1,0:T(1,128)} all-to-all(f32[8,1,49152]{2,1,0:T(1,128)S(1)} %reshape.130), channel_id=1, replica_groups=mesh['tm'=32,'space'=8] {'space'}, dimensions={0} | all-to-all | bytes 3145728 | tf_op jit(solution)/shard_map/all_to_all | solution.py:134
  437.4 5.7 reduce.3
  446.9 5.3 copy.55
  456.2 7.7 %fusion.37 = f32[3,4,64,512]{3,2,1,0:T(8,128)S(1)} fusion(f32[3,4,512,64]{2,3,1,0:T(8,128)} %all_to_all.85, f32[512]{0:T(512)S(1)} %get-tuple-element.678, f32[512]{0:T(512)S(1)} %get-tuple-element.679), kind=kOutput, calls=%fused_computation.62 | convolution fusion | flops 2416705536 | bytes 3149824 | tf_op jit(solution)/shard_map/ftki,kj->ftij/dot_general | solution.py:135
  474.9 9.9 %collective-permute-done.26 = f32[1,64,512]{2,1,0:T(8,128)S(1)} collective-permute-done((f32[1,64,512]{2,1,0:T(8,128)S(1)}, f32[1,64,512]{2,1,0:T(8,128)S(1)}, u32[]{:S(2)}, u32[]{:S(2)}) %collective-permute-start.26) | collective-permute-done | bytes 131104 | tf_op jit(solution)/shard_map/ppermute | solution.py:17
  485.2 6.5 convolution_bitcast_fusion
  498.4 6.0 all-to-all-start.4
  504.4 15.0 %all-to-all-done.4 = f32[8,1,32768]{2,1,0:T(1,128)} async-done(((f32[8,1,32768]{2,1,0:T(1,128)}), f32[8,1,32768]{2,1,0:T(1,128)}, u32[]{:S(2)}, u32[]{:S(2)}) %all-to-all-start.4) | async-done | bytes 1048608 | tf_op jit(solution)/shard_map/all_to_all | solution.py:114
  519.4 5.2 reduce.4
  537.5 6.9 fusion.45
  545.3 7.1 while.94
  552.3 7.1 collective-permute-done.27
  559.7 7.1 collective-permute-done.28
  567.1 9.1 %collective-permute-done.29 = f32[64,512]{1,0:T(8,128)S(1)} collective-permute-done((f32[64,512]{1,0:T(8,128)S(1)}, f32[64,512]{1,0:T(8,128)S(1)}, u32[]{:S(2)}, u32[]{:S(2)}) %collective-permute-start.29) | collective-permute-done | bytes 131104 | tf_op jit(solution)/shard_map/ppermute | solution.py:17
  576.5 11.3 %collective-permute-done.30 = f32[64,512]{1,0:T(8,128)S(1)} collective-permute-done((f32[64,512]{1,0:T(8,128)S(1)}, f32[64,512]{1,0:T(8,128)S(1)}, u32[]{:S(2)}, u32[]{:S(2)}) %collective-permute-start.30) | collective-permute-done | bytes 131104 | tf_op jit(solution)/shard_map/ppermute | solution.py:17
  588.0 5.0 collective-permute-done.31
  593.9 5.6 collective-permute-done.32
  603.7 7.1 while.95
  621.7 4.9 collective-permute-done.35
  626.9 7.7 %collective-permute-done.36 = f32[64,512]{1,0:T(8,128)S(1)} collective-permute-done((f32[64,512]{1,0:T(8,128)S(1)}, f32[64,512]{1,0:T(8,128)S(1)}, u32[]{:S(2)}, u32[]{:S(2)}) %collective-permute-start.36) | collective-permute-done | bytes 131104 | tf_op jit(solution)/shard_map/ppermute | solution.py:17
  645.4 5.5 fusion.30
  657.0 5.5 reshape.134
  662.5 36.5 %all_to_all.101 = f32[8,1,49152]{2,1,0:T(1,128)} all-to-all(f32[8,1,49152]{2,1,0:T(1,128)} %reshape.134), channel_id=1, replica_groups=mesh['tm'=32,'space'=8] {'space'}, dimensions={0} | all-to-all | bytes 3145728 | tf_op jit(solution)/shard_map/all_to_all | solution.py:134
  699.0 6.9 reduce.5
  705.9 5.2 reshape.135
  711.1 5.4 copy.54
  720.4 6.5 fusion.12
  (252 shorter events, 204.3 us)
Async XLA Ops:
  0.6 4.0 copy-start.14
  0.6 4.0 copy-start.4
  4.7 232.5 %copy-start = (f32[4,64,512]{2,1,0:T(8,128)}, f32[4,64,512]{2,1,0:T(8,128)S(1)}, u32[]{:S(2)}) copy-start(f32[4,64,512]{2,1,0:T(8,128)S(1)} %get-tuple-element.663) | copy-start | bytes 1572868
  4.7 12.1 %copy-start.8 = (f32[4,64,512]{2,1,0:T(8,128)S(1)}, f32[4,64,512]{2,1,0:T(8,128)}, u32[]{:S(2)}) copy-start(f32[4,64,512]{2,1,0:T(8,128)} %param.19) | copy-start | bytes 1572868
  4.9 11.9 %collective-permute-start = (f32[1,64,512]{2,1,0:T(8,128)S(1)}, f32[1,64,512]{2,1,0:T(8,128)S(1)}, u32[]{:S(2)}, u32[]{:S(2)}) collective-permute-start(f32[1,64,512]{2,1,0:T(8,128)S(1)} %slice.179), channel_id=1, source_target_pairs={{248,0},{0,8},{8,16},{16,24},{24,32},{32,40},{40,48},{48,56},{56,6... | collective-permute-start | bytes 393224 | tf_op jit(solution)/shard_map/ppermute | solution.py:17
  7.4 57.2 %copy-start.16 = (pred[512]{0:T(512)(128)(4,1)}, pred[512]{0:T(512)(128)(4,1)S(1)}, u32[]{:S(2)}) copy-start(pred[512]{0:T(512)(128)(4,1)S(1)} %iota_compare_fusion) | copy-start | bytes 1540
  28.5 21.2 %all-to-all-start = ((f32[8,1,32768]{2,1,0:T(1,128)}), f32[8,1,32768]{2,1,0:T(1,128)S(1)}, u32[]{:S(2)}, u32[]{:S(2)}) async-start(f32[8,1,32768]{2,1,0:T(1,128)} %reshape.124), calls=%async_computation | async-start | bytes 2097152 | tf_op jit(solution)/shard_map/all_to_all | solution.py:114
  71.4 7.2 collective-permute-start.1
  78.6 7.3 %collective-permute-start.2 = (f32[64,512]{1,0:T(8,128)S(1)}, f32[64,512]{1,0:T(8,128)S(1)}, u32[]{:S(2)}, u32[]{:S(2)}) collective-permute-start(f32[64,512]{1,0:T(8,128)S(1)} %collective-permute-done.1), channel_id=1, source_target_pairs={{248,0},{0,8},{8,16},{16,24},{24,32},{32,40},{40,48},{48,56},{56,6... | collective-permute-start | bytes 393224 | tf_op jit(solution)/shard_map/ppermute | solution.py:17
  86.1 9.1 %collective-permute-start.3 = (f32[64,512]{1,0:T(8,128)S(1)}, f32[64,512]{1,0:T(8,128)S(1)}, u32[]{:S(2)}, u32[]{:S(2)}) collective-permute-start(f32[64,512]{1,0:T(8,128)S(1)} %multiply_add_fusion.29), channel_id=1, source_target_pairs={{240,0},{248,8},{0,16},{8,24},{16,32},{24,40},{32,48},{40,56},{48,... | collective-permute-start | bytes 393224 | tf_op jit(solution)/shard_map/ppermute | solution.py:17
  95.4 10.4 %collective-permute-start.4 = (f32[64,512]{1,0:T(8,128)S(1)}, f32[64,512]{1,0:T(8,128)S(1)}, u32[]{:S(2)}, u32[]{:S(2)}) collective-permute-start(f32[64,512]{1,0:T(8,128)S(1)} %multiply_add_fusion.28), channel_id=1, source_target_pairs={{224,0},{232,8},{240,16},{248,24},{0,32},{8,40},{16,48},{24,56},{3... | collective-permute-start | bytes 393224 | tf_op jit(solution)/shard_map/ppermute | solution.py:17
  105.9 5.1 collective-permute-start.5
  111.3 5.5 collective-permute-start.6
  111.4 5.9 copy-start.22
  118.2 3.9 collective-permute-start.7
  122.1 5.7 collective-permute-start.8
  128.0 6.2 collective-permute-start.9
  134.4 7.9 %collective-permute-start.10 = (f32[64,512]{1,0:T(8,128)S(1)}, f32[64,512]{1,0:T(8,128)S(1)}, u32[]{:S(2)}, u32[]{:S(2)}) collective-permute-start(f32[64,512]{1,0:T(8,128)S(1)} %multiply_add_fusion.24), channel_id=1, source_target_pairs={{32,0},{40,8},{48,16},{56,24},{64,32},{72,40},{80,48},{88,56},{96,... | collective-permute-start | bytes 393224 | tf_op jit(solution)/shard_map/ppermute | solution.py:17
  142.5 3.9 collective-permute-start.11
  146.6 5.6 collective-permute-start.12
  146.9 5.8 copy-start.19
  232.3 1.0 copy-start.5
  237.2 1.1 copy-start.2
  237.2 15.6 %copy-start.9 = (f32[4,64,512]{2,1,0:T(8,128)S(1)}, f32[4,64,512]{2,1,0:T(8,128)}, u32[]{:S(2)}) copy-start(f32[4,64,512]{2,1,0:T(8,128)} %param.19) | copy-start | bytes 1572868
  237.2 15.6 %copy-start.17 = (pred[512]{0:T(512)(128)(4,1)S(1)}, pred[512]{0:T(512)(128)(4,1)}, u32[]{:S(2)}) copy-start(pred[512]{0:T(512)(128)(4,1)} %copy-done.16) | copy-start | bytes 1540
  238.3 14.5 %collective-permute-start.13 = (f32[1,64,512]{2,1,0:T(8,128)S(1)}, f32[1,64,512]{2,1,0:T(8,128)S(1)}, u32[]{:S(2)}, u32[]{:S(2)}) collective-permute-start(f32[1,64,512]{2,1,0:T(8,128)S(1)} %slice.194), channel_id=1, source_target_pairs={{248,0},{0,8},{8,16},{16,24},{24,32},{32,40},{40,48},{48,56},{56,6... | collective-permute-start | bytes 393224 | tf_op jit(solution)/shard_map/ppermute | solution.py:17
  264.4 21.0 %all-to-all-start.2 = ((f32[8,1,32768]{2,1,0:T(1,128)}), f32[8,1,32768]{2,1,0:T(1,128)}, u32[]{:S(2)}, u32[]{:S(2)}) async-start(f32[8,1,32768]{2,1,0:T(1,128)} %reshape.128), calls=%async_computation.2 | async-start | bytes 2097152 | tf_op jit(solution)/shard_map/all_to_all | solution.py:114
  305.8 46.9 %copy-start.23 = (f32[4]{0:T(128)S(1)}, f32[4]{0:T(128)}, u32[]{:S(2)}) copy-start(f32[4]{0:T(128)} %copy-done.22) | copy-start | bytes 52
  305.8 7.2 collective-permute-start.14
  313.0 7.5 %collective-permute-start.15 = (f32[64,512]{1,0:T(8,128)S(1)}, f32[64,512]{1,0:T(8,128)S(1)}, u32[]{:S(2)}, u32[]{:S(2)}) collective-permute-start(f32[64,512]{1,0:T(8,128)S(1)} %collective-permute-done.14), channel_id=1, source_target_pairs={{248,0},{0,8},{8,16},{16,24},{24,32},{32,40},{40,48},{48,56},{56,6... | collective-permute-start | bytes 393224 | tf_op jit(solution)/shard_map/ppermute | solution.py:17
  320.7 9.2 %collective-permute-start.16 = (f32[64,512]{1,0:T(8,128)S(1)}, f32[64,512]{1,0:T(8,128)S(1)}, u32[]{:S(2)}, u32[]{:S(2)}) collective-permute-start(f32[64,512]{1,0:T(8,128)S(1)} %multiply_add_fusion.21), channel_id=1, source_target_pairs={{240,0},{248,8},{0,16},{8,24},{16,32},{24,40},{32,48},{40,56},{48,... | collective-permute-start | bytes 393224 | tf_op jit(solution)/shard_map/ppermute | solution.py:17
  330.1 11.3 %collective-permute-start.17 = (f32[64,512]{1,0:T(8,128)S(1)}, f32[64,512]{1,0:T(8,128)S(1)}, u32[]{:S(2)}, u32[]{:S(2)}) collective-permute-start(f32[64,512]{1,0:T(8,128)S(1)} %multiply_add_fusion.20), channel_id=1, source_target_pairs={{224,0},{232,8},{240,16},{248,24},{0,32},{8,40},{16,48},{24,56},{3... | collective-permute-start | bytes 393224 | tf_op jit(solution)/shard_map/ppermute | solution.py:17
  341.6 5.1 collective-permute-start.18
  347.0 5.4 collective-permute-start.19
  353.8 34.1 %copy-start.20 = (f32[4]{0:T(128)S(1)}, f32[4]{0:T(128)}, u32[]{:S(2)}) copy-start(f32[4]{0:T(128)} %copy-done.19) | copy-start | bytes 52
  353.8 3.9 collective-permute-start.20
  357.7 5.3 collective-permute-start.21
  363.2 6.6 collective-permute-start.22
  370.0 7.8 %collective-permute-start.23 = (f32[64,512]{1,0:T(8,128)S(1)}, f32[64,512]{1,0:T(8,128)S(1)}, u32[]{:S(2)}, u32[]{:S(2)}) collective-permute-start(f32[64,512]{1,0:T(8,128)S(1)} %multiply_add_fusion.16), channel_id=1, source_target_pairs={{32,0},{40,8},{48,16},{56,24},{64,32},{72,40},{80,48},{88,56},{96,... | collective-permute-start | bytes 393224 | tf_op jit(solution)/shard_map/ppermute | solution.py:17
  378.0 3.9 collective-permute-start.24
  382.1 5.6 collective-permute-start.25
  456.2 8.2 %copy-start.13 = (f32[4,64,512]{2,1,0:T(8,128)S(1)}, f32[4,64,512]{2,1,0:T(8,128)}, u32[]{:S(2)}) copy-start(f32[4,64,512]{2,1,0:T(8,128)} %get-tuple-element.657) | copy-start | bytes 1572868
  464.0 1.2 copy-start.3
  464.0 1.3 copy-start.6
  464.0 1.5 copy-start.7
  469.6 1.1 copy-start.12
  469.6 15.2 %copy-start.10 = (f32[4,64,512]{2,1,0:T(8,128)S(1)}, f32[4,64,512]{2,1,0:T(8,128)}, u32[]{:S(2)}) copy-start(f32[4,64,512]{2,1,0:T(8,128)} %param.19) | copy-start | bytes 1572868
  469.6 15.2 %copy-start.18 = (pred[512]{0:T(512)(128)(4,1)S(1)}, pred[512]{0:T(512)(128)(4,1)}, u32[]{:S(2)}) copy-start(pred[512]{0:T(512)(128)(4,1)} %copy-done.16) | copy-start | bytes 1540
  470.7 14.1 %collective-permute-start.26 = (f32[1,64,512]{2,1,0:T(8,128)S(1)}, f32[1,64,512]{2,1,0:T(8,128)S(1)}, u32[]{:S(2)}, u32[]{:S(2)}) collective-permute-start(f32[1,64,512]{2,1,0:T(8,128)S(1)} %slice.209), channel_id=1, source_target_pairs={{248,0},{0,8},{8,16},{16,24},{24,32},{32,40},{40,48},{48,56},{56,6... | collective-permute-start | bytes 393224 | tf_op jit(solution)/shard_map/ppermute | solution.py:17
  498.4 21.0 %all-to-all-start.4 = ((f32[8,1,32768]{2,1,0:T(1,128)}), f32[8,1,32768]{2,1,0:T(1,128)}, u32[]{:S(2)}, u32[]{:S(2)}) async-start(f32[8,1,32768]{2,1,0:T(1,128)} %reshape.132), calls=%async_computation.4 | async-start | bytes 2097152 | tf_op jit(solution)/shard_map/all_to_all | solution.py:114
  552.3 7.1 collective-permute-start.27
  559.5 7.3 %collective-permute-start.28 = (f32[64,512]{1,0:T(8,128)S(1)}, f32[64,512]{1,0:T(8,128)S(1)}, u32[]{:S(2)}, u32[]{:S(2)}) collective-permute-start(f32[64,512]{1,0:T(8,128)S(1)} %collective-permute-done.27), channel_id=1, source_target_pairs={{248,0},{0,8},{8,16},{16,24},{24,32},{32,40},{40,48},{48,56},{56,6... | collective-permute-start | bytes 393224 | tf_op jit(solution)/shard_map/ppermute | solution.py:17
  567.0 9.2 %collective-permute-start.29 = (f32[64,512]{1,0:T(8,128)S(1)}, f32[64,512]{1,0:T(8,128)S(1)}, u32[]{:S(2)}, u32[]{:S(2)}) collective-permute-start(f32[64,512]{1,0:T(8,128)S(1)} %multiply_add_fusion.13), channel_id=1, source_target_pairs={{240,0},{248,8},{0,16},{8,24},{16,32},{24,40},{32,48},{40,56},{48,... | collective-permute-start | bytes 393224 | tf_op jit(solution)/shard_map/ppermute | solution.py:17
  576.4 11.3 %collective-permute-start.30 = (f32[64,512]{1,0:T(8,128)S(1)}, f32[64,512]{1,0:T(8,128)S(1)}, u32[]{:S(2)}, u32[]{:S(2)}) collective-permute-start(f32[64,512]{1,0:T(8,128)S(1)} %multiply_add_fusion.12), channel_id=1, source_target_pairs={{224,0},{232,8},{240,16},{248,24},{0,32},{8,40},{16,48},{24,56},{3... | collective-permute-start | bytes 393224 | tf_op jit(solution)/shard_map/ppermute | solution.py:17
  587.9 5.1 collective-permute-start.31
  593.9 5.6 collective-permute-start.32
  610.7 34.3 %copy-start.15 = (f32[4,64,512]{2,1,0:T(8,128)S(1)}, f32[4,64,512]{2,1,0:T(8,128)}, u32[]{:S(2)}) copy-start(f32[4,64,512]{2,1,0:T(8,128)} %get-tuple-element.410) | copy-start | bytes 1572868
  610.7 34.3 %copy-start.21 = (f32[4]{0:T(128)S(1)}, f32[4]{0:T(128)}, u32[]{:S(2)}) copy-start(f32[4]{0:T(128)} %copy-done.19) | copy-start | bytes 52
  610.7 3.8 collective-permute-start.33
  614.5 5.3 collective-permute-start.34
  620.0 6.6 collective-permute-start.35
  626.8 7.8 %collective-permute-start.36 = (f32[64,512]{1,0:T(8,128)S(1)}, f32[64,512]{1,0:T(8,128)S(1)}, u32[]{:S(2)}, u32[]{:S(2)}) collective-permute-start(f32[64,512]{1,0:T(8,128)S(1)} %multiply_add_fusion.8), channel_id=1, source_target_pairs={{32,0},{40,8},{48,16},{56,24},{64,32},{72,40},{80,48},{88,56},{96,... | collective-permute-start | bytes 393224 | tf_op jit(solution)/shard_map/ppermute | solution.py:17
  634.8 3.9 collective-permute-start.37
  638.9 5.8 collective-permute-start.38
  (2 other events, 2.0 us)
where the time goes:
time: 739 us; the launch traced here: 727 us
  waiting for transfers between devices  287 us (39%)
  local copies, waits for them, and re-layouts  122 us (17%)
  blocking collectives  111 us (15%)
  other arithmetic  78.8 us (11%)
  matrix products  74.5 us (10%)
  starting transfers between devices  51.5 us (7%)
    ppermute x39, waiting for transfers between devices, shifted_2(): return lax.ppermute(block, axis, route)  242 us
    all_to_all x3, blocking collectives, local(): lax.all_to_all(back_stack, 'space', split_axis=3, concat_axis=2, tiled=True)  111 us
    unnamed x60, local copies, waits for them, and re-layouts  51.7 us
    all_to_all x3, waiting for transfers between devices, local(): lax.all_to_all(spectral, 'space', split_axis=2, concat_axis=3, tiled=True)  44.8 us
    ppermute x39, starting transfers between devices, shifted_2(): return lax.ppermute(block, axis, route)  33.3 us
    all_to_all x6, local copies, waits for them, and re-layouts, local(): lax.all_to_all(back_stack, 'space', split_axis=3, concat_axis=2, tiled=True)  28.2 us
    dot_general x3, matrix products, local(): forcing = jnp.einsum('tai,ki->tak', mixed_rhs, cosine, precision=highest)  18.5 us
    all_to_all x3, other arithmetic, local(): lax.all_to_all(back_stack, 'space', split_axis=3, concat_axis=2, tiled=True)  18.3 us
  transfers between devices with their start and end apart: 42, of which 42 were waited for; matrix products, arithmetic and copies ran while one was open for 0% of the time, Pallas kernels for 0%

commit v1 on v0

v1 whole, which is shorter than its diff:
```python
import functools

import jax
import jax.numpy as jnp
import numpy as np
from jax import lax
from jax.experimental import pallas as pl
from jax.experimental.pallas import tpu as pltpu
from jax.sharding import PartitionSpec as P

ITERS = 3
NEWTON = 10
TAU_STEP = 1.0
SLOW_LOOP = 2.25
INTERPRET = False
BOTH = ("tm", "space")
f32 = jnp.float32
bf16 = jnp.bfloat16
NN = (((1,), (0,)), ((), ()))
NT = (((1,), (1,)), ((), ()))
TN = (((0,), (0,)), ((), ()))


def halves(value):
    high = value.astype(bf16)
    return high, (value - high.astype(f32)).astype(bf16)


def dot3(left, right, dims):
    dot = functools.partial(lax.dot_general, dimension_numbers=dims, preferred_element_type=f32)
    return dot(left[0], right[0]) + (dot(left[0], right[1]) + dot(left[1], right[0]))


def cosine_matrix(points):
    one = np.float32
    frequency = np.arange(points, dtype=one)[:, None]
    sample = np.arange(points, dtype=one)[None, :]
    scaling = np.where(frequency == 0, np.sqrt(one(1.0 / points)), np.sqrt(one(2.0 / points))).astype(one)
    angle = one(np.pi) * (sample + one(0.5)) * frequency / one(points)
    return (scaling * np.cos(angle.astype(np.float64)).astype(one)).astype(one)


def neumann_spectrum(points):
    half_angle = np.pi * np.arange(points) / (2.0 * points)
    return (4.0 * np.sin(half_angle) ** 2).astype(np.float32)


def loop_basis(length, slabs):
    rows = [np.full(length, np.sqrt(1.0 / length))]
    values = [0.0]
    moment = np.arange(length)
    for k in range(1, length // 2):
        angle = 2.0 * np.pi * ((k * moment) % length) / length
        rows += [np.sqrt(2.0 / length) * np.cos(angle), np.sqrt(2.0 / length) * np.sin(angle)]
        values += [4.0 * np.sin(np.pi * k / length) ** 2] * 2
    rows.append(np.sqrt(1.0 / length) * (-1.0) ** moment)
    values.append(4.0)
    basis = np.stack(rows).reshape(length, slabs, length // slabs).transpose(0, 2, 1).reshape(length, length)
    return basis.astype(np.float32), np.asarray(values, np.float32)


def np_halves(matrix):
    high = matrix.astype(bf16)
    return high, (matrix - high.astype(np.float32)).astype(bf16)


def call(body, outs, scratch=(), scalars=0, n_in=0, cost=None, **kw):
    vmem = pl.BlockSpec(memory_space=pltpu.VMEM)
    smem = pl.BlockSpec(memory_space=pltpu.SMEM)
    return pl.pallas_call(
        body,
        out_shape=[jax.ShapeDtypeStruct(s, f32) for s in outs],
        in_specs=[smem] * scalars + [vmem] * n_in,
        out_specs=[vmem] * len(outs),
        scratch_shapes=list(scratch),
        cost_estimate=pl.CostEstimate(flops=int(cost[0]), bytes_accessed=int(cost[1]), transcendentals=0),
        interpret=INTERPRET,
        **kw,
    )


def newton(mass, along_x, along_y):
    target = 0.5 * TAU_STEP * (along_x * along_x + along_y * along_y)
    root = jnp.maximum(mass, 0.0) + jnp.exp(jnp.log(target) * (1.0 / 3.0))
    for _ in range(NEWTON):
        shifted = root + TAU_STEP
        gap = root - mass
        product = gap * shifted
        residue = product * shifted - target
        derivative = shifted * (shifted + (gap + gap))
        root = jnp.maximum(root - residue / derivative, 0.0)
    factor = root / (root + TAU_STEP)
    return root, factor * along_x, factor * along_y


def last_of(shape, axis, count):
    return lax.broadcasted_iota(jnp.int32, shape, axis) == count - 1


def prox_body(with_dual, last_place, *refs):
    if with_dual:
        place, d, fx, fy, u, u_plane, u_rows, nd, nx, ny, bar_plane, bar_rows = refs
    else:
        place, d, fx, fy, nd, nx, ny, bar_plane, bar_rows = refs
        u = None
    steps, rows, width = d.shape
    chunk = 16
    per = rows // chunk
    if with_dual:
        end_row = last_of((rows, width), 0, rows)
        end_column = last_of((rows, width), 1, width)
        for t in range(steps):
            here = u[t]
            later = u[t + 1] if t + 1 < steps else u_plane[...]
            edge = jnp.where(place[0] == last_place, here[rows - 1 :, :], u_rows[t : t + 1, :])
            below = jnp.where(end_row, edge, pltpu.roll(here, rows - 1, 0))
            right = jnp.where(end_column, here, pltpu.roll(here, width - 1, 1))
            nd[t] = d[t] - TAU_STEP * (here - later)
            nx[t] = fx[t] - TAU_STEP * (here - below)
            ny[t] = fy[t] - TAU_STEP * (here - right)
    source = (nd, nx, ny) if with_dual else (d, fx, fy)

    def step(index, carry):
        t = index // per
        span = pl.ds(pl.multiple_of((index % per) * chunk, chunk), chunk)
        out = newton(*[ref[t, span, :] for ref in source])
        for ref, value in zip((nd, nx, ny), out):
            ref[t, span, :] = value
        return carry

    lax.fori_loop(0, steps * per, step, 0)
    bar_plane[...] = 2.0 * nd[steps - 1] - d[steps - 1]
    for t in range(steps):
        bar_rows[t : t + 1, :] = 2.0 * nx[t, rows - 1 :, :] - fx[t, rows - 1 :, :]


def forward_body(last_place, place, d, fx, fy, nd, nx, ny, src, bar_plane, bar_rows, ch, cl, out, rh, rl):
    steps, rows, width = d.shape
    shape = (rows, width)
    row = lax.broadcasted_iota(jnp.int32, shape, 0)
    column = lax.broadcasted_iota(jnp.int32, shape, 1)
    final_row = (row == rows - 1) & (place[0] == last_place)
    before = bar_plane[...]
    for t in range(steps):
        mass = 2.0 * nd[t] - d[t]
        along_x = 2.0 * nx[t] - fx[t]
        along_y = 2.0 * ny[t] - fy[t]
        x_before = jnp.where(row == 0, bar_rows[t : t + 1, :], pltpu.roll(along_x, 1, 0))
        y_before = jnp.where(column == 0, 0.0, pltpu.roll(along_y, 1, 1))
        value = mass - before
        value = value + (jnp.where(final_row, 0.0, along_x) - x_before)
        value = value + (jnp.where(column == width - 1, 0.0, along_y) - y_before)
        value = value - src[t]
        before = mass
        high, low = halves(value)
        rh[t * rows : (t + 1) * rows, :] = high
        rl[t * rows : (t + 1) * rows, :] = low
    modes = dot3((ch[...], cl[...]), (rh[...], rl[...]), NT)
    lanes = 2 * rows
    for pair in range(steps // 2):
        out[pl.ds(pair, width, stride=steps // 2), :] = modes[:, pair * lanes : (pair + 1) * lanes]


def solve_body(slabs, places, steps, with_sum, *refs):
    if with_sum:
        z, ch, cl, wh, wl, vh, vl, den, so_far, out, total, field = refs
    else:
        z, ch, cl, wh, wl, vh, vl, den, out, total, field = refs
    length = slabs * steps
    pairs = steps // 2
    stride = places * 2 * pairs
    lanes = z.shape[1]
    low_half = lax.broadcasted_iota(jnp.int32, (slabs, lanes), 1) < lanes // 2

    def at(place, mode, pair):
        return pl.ds((place * 2 + mode) * pairs + pair, slabs, stride=stride)

    for mode in range(2):
        for pair in range(pairs):
            for q in range(places // 2):
                a = z[at(2 * q, mode, pair), :]
                b = z[at(2 * q + 1, mode, pair), :]
                top = mode * length + 2 * pair * slabs
                span = slice(q * lanes, (q + 1) * lanes)
                field[top : top + slabs, span] = jnp.where(low_half, a, pltpu.roll(b, lanes // 2, 1))
                field[top + slabs : top + 2 * slabs, span] = jnp.where(low_half, pltpu.roll(a, lanes // 2, 1), b)
    cosine = (ch[...], cl[...])
    for mode in range(2):
        span = slice(mode * length, (mode + 1) * length)
        field[span, :] = dot3((wh[...], wl[...]), halves(field[span, :]), NN)
    solved = dot3(halves(field[...]), cosine, NT) / den[...]
    if with_sum:
        solved = solved + so_far[...]
    total[...] = solved
    field[...] = dot3(halves(solved), cosine, NN)
    for mode in range(2):
        span = slice(mode * length, (mode + 1) * length)
        field[span, :] = dot3((vh[...], vl[...]), halves(field[span, :]), NN)
    for mode in range(2):
        for pair in range(pairs):
            for q in range(places // 2):
                top = mode * length + 2 * pair * slabs
                span = slice(q * lanes, (q + 1) * lanes)
                a = field[top : top + slabs, span]
                b = field[top + slabs : top + 2 * slabs, span]
                out[at(2 * q, mode, pair), :] = jnp.where(low_half, a, pltpu.roll(b, lanes // 2, 1))
                out[at(2 * q + 1, mode, pair), :] = jnp.where(low_half, pltpu.roll(a, lanes // 2, 1), b)


def backward_body(y, ch, cl, u, u_plane, u_rows):
    steps, rows, width = u.shape
    pairs = steps // 2
    cosine = (ch[...], cl[...])
    for pair in range(pairs):
        modes = halves(y[pl.ds(pair, width, stride=pairs), :])
        value = dot3(modes, cosine, TN)
        for half in range(2):
            t = 2 * pair + half
            u[t] = value[half * rows : (half + 1) * rows, :]
            u_rows[t : t + 1, :] = value[half * rows : half * rows + 1, :]
    u_plane[...] = u[0]


def local(density, flux_x, flux_y, source):
    steps, rows, width = density.shape
    slabs = lax.axis_size("tm")
    places = lax.axis_size("space")
    length = steps * slabs
    screen = SLOW_LOOP / float(length * length)
    ch, cl = (jnp.asarray(m) for m in np_halves(cosine_matrix(width)))
    basis, loop_values = loop_basis(length, slabs)
    wh, wl = (jnp.asarray(m) for m in np_halves(basis))
    vh, vl = (jnp.asarray(m) for m in np_halves(np.ascontiguousarray(basis.T)))
    spectrum = jnp.asarray(neumann_spectrum(width))
    place = lax.axis_index("space")
    first = 2 * (lax.axis_index("tm") * places + place)
    own = lax.dynamic_slice_in_dim(spectrum, first, 2)
    den = own[:, None, None] + jnp.asarray(loop_values)[None, :, None] + spectrum[None, None, :] + screen
    den = den.reshape(2 * length, width)
    place = place.astype(jnp.int32).reshape(1)
    nbytes = density.size * 4
    mega = density.size * width * 6
    field = (steps, rows, width)
    edges = [(rows, width), (steps, width)]
    packed = (width * steps // 2, 2 * rows)
    chunk = packed[0] * packed[1] // (slabs * places)
    loop_next = [(i, (i + 1) % slabs) for i in range(slabs)]
    loop_back = [((i + 1) % slabs, i) for i in range(slabs)]
    row_next = [(i, i + 1) for i in range(places - 1)]
    row_back = [(i + 1, i) for i in range(places - 1)]

    def exchange(value):
        value = value.reshape(slabs * places, 1, chunk)
        value = lax.all_to_all(value, BOTH, split_axis=0, concat_axis=0, tiled=True)
        return value.reshape(packed)

    dual = ()
    total = ()
    for iteration in range(ITERS):
        new_d, new_x, new_y, plane, edge = call(
            functools.partial(prox_body, bool(dual), places - 1),
            [field] * 3 + edges, scalars=1, n_in=3 + len(dual), cost=(density.size * 200, 8 * nbytes), name="prox",
        )(place, density, flux_x, flux_y, *dual)
        plane = lax.ppermute(plane, "tm", loop_next)
        edge = lax.ppermute(edge, "space", row_next)
        (modes,) = call(
            functools.partial(forward_body, places - 1), [packed],
            scratch=[pltpu.VMEM((steps * rows, width), bf16)] * 2, scalars=1, n_in=11, cost=(mega, 9 * nbytes), name="forward",
        )(place, density, flux_x, flux_y, new_d, new_x, new_y, source, plane, edge, ch, cl)
        modes = exchange(modes)
        modes, solved = call(
            functools.partial(solve_body, slabs, places, steps, bool(total)),
            [packed, (2 * length, width)], scratch=[pltpu.VMEM((2 * length, width), f32)],
            n_in=8 + len(total), cost=(3 * mega, 6 * nbytes), name="solve",
        )(modes, ch, cl, wh, wl, vh, vl, den, *total)
        total = (solved,)
        modes = exchange(modes)
        update, plane, edge = call(
            backward_body, [field] + edges, n_in=3, cost=(mega, 3 * nbytes), name="backward",
        )(modes, ch, cl)
        density, flux_x, flux_y = new_d, new_x, new_y
        if iteration + 1 < ITERS:
            dual = (update, lax.ppermute(plane, "tm", loop_back), lax.ppermute(edge, "space", row_back))
    return density, flux_x, flux_y, update


def solution(mesh):
    spec = P("tm", "space", None)
    return jax.shard_map(local, mesh=mesh, in_specs=(spec,) * 4, out_specs=(spec,) * 4, check_vma=False)
```

time: 739 us -> 267 us (0.36); the launches traced: 727 us -> 266 us
  waiting for transfers between devices: 287 us -> 39.9 us
  local copies, waits for them, and re-layouts: 122 us -> 5.39 us
  other arithmetic: 78.8 us -> 0.97 us
  matrix products: 74.5 us -> 0 us
  Pallas kernels: 0 us -> 53 us
  blocking collectives: 111 us -> 136 us
  starting transfers between devices: 51.5 us -> 30 us
    ppermute x39 -> x10, waiting for transfers between devices: 242 us -> 21.7 us  [the longest x3 13.8 us: local(): plane = lax.ppermute(plane, 'tm', loop_next)]
    dot_general x11 -> x0, matrix products: 67.9 us -> none  [the longest x3 18.5 us: local(): forcing = jnp.einsum('tai,ki->tak', mixed_rhs, cosine, precision=highest)]
    pallas_call x0 -> x12, Pallas kernels: none -> 53 us  [the longest x3 18.7 us: local(): call(functools.partial(prox_body, bool(dual), places - 1), [field] * 3 +...]
    unnamed x60 -> x26, local copies, waits for them, and re-layouts: 51.7 us -> 5.31 us
    all_to_all x10 -> x0, local copies, waits for them, and re-layouts: 37.1 us -> none  [the longest x6 28.2 us: local(): lax.all_to_all(back_stack, 'space', split_axis=3, concat_axis=2, tiled=True)]
    all_to_all x6 -> x0, other arithmetic: 32.1 us -> none  [the longest x3 18.3 us: local(): lax.all_to_all(back_stack, 'space', split_axis=3, concat_axis=2, tiled=True)]
    all_to_all x3 -> x1, waiting for transfers between devices: 44.8 us -> 18.2 us  [exchange(): value = lax.all_to_all(value, BOTH, split_axis=0, concat_axis=0, tiled=True)]
    all_to_all x3 -> x5, blocking collectives: 111 us -> 136 us  [exchange(): value = lax.all_to_all(value, BOTH, split_axis=0, concat_axis=0, tiled=True)]
  transfers between devices with their start and end apart: 42 -> 11, of which waited for: 42 -> 9; matrix products, arithmetic and copies ran while one was open for 0% -> 0% of each run, Pallas kernels for 0% -> 0%
where the time goes in v1:
time: 267 us; the launch traced here: 266 us
  blocking collectives  136 us (51%)
  Pallas kernels  53 us (20%)
  waiting for transfers between devices  39.9 us (15%)
  starting transfers between devices  30 us (11%)
  local copies, waits for them, and re-layouts  5.39 us (2%)
    all_to_all x5, blocking collectives, exchange(): value = lax.all_to_all(value, BOTH, split_axis=0, concat_axis=0, tiled=True)  136 us
    pallas_call x3, Pallas kernels, local(): call(functools.partial(prox_body, bool(dual), places - 1), [field] * 3 +...  18.7 us
    all_to_all x1, waiting for transfers between devices, exchange(): value = lax.all_to_all(value, BOTH, split_axis=0, concat_axis=0, tiled=True)  18.2 us
    pallas_call x3, Pallas kernels, local(): call(functools.partial(solve_body, slabs, places, steps, bool(total)), [p...  14 us
    ppermute x3, waiting for transfers between devices, local(): plane = lax.ppermute(plane, 'tm', loop_next)  13.8 us
    pallas_call x3, Pallas kernels, local(): call(functools.partial(forward_body, places - 1), [packed], scratch=[pltp...  12.1 us
    all_to_all x1, starting transfers between devices, exchange(): value = lax.all_to_all(value, BOTH, split_axis=0, concat_axis=0, tiled=True)  10.3 us
    ppermute x3, starting transfers between devices, local(): edge = lax.ppermute(edge, 'space', row_next)  8.79 us
  transfers between devices with their start and end apart: 11, of which 9 were waited for; matrix products, arithmetic and copies ran while one was open for 0% of the time, Pallas kernels for 0%

profile of v1, /device:TPU:1, one launch (start us, length us, event | category | flops | bytes accessed | tf_op | source)
XLA Modules:
  0.0 266.2 jit_solution(1962162359124038650)
XLA Ops:
  0.6 5.9 %prox.3 = (f32[4,64,512]{2,1,0:T(8,128)}, f32[4,64,512]{2,1,0:T(8,128)}, f32[4,64,512]{2,1,0:T(8,128)}, f32[64,512]{1,0:T(8,128)}, f32[4,512]{1,0:T(4,128)}) custom-call(s32[1]{0:T(128)} %bitcast.refs_0_.place, f32[4,64,512]{2,1,0:T(8,128)} %d.1, f32[4,64,512]{2,1,0:T(8,128)} %fx.1, f32[4,64,512]{2,1,0:T(8,128)} %fy.1), custom_call_target="tpu_custom_call" | custom-call | flops 26214400 | bytes 4194304 | tf_op jit(solution)/shard_map/prox/pallas_call | solution.py:260
  6.6 2.5 collective-permute-start
  9.0 4.0 %collective-permute-start.1 = (f32[4,512]{1,0:T(4,128)}, f32[4,512]{1,0:T(4,128)S(1)}, u32[]{:S(2)}, u32[]{:S(2)}) collective-permute-start(f32[4,512]{1,0:T(4,128)} %get-tuple-element.35), channel_id=1, source_target_pairs={{0,1},{1,2},{2,3},{3,4},{4,5},{5,6},{6,7},{8,9},{9,10},{10,11},{11... | collective-permute-start | bytes 24584 | tf_op jit(solution)/shard_map/ppermute | solution.py:265
  13.1 1.0 collective-permute-done.1.bar_rows
  14.0 0.0 copy-start.10
  14.1 4.5 %collective-permute-done.bar_plane = f32[64,512]{1,0:T(8,128)S(1)} collective-permute-done((f32[64,512]{1,0:T(8,128)}, f32[64,512]{1,0:T(8,128)S(1)}, u32[]{:S(2)}, u32[]{:S(2)}) %collective-permute-start) | collective-permute-done | bytes 131104 | tf_op jit(solution)/shard_map/ppermute | solution.py:264
  18.6 0.0 copy-start.5
  18.6 0.0 copy-done.10
  18.6 0.6 copy-done.5
  19.2 4.0 %forward.3 = f32[1024,128]{1,0:T(8,128)} custom-call(s32[1]{0:T(128)} %bitcast.refs_0_.place, f32[4,64,512]{2,1,0:T(8,128)} %d.1, f32[4,64,512]{2,1,0:T(8,128)} %fx.1, f32[4,64,512]{2,1,0:T(8,128)} %fy.1, f32[4,64,512]{2,1,0:T(8,128)} %get-tuple-element.31.nd.refs_1_.d, f32[4,64,512]{2,1,0:T(8,128)} %get-tuple-element.32.nx.refs_2_.fx, ...), custom_call_target="tpu_custom_call" | custom-call | flops 402653184 | bytes 4718592 | tf_op jit(solution)/shard_map/forward/pallas_call | solution.py:266
  23.2 10.3 %all-to-all-start = ((f32[256,1,512]{2,1,0:T(1,128)}), f32[256,1,512]{2,1,0:T(1,128)S(1)}, u32[]{:S(2)}, u32[]{:S(2)}) async-start(f32[256,1,512]{2,1,0:T(1,128)} %bitcast.19), calls=%async_computation | async-start | bytes 1048576 | tf_op jit(solution)/shard_map/all_to_all | solution.py:254
  33.6 0.0 copy-start.11
  33.6 0.7 copy-done.11
  34.2 0.0 copy-start.12
  34.2 0.1 dynamic_slice.3
  34.3 0.6 copy-done.12
  34.9 0.1 bitcast_add_fusion
  35.0 0.9 add_add_fusion.refs_7_
  35.9 18.2 %all-to-all-done = f32[256,1,512]{2,1,0:T(1,128)S(1)} async-done(((f32[256,1,512]{2,1,0:T(1,128)}), f32[256,1,512]{2,1,0:T(1,128)S(1)}, u32[]{:S(2)}, u32[]{:S(2)}) %all-to-all-start) | async-done | bytes 524320 | tf_op jit(solution)/shard_map/all_to_all | solution.py:254
  54.1 0.0 copy-start
  54.1 0.8 copy-done
  54.9 4.5 %solve.3 = (f32[1024,128]{1,0:T(8,128)}, f32[256,512]{1,0:T(8,128)}) custom-call(f32[1024,128]{1,0:T(8,128)} %bitcast.22, bf16[512,512]{1,0:T(8,128)(2,1)} %constant.35.clone.ch.refs_1_, bf16[512,512]{1,0:T(8,128)(2,1)} %constant.36.clone.cl.refs_2_, bf16[128,128]{1,0:T(8,128)(2,1)} %constant.37.clone.refs_3_, bf16[128,128]{1,0:T(8,128)(2,1)} %constant.38.clone.refs_4_, ...), custom_call_target="tpu_custom_call" | custom-call | flops 1207959552 | bytes 3145728 | tf_op jit(solution)/shard_map/solve/pallas_call | solution.py:271
  59.4 26.8 %all_to_all.30 = f32[256,1,512]{2,1,0:T(1,128)} all-to-all(f32[256,1,512]{2,1,0:T(1,128)} %bitcast.27), channel_id=1, replica_groups=mesh['tm'=32,'space'=8] {'tm','space'}, dimensions={0} | all-to-all | bytes 1048576 | tf_op jit(solution)/shard_map/all_to_all | solution.py:254
  86.3 2.8 %backward.3 = (f32[4,64,512]{2,1,0:T(8,128)}, f32[64,512]{1,0:T(8,128)}, f32[4,512]{1,0:T(4,128)}) custom-call(f32[1024,128]{1,0:T(8,128)} %bitcast.17, bf16[512,512]{1,0:T(8,128)(2,1)} %constant.35.clone.ch.refs_1_, bf16[512,512]{1,0:T(8,128)(2,1)} %constant.36.clone.cl.refs_2_), custom_call_target="tpu_custom_call" | custom-call | flops 402653184 | bytes 1572864 | tf_op jit(solution)/shard_map/backward/pallas_call | solution.py:278
  89.0 1.0 collective-permute-start.2
  90.0 2.7 %collective-permute-start.3 = (f32[4,512]{1,0:T(4,128)}, f32[4,512]{1,0:T(4,128)S(1)}, u32[]{:S(2)}, u32[]{:S(2)}) collective-permute-start(f32[4,512]{1,0:T(4,128)} %get-tuple-element.39), channel_id=1, source_target_pairs={{1,0},{2,1},{3,2},{4,3},{5,4},{6,5},{7,6},{9,8},{10,9},{11,10},{12... | collective-permute-start | bytes 24584 | tf_op jit(solution)/shard_map/ppermute | solution.py:283
  92.7 2.4 collective-permute-done.3.refs_6_
  95.1 0.0 copy-start.6
  95.1 0.0 collective-permute-done.2.refs_5_
  95.1 0.0 copy-start.1
  95.1 0.6 copy-done.6
  95.7 0.1 copy-done.1
  95.8 6.4 %prox.4 = (f32[4,64,512]{2,1,0:T(8,128)}, f32[4,64,512]{2,1,0:T(8,128)}, f32[4,64,512]{2,1,0:T(8,128)}, f32[64,512]{1,0:T(8,128)}, f32[4,512]{1,0:T(4,128)}) custom-call(s32[1]{0:T(128)} %bitcast.refs_0_.place, f32[4,64,512]{2,1,0:T(8,128)} %get-tuple-element.31.nd.refs_1_.d, f32[4,64,512]{2,1,0:T(8,128)} %get-tuple-element.32.nx.refs_2_.fx, ...), custom_call_target="tpu_custom_call" | custom-call | flops 26214400 | bytes 4194304 | tf_op jit(solution)/shard_map/prox/pallas_call | solution.py:260
  102.2 0.5 collective-permute-start.4
  102.8 2.4 collective-permute-start.5
  105.2 1.0 collective-permute-done.5.bar_rows
  106.1 0.0 copy-start.9
  106.1 4.7 %collective-permute-done.4.bar_plane = f32[64,512]{1,0:T(8,128)S(1)} collective-permute-done((f32[64,512]{1,0:T(8,128)}, f32[64,512]{1,0:T(8,128)S(1)}, u32[]{:S(2)}, u32[]{:S(2)}) %collective-permute-start.4) | collective-permute-done | bytes 131104 | tf_op jit(solution)/shard_map/ppermute | solution.py:264
  110.8 0.0 copy-start.4
  110.8 0.0 copy-done.9
  110.8 0.6 copy-done.4
  111.5 4.0 %forward.4 = f32[1024,128]{1,0:T(8,128)} custom-call(s32[1]{0:T(128)} %bitcast.refs_0_.place, f32[4,64,512]{2,1,0:T(8,128)} %get-tuple-element.31.nd.refs_1_.d, f32[4,64,512]{2,1,0:T(8,128)} %get-tuple-element.32.nx.refs_2_.fx, f32[4,64,512]{2,1,0:T(8,128)} %get-tuple-element.33.ny.refs_3_.fy, f32[4,64,512]{2,1,0:T(8,128)} %get-tuple-element.40.nd.refs_1_.d, ...), custom_call_target="tpu_custom_call" | custom-call | flops 402653184 | bytes 4718592 | tf_op jit(solution)/shard_map/forward/pallas_call | solution.py:266
  115.5 27.8 %all_to_all.31 = f32[256,1,512]{2,1,0:T(1,128)} all-to-all(f32[256,1,512]{2,1,0:T(1,128)} %bitcast.21), channel_id=1, replica_groups=mesh['tm'=32,'space'=8] {'tm','space'}, dimensions={0} | all-to-all | bytes 1048576 | tf_op jit(solution)/shard_map/all_to_all | solution.py:254
  143.3 4.7 %solve.4 = (f32[1024,128]{1,0:T(8,128)}, f32[256,512]{1,0:T(8,128)}) custom-call(f32[1024,128]{1,0:T(8,128)} %bitcast.25, bf16[512,512]{1,0:T(8,128)(2,1)} %constant.35.clone.ch.refs_1_, bf16[512,512]{1,0:T(8,128)(2,1)} %constant.36.clone.cl.refs_2_, bf16[128,128]{1,0:T(8,128)(2,1)} %constant.37.clone.refs_3_, bf16[128,128]{1,0:T(8,128)(2,1)} %constant.38.clone.refs_4_, ...), custom_call_target="tpu_custom_call" | custom-call | flops 1207959552 | bytes 3145728 | tf_op jit(solution)/shard_map/solve/pallas_call | solution.py:271
  148.0 26.9 %all_to_all.32 = f32[256,1,512]{2,1,0:T(1,128)} all-to-all(f32[256,1,512]{2,1,0:T(1,128)} %bitcast.26), channel_id=1, replica_groups=mesh['tm'=32,'space'=8] {'tm','space'}, dimensions={0} | all-to-all | bytes 1048576 | tf_op jit(solution)/shard_map/all_to_all | solution.py:254
  174.8 2.8 %backward.4 = (f32[4,64,512]{2,1,0:T(8,128)}, f32[64,512]{1,0:T(8,128)}, f32[4,512]{1,0:T(4,128)}) custom-call(f32[1024,128]{1,0:T(8,128)} %bitcast.18, bf16[512,512]{1,0:T(8,128)(2,1)} %constant.35.clone.ch.refs_1_, bf16[512,512]{1,0:T(8,128)(2,1)} %constant.36.clone.cl.refs_2_), custom_call_target="tpu_custom_call" | custom-call | flops 402653184 | bytes 1572864 | tf_op jit(solution)/shard_map/backward/pallas_call | solution.py:278
  177.6 1.0 collective-permute-start.6
  178.6 2.7 %collective-permute-start.7 = (f32[4,512]{1,0:T(4,128)}, f32[4,512]{1,0:T(4,128)S(1)}, u32[]{:S(2)}, u32[]{:S(2)}) collective-permute-start(f32[4,512]{1,0:T(4,128)} %get-tuple-element.49), channel_id=1, source_target_pairs={{1,0},{2,1},{3,2},{4,3},{5,4},{6,5},{7,6},{9,8},{10,9},{11,10},{12... | collective-permute-start | bytes 24584 | tf_op jit(solution)/shard_map/ppermute | solution.py:283
  181.3 2.4 collective-permute-done.7.refs_6_
  183.7 0.0 collective-permute-done.6.refs_5_
  183.7 0.6 copy-done.7
  184.3 0.1 copy-done.2
  184.4 6.3 %prox.5 = (f32[4,64,512]{2,1,0:T(8,128)}, f32[4,64,512]{2,1,0:T(8,128)}, f32[4,64,512]{2,1,0:T(8,128)}, f32[64,512]{1,0:T(8,128)}, f32[4,512]{1,0:T(4,128)}) custom-call(s32[1]{0:T(128)} %bitcast.refs_0_.place, f32[4,64,512]{2,1,0:T(8,128)} %get-tuple-element.40.nd.refs_1_.d, f32[4,64,512]{2,1,0:T(8,128)} %get-tuple-element.41.nx.refs_2_.fx, ...), custom_call_target="tpu_custom_call" | custom-call | flops 26214400 | bytes 4194304 | tf_op jit(solution)/shard_map/prox/pallas_call | solution.py:260
  190.7 0.6 collective-permute-start.8
  191.3 2.4 collective-permute-start.9
  193.7 1.0 collective-permute-done.9.bar_rows
  194.7 4.7 %collective-permute-done.8.bar_plane = f32[64,512]{1,0:T(8,128)S(1)} collective-permute-done((f32[64,512]{1,0:T(8,128)}, f32[64,512]{1,0:T(8,128)S(1)}, u32[]{:S(2)}, u32[]{:S(2)}) %collective-permute-start.8) | collective-permute-done | bytes 131104 | tf_op jit(solution)/shard_map/ppermute | solution.py:264
  199.3 0.0 copy-done.8
  199.3 0.6 copy-done.3
  200.0 4.1 %forward.5 = f32[1024,128]{1,0:T(8,128)} custom-call(s32[1]{0:T(128)} %bitcast.refs_0_.place, f32[4,64,512]{2,1,0:T(8,128)} %get-tuple-element.40.nd.refs_1_.d, f32[4,64,512]{2,1,0:T(8,128)} %get-tuple-element.41.nx.refs_2_.fx, f32[4,64,512]{2,1,0:T(8,128)} %get-tuple-element.42.ny.refs_3_.fy, f32[4,64,512]{2,1,0:T(8,128)} %get-tuple-element.27.nd, ...), custom_call_target="tpu_custom_call" | custom-call | flops 402653184 | bytes 4718592 | tf_op jit(solution)/shard_map/forward/pallas_call | solution.py:266
  204.1 27.8 %all_to_all.33 = f32[256,1,512]{2,1,0:T(1,128)} all-to-all(f32[256,1,512]{2,1,0:T(1,128)} %bitcast.20), channel_id=1, replica_groups=mesh['tm'=32,'space'=8] {'tm','space'}, dimensions={0} | all-to-all | bytes 1048576 | tf_op jit(solution)/shard_map/all_to_all | solution.py:254
  231.8 4.7 %solve.5 = (f32[1024,128]{1,0:T(8,128)}, f32[256,512]{1,0:T(8,128)}) custom-call(f32[1024,128]{1,0:T(8,128)} %bitcast.23, bf16[512,512]{1,0:T(8,128)(2,1)} %constant.35.clone.ch.refs_1_, bf16[512,512]{1,0:T(8,128)(2,1)} %constant.36.clone.cl.refs_2_, bf16[128,128]{1,0:T(8,128)(2,1)} %constant.37.clone.refs_3_, bf16[128,128]{1,0:T(8,128)(2,1)} %constant.38.clone.refs_4_, ...), custom_call_target="tpu_custom_call" | custom-call | flops 1207959552 | bytes 3145728 | tf_op jit(solution)/shard_map/solve/pallas_call | solution.py:271
  236.5 26.9 %all_to_all.34 = f32[256,1,512]{2,1,0:T(1,128)} all-to-all(f32[256,1,512]{2,1,0:T(1,128)} %bitcast.24), channel_id=1, replica_groups=mesh['tm'=32,'space'=8] {'tm','space'}, dimensions={0} | all-to-all | bytes 1048576 | tf_op jit(solution)/shard_map/all_to_all | solution.py:254
  263.4 2.8 %backward.5 = (f32[4,64,512]{2,1,0:T(8,128)}, f32[64,512]{1,0:T(8,128)}, f32[4,512]{1,0:T(4,128)}) custom-call(f32[1024,128]{1,0:T(8,128)} %bitcast.16, bf16[512,512]{1,0:T(8,128)(2,1)} %constant.35.clone.ch.refs_1_, bf16[512,512]{1,0:T(8,128)(2,1)} %constant.36.clone.cl.refs_2_), custom_call_target="tpu_custom_call" | custom-call | flops 402653184 | bytes 1572864 | tf_op jit(solution)/shard_map/backward/pallas_call | solution.py:278
  (5 shorter events, 0.0 us)
Async XLA Ops:
  6.6 12.0 %collective-permute-start = (f32[64,512]{1,0:T(8,128)}, f32[64,512]{1,0:T(8,128)S(1)}, u32[]{:S(2)}, u32[]{:S(2)}) collective-permute-start(f32[64,512]{1,0:T(8,128)} %get-tuple-element.34), channel_id=1, source_target_pairs={{0,8},{8,16},{16,24},{24,32},{32,40},{40,48},{48,56},{56,64},{64,7... | collective-permute-start | bytes 393224 | tf_op jit(solution)/shard_map/ppermute | solution.py:264
  9.0 5.0 %collective-permute-start.1 = (f32[4,512]{1,0:T(4,128)}, f32[4,512]{1,0:T(4,128)S(1)}, u32[]{:S(2)}, u32[]{:S(2)}) collective-permute-start(f32[4,512]{1,0:T(4,128)} %get-tuple-element.35), channel_id=1, source_target_pairs={{0,1},{1,2},{2,3},{3,4},{4,5},{5,6},{6,7},{8,9},{9,10},{10,11},{11... | collective-permute-start | bytes 24584 | tf_op jit(solution)/shard_map/ppermute | solution.py:265
  14.0 4.5 %copy-start.10 = (f32[4,512]{1,0:T(4,128)}, f32[4,512]{1,0:T(4,128)S(1)}, u32[]{:S(2)}) copy-start(f32[4,512]{1,0:T(4,128)S(1)} %collective-permute-done.1.bar_rows) | copy-start | bytes 24580
  18.6 0.7 copy-start.5
  23.2 30.9 %all-to-all-start = ((f32[256,1,512]{2,1,0:T(1,128)}), f32[256,1,512]{2,1,0:T(1,128)S(1)}, u32[]{:S(2)}, u32[]{:S(2)}) async-start(f32[256,1,512]{2,1,0:T(1,128)} %bitcast.19), calls=%async_computation | async-start | bytes 1048576 | tf_op jit(solution)/shard_map/all_to_all | solution.py:254
  33.6 0.7 copy-start.11
  34.2 0.7 copy-start.12
  54.1 0.8 copy-start
  89.0 6.1 %collective-permute-start.2 = (f32[64,512]{1,0:T(8,128)}, f32[64,512]{1,0:T(8,128)S(1)}, u32[]{:S(2)}, u32[]{:S(2)}) collective-permute-start(f32[64,512]{1,0:T(8,128)} %get-tuple-element.38), channel_id=1, source_target_pairs={{8,0},{16,8},{24,16},{32,24},{40,32},{48,40},{56,48},{64,56},{72,6... | collective-permute-start | bytes 393224 | tf_op jit(solution)/shard_map/ppermute | solution.py:283
  90.0 5.2 %collective-permute-start.3 = (f32[4,512]{1,0:T(4,128)}, f32[4,512]{1,0:T(4,128)S(1)}, u32[]{:S(2)}, u32[]{:S(2)}) collective-permute-start(f32[4,512]{1,0:T(4,128)} %get-tuple-element.39), channel_id=1, source_target_pairs={{1,0},{2,1},{3,2},{4,3},{5,4},{6,5},{7,6},{9,8},{10,9},{11,10},{12... | collective-permute-start | bytes 24584 | tf_op jit(solution)/shard_map/ppermute | solution.py:283
  95.1 0.6 copy-start.6
  95.1 0.7 copy-start.1
  102.2 8.6 %collective-permute-start.4 = (f32[64,512]{1,0:T(8,128)}, f32[64,512]{1,0:T(8,128)S(1)}, u32[]{:S(2)}, u32[]{:S(2)}) collective-permute-start(f32[64,512]{1,0:T(8,128)} %get-tuple-element.43), channel_id=1, source_target_pairs={{0,8},{8,16},{16,24},{24,32},{32,40},{40,48},{48,56},{56,64},{64,7... | collective-permute-start | bytes 393224 | tf_op jit(solution)/shard_map/ppermute | solution.py:264
  102.8 3.4 %collective-permute-start.5 = (f32[4,512]{1,0:T(4,128)}, f32[4,512]{1,0:T(4,128)S(1)}, u32[]{:S(2)}, u32[]{:S(2)}) collective-permute-start(f32[4,512]{1,0:T(4,128)} %get-tuple-element.44), channel_id=1, source_target_pairs={{0,1},{1,2},{2,3},{3,4},{4,5},{5,6},{6,7},{8,9},{9,10},{10,11},{11... | collective-permute-start | bytes 24584 | tf_op jit(solution)/shard_map/ppermute | solution.py:265
  106.1 4.7 %copy-start.9 = (f32[4,512]{1,0:T(4,128)}, f32[4,512]{1,0:T(4,128)S(1)}, u32[]{:S(2)}) copy-start(f32[4,512]{1,0:T(4,128)S(1)} %collective-permute-done.5.bar_rows) | copy-start | bytes 24580
  110.8 0.6 copy-start.4
  177.6 6.1 %collective-permute-start.6 = (f32[64,512]{1,0:T(8,128)}, f32[64,512]{1,0:T(8,128)S(1)}, u32[]{:S(2)}, u32[]{:S(2)}) collective-permute-start(f32[64,512]{1,0:T(8,128)} %get-tuple-element.48), channel_id=1, source_target_pairs={{8,0},{16,8},{24,16},{32,24},{40,32},{48,40},{56,48},{64,56},{72,6... | collective-permute-start | bytes 393224 | tf_op jit(solution)/shard_map/ppermute | solution.py:283
  178.6 5.2 %collective-permute-start.7 = (f32[4,512]{1,0:T(4,128)}, f32[4,512]{1,0:T(4,128)S(1)}, u32[]{:S(2)}, u32[]{:S(2)}) collective-permute-start(f32[4,512]{1,0:T(4,128)} %get-tuple-element.49), channel_id=1, source_target_pairs={{1,0},{2,1},{3,2},{4,3},{5,4},{6,5},{7,6},{9,8},{10,9},{11,10},{12... | collective-permute-start | bytes 24584 | tf_op jit(solution)/shard_map/ppermute | solution.py:283
  183.7 0.6 copy-start.7
  183.7 0.7 copy-start.2
  190.7 8.6 %collective-permute-start.8 = (f32[64,512]{1,0:T(8,128)}, f32[64,512]{1,0:T(8,128)S(1)}, u32[]{:S(2)}, u32[]{:S(2)}) collective-permute-start(f32[64,512]{1,0:T(8,128)} %get-tuple-element.53), channel_id=1, source_target_pairs={{0,8},{8,16},{16,24},{24,32},{32,40},{40,48},{48,56},{56,64},{64,7... | collective-permute-start | bytes 393224 | tf_op jit(solution)/shard_map/ppermute | solution.py:264
  191.3 3.4 %collective-permute-start.9 = (f32[4,512]{1,0:T(4,128)}, f32[4,512]{1,0:T(4,128)S(1)}, u32[]{:S(2)}, u32[]{:S(2)}) collective-permute-start(f32[4,512]{1,0:T(4,128)} %get-tuple-element.54), channel_id=1, source_target_pairs={{0,1},{1,2},{2,3},{3,4},{4,5},{5,6},{6,7},{8,9},{9,10},{10,11},{11... | collective-permute-start | bytes 24584 | tf_op jit(solution)/shard_map/ppermute | solution.py:265
  194.7 4.7 %copy-start.8 = (f32[4,512]{1,0:T(4,128)}, f32[4,512]{1,0:T(4,128)S(1)}, u32[]{:S(2)}) copy-start(f32[4,512]{1,0:T(4,128)S(1)} %collective-permute-done.9.bar_rows) | copy-start | bytes 24580
  199.3 0.6 copy-start.3

commit v2 on v1

v2 whole, which is shorter than its diff:
```python
import functools

import jax
import jax.numpy as jnp
import numpy as np
from jax import lax
from jax.experimental import pallas as pl
from jax.experimental.pallas import tpu as pltpu
from jax.sharding import PartitionSpec as P

ITERS = 3
NEWTON = 10
TAU_STEP = 1.0
SLOW_LOOP = 2.25
INTERPRET = False
BOTH = ("tm", "space")
f32 = jnp.float32
bf16 = jnp.bfloat16
NN = (((1,), (0,)), ((), ()))
NT = (((1,), (1,)), ((), ()))
TN = (((0,), (0,)), ((), ()))


def halves(value):
    high = value.astype(bf16)
    return high, (value - high.astype(f32)).astype(bf16)


def dot3(left, right, dims):
    dot = functools.partial(lax.dot_general, dimension_numbers=dims, preferred_element_type=f32)
    return dot(left[0], right[0]) + (dot(left[0], right[1]) + dot(left[1], right[0]))


def cosine_matrix(points):
    one = np.float32
    frequency = np.arange(points, dtype=one)[:, None]
    sample = np.arange(points, dtype=one)[None, :]
    scaling = np.where(frequency == 0, np.sqrt(one(1.0 / points)), np.sqrt(one(2.0 / points))).astype(one)
    angle = one(np.pi) * (sample + one(0.5)) * frequency / one(points)
    return (scaling * np.cos(angle.astype(np.float64)).astype(one)).astype(one)


def neumann_spectrum(points):
    half_angle = np.pi * np.arange(points) / (2.0 * points)
    return (4.0 * np.sin(half_angle) ** 2).astype(np.float32)


def loop_basis(length, slabs):
    rows = [np.full(length, np.sqrt(1.0 / length))]
    values = [0.0]
    moment = np.arange(length)
    for k in range(1, length // 2):
        angle = 2.0 * np.pi * ((k * moment) % length) / length
        rows += [np.sqrt(2.0 / length) * np.cos(angle), np.sqrt(2.0 / length) * np.sin(angle)]
        values += [4.0 * np.sin(np.pi * k / length) ** 2] * 2
    rows.append(np.sqrt(1.0 / length) * (-1.0) ** moment)
    values.append(4.0)
    basis = np.stack(rows).reshape(length, slabs, length // slabs).transpose(0, 2, 1).reshape(length, length)
    return basis.astype(np.float32), np.asarray(values, np.float32)


def np_halves(matrix):
    high = matrix.astype(bf16)
    return high, (matrix - high.astype(np.float32)).astype(bf16)


def call(body, outs, scratch=(), scalars=0, n_in=0, cost=None, **kw):
    vmem = pl.BlockSpec(memory_space=pltpu.VMEM)
    smem = pl.BlockSpec(memory_space=pltpu.SMEM)
    return pl.pallas_call(
        body,
        out_shape=[jax.ShapeDtypeStruct(s, f32) for s in outs],
        in_specs=[smem] * scalars + [vmem] * n_in,
        out_specs=[vmem] * len(outs),
        scratch_shapes=list(scratch),
        cost_estimate=pl.CostEstimate(flops=int(cost[0]), bytes_accessed=int(cost[1]), transcendentals=0),
        interpret=INTERPRET,
        **kw,
    )


def newton(mass, along_x, along_y):
    target = 0.5 * TAU_STEP * (along_x * along_x + along_y * along_y)
    root = jnp.maximum(mass, 0.0) + jnp.exp(jnp.log(target) * (1.0 / 3.0))
    shifted = root + TAU_STEP
    base = mass + TAU_STEP
    base_twice = base + base
    for _ in range(NEWTON):
        twice = shifted + shifted
        above = (shifted * shifted) * (twice - base) + target
        below = shifted * ((twice + shifted) - base_twice)
        shifted = jnp.maximum(above / below, TAU_STEP)
    root = shifted - TAU_STEP
    factor = root / shifted
    return root, factor * along_x, factor * along_y


def prox_cells(source, result):
    steps, rows, width = result[0].shape
    chunk = 16
    per = rows // chunk

    def step(index, carry):
        t = index // per
        span = pl.ds(pl.multiple_of((index % per) * chunk, chunk), chunk)
        out = newton(*[ref[t, span, :] for ref in source])
        for ref, value in zip(result, out):
            ref[t, span, :] = value
        return carry

    lax.fori_loop(0, steps * per, step, 0)


def transform_back(y, ch, cl, u, pairs, group):
    cosine = (ch[...], cl[...])
    count = y.shape[0] // group
    lanes = y.shape[1]
    for pair in range(pairs):
        even = y[pl.ds(pair, count, stride=group), :]
        odd = y[pl.ds(group // 2 + pair, count, stride=group), :]
        u[pair * lanes : (pair + 1) * lanes, :] = dot3(halves(jnp.concatenate([even, odd], axis=0)), cosine, TN)


def dual_step(d, fx, fy, edge, u, nd, nx, ny):
    steps, rows, width = d.shape
    below_at = (steps + 1) * rows
    above_at = below_at + 8
    end_row = lax.broadcasted_iota(jnp.int32, (rows, width), 0) == rows - 1
    end_column = lax.broadcasted_iota(jnp.int32, (rows, width), 1) == width - 1
    for t in range(steps):
        here = u[t * rows : (t + 1) * rows, :]
        later = u[(t + 1) * rows : (t + 2) * rows, :]
        below = jnp.where(end_row, u[below_at + t : below_at + t + 1, :], pltpu.roll(here, rows - 1, 0))
        right = jnp.where(end_column, here, pltpu.roll(here, width - 1, 1))
        nd[t] = d[t] - TAU_STEP * (here - later)
        nx[t] = fx[t] - TAU_STEP * (here - below)
        ny[t] = fy[t] - TAU_STEP * (here - right)
    here = u[above_at : above_at + steps, :]
    later = u[above_at + 1 : above_at + 1 + steps, :]
    below = jnp.concatenate([u[t * rows : t * rows + 1, :] for t in range(steps)], axis=0)
    right = jnp.where(end_column[:steps, :], here, pltpu.roll(here, width - 1, 1))
    return (
        edge[0] - TAU_STEP * (here - later),
        edge[1] - TAU_STEP * (here - below),
        edge[2] - TAU_STEP * (here - right),
    )


def residual_modes(place, last_place, d, fx, fy, nd, nx, ny, src, edge_x, new_edge_x, ch, cl, out, rh, rl):
    steps, rows, width = d.shape
    shape = (rows, width)
    row = lax.broadcasted_iota(jnp.int32, shape, 0)
    column = lax.broadcasted_iota(jnp.int32, shape, 1)
    final_row = (row == rows - 1) & (place == last_place)
    edge_bar = jnp.where(place == 0, 0.0, 2.0 * new_edge_x - edge_x)
    before = None
    for t in range(steps):
        mass = 2.0 * nd[t] - d[t]
        along_x = 2.0 * nx[t] - fx[t]
        along_y = 2.0 * ny[t] - fy[t]
        x_before = jnp.where(row == 0, edge_bar[t : t + 1, :], pltpu.roll(along_x, 1, 0))
        y_before = jnp.where(column == 0, 0.0, pltpu.roll(along_y, 1, 1))
        value = mass if before is None else mass - before
        value = value + (jnp.where(final_row, 0.0, along_x) - x_before)
        value = value + (jnp.where(column == width - 1, 0.0, along_y) - y_before)
        value = value - src[t]
        before = mass
        high, low = halves(value)
        rh[t * rows : (t + 1) * rows, :] = high
        rl[t * rows : (t + 1) * rows, :] = low
    high, low = halves(before)
    for t in (steps, steps + 1):
        rh[t * rows : (t + 1) * rows, :] = high
        rl[t * rows : (t + 1) * rows, :] = low
    modes = dot3((ch[...], cl[...]), (rh[...], rl[...]), NT)
    lanes = 2 * rows
    pairs = steps // 2
    count = width // 2
    group = 2 * pairs + 1
    for pair in range(pairs):
        span = slice(pair * lanes, (pair + 1) * lanes)
        out[pl.ds(pair, count, stride=group), :] = modes[:count, span]
        out[pl.ds(pairs + pair, count, stride=group), :] = modes[count:, span]
    span = slice(pairs * lanes, (pairs + 1) * lanes)
    low_half = lax.broadcasted_iota(jnp.int32, (count, lanes), 1) < rows
    out[pl.ds(2 * pairs, count, stride=group), :] = jnp.where(low_half, modes[:count, span], modes[count:, span])


def prox_body(d, fx, fy, nd, nx, ny):
    prox_cells((d, fx, fy), (nd, nx, ny))


def forward_body(last_place, place, d, fx, fy, nd, nx, ny, src, edge, ch, cl, out, new_edge, rh, rl):
    fresh = newton(edge[0], edge[1], edge[2])
    for k in range(3):
        new_edge[k] = fresh[k]
    residual_modes(place[0], last_place, d, fx, fy, nd, nx, ny, src, edge[1], fresh[1], ch, cl, out, rh, rl)


def middle_body(last_place, place, y, d, fx, fy, src, edge, ch, cl, nd, nx, ny, out, new_edge, u, rh, rl):
    steps = d.shape[0]
    pairs = steps // 2 + 1
    transform_back(y, ch, cl, u, pairs, 2 * pairs)
    fresh = newton(*dual_step(d, fx, fy, edge, u, nd, nx, ny))
    for k in range(3):
        new_edge[k] = fresh[k]
    prox_cells((nd, nx, ny), (nd, nx, ny))
    residual_modes(place[0], last_place, d, fx, fy, nd, nx, ny, src, edge[1], fresh[1], ch, cl, out, rh, rl)


def last_body(y, ch, cl, u, flat):
    steps, rows, _ = u.shape
    transform_back(y, ch, cl, flat, steps // 2, steps)
    for t in range(steps):
        u[t] = flat[t * rows : (t + 1) * rows, :]


def solve_body(slabs, places, steps, with_sum, with_edges, *refs):
    if with_sum:
        z, ch, cl, wh, wl, vh, vl, den, so_far, out, total, field = refs
    else:
        z, ch, cl, wh, wl, vh, vl, den, out, total, field = refs
    length = slabs * steps
    pairs = steps // 2
    lanes = z.shape[1]
    rows = lanes // 2
    lane = lax.broadcasted_iota(jnp.int32, (slabs, lanes), 1)
    low_half = lane < rows

    def swap(a, b):
        return jnp.where(low_half, a, pltpu.roll(b, rows, 1)), jnp.where(low_half, pltpu.roll(a, rows, 1), b)

    group = 2 * pairs + 1

    def arrived(place, item):
        return z[pl.ds(place * group + item, slabs, stride=places * group), :]

    for q in range(places // 2):
        span = slice(q * lanes, (q + 1) * lanes)
        planes = swap(arrived(2 * q, 2 * pairs), arrived(2 * q + 1, 2 * pairs))
        for mode in range(2):
            for pair in range(pairs):
                item = mode * pairs + pair
                first, second = swap(arrived(2 * q, item), arrived(2 * q + 1, item))
                if pair == 0:
                    first = first - pltpu.roll(planes[mode], 1, 0)
                top = mode * length + 2 * pair * slabs
                field[top : top + slabs, span] = first
                field[top + slabs : top + 2 * slabs, span] = second
    cosine = (ch[...], cl[...])
    for mode in range(2):
        span = slice(mode * length, (mode + 1) * length)
        field[span, :] = dot3((wh[...], wl[...]), halves(field[span, :]), NN)
    solved = dot3(halves(field[...]), cosine, NT) / den[...]
    if with_sum:
        solved = solved + so_far[...]
    total[...] = solved
    field[...] = dot3(halves(solved), cosine, NN)
    for mode in range(2):
        span = slice(mode * length, (mode + 1) * length)
        field[span, :] = dot3((vh[...], vl[...]), halves(field[span, :]), NN)
    per_mode = pairs + 1 if with_edges else pairs
    group_out = 2 * per_mode

    def leaving(place, item):
        return pl.ds(place * group_out + item, slabs, stride=places * group_out)

    for mode in range(2):
        top = mode * length
        for q in range(places // 2):
            span = slice(q * lanes, (q + 1) * lanes)
            for pair in range(pairs):
                at = top + 2 * pair * slabs
                first, second = swap(field[at : at + slabs, span], field[at + slabs : at + 2 * slabs, span])
                out[leaving(2 * q, mode * per_mode + pair), :] = first
                out[leaving(2 * q + 1, mode * per_mode + pair), :] = second
            if not with_edges:
                continue
            ahead = pltpu.roll(field[top : top + slabs, span], slabs - 1, 0)
            for place, value in ((2 * q, ahead), (2 * q + 1, pltpu.roll(ahead, rows, 1))):
                after = (place + 1) * rows if place + 1 < places else (place + 1) * rows - 1
                for t in range(steps):
                    column = field[top + t * slabs : top + (t + 1) * slabs, after : after + 1]
                    value = jnp.where(lane == rows + t, column, value)
                if place:
                    before = place * rows - 1
                    for t in range(steps + 1):
                        column = field[top + (t % steps) * slabs : top + (t % steps + 1) * slabs, before : before + 1]
                        if t == steps:
                            column = pltpu.roll(jnp.broadcast_to(column, (slabs, lanes)), slabs - 1, 0)
                        value = jnp.where(lane == rows + 8 + t, column, value)
                out[leaving(place, mode * per_mode + pairs), :] = value


def local(density, flux_x, flux_y, source):
    steps, rows, width = density.shape
    slabs = lax.axis_size("tm")
    places = lax.axis_size("space")
    length = steps * slabs
    screen = SLOW_LOOP / float(length * length)
    order = np.concatenate([np.arange(0, width, 2), np.arange(1, width, 2)])
    ch, cl = (jnp.asarray(m) for m in np_halves(cosine_matrix(width)[order]))
    basis, loop_values = loop_basis(length, slabs)
    wh, wl = (jnp.asarray(m) for m in np_halves(basis))
    vh, vl = (jnp.asarray(m) for m in np_halves(np.ascontiguousarray(basis.T)))
    spectrum = neumann_spectrum(width)
    place = lax.axis_index("space")
    first = 2 * (lax.axis_index("tm") * places + place)
    own = lax.dynamic_slice_in_dim(jnp.asarray(spectrum), first, 2)
    den = own[:, None, None] + jnp.asarray(loop_values)[None, :, None] + jnp.asarray(spectrum[order])[None, None, :]
    den = (den + screen).reshape(2 * length, width)
    place = place.astype(jnp.int32).reshape(1)
    nbytes = density.size * 4
    mega = density.size * width * 6
    field = (steps, rows, width)
    edge_shape = (3, steps, width)
    lanes = 2 * rows
    devices = slabs * places

    def packed(items):
        return (devices * items, lanes)

    forward_items = steps + 1
    backward_items = steps + 2

    def exchange(value):
        shape = value.shape
        value = value.reshape(devices, 1, shape[0] // devices * lanes)
        value = lax.all_to_all(value, BOTH, split_axis=0, concat_axis=0, tiled=True)
        return value.reshape(shape)

    edge = jnp.stack([density[:, rows - 1], flux_x[:, rows - 1], flux_y[:, rows - 1]])
    edge = lax.ppermute(edge, "space", [(i, i + 1) for i in range(places - 1)])
    split = [pltpu.VMEM(((steps + 2) * rows, width), bf16)] * 2
    new_d, new_x, new_y = call(
        prox_body, [field] * 3, n_in=3, cost=(density.size * 200, 6 * nbytes), name="prox"
    )(density, flux_x, flux_y)
    modes, edge = call(
        functools.partial(forward_body, places - 1), [packed(forward_items), edge_shape],
        scratch=split, scalars=1, n_in=10, cost=(mega, 8 * nbytes), name="forward",
    )(place, density, flux_x, flux_y, new_d, new_x, new_y, source, edge, ch, cl)
    density, flux_x, flux_y = new_d, new_x, new_y
    total = ()
    for iteration in range(ITERS):
        final = iteration + 1 == ITERS
        modes = exchange(modes)
        modes, solved = call(
            functools.partial(solve_body, slabs, places, steps, bool(total), not final),
            [packed(steps if final else backward_items), (2 * length, width)],
            scratch=[pltpu.VMEM((2 * length, width), f32)],
            n_in=8 + len(total), cost=(3 * mega, 6 * nbytes), name="solve",
        )(modes, ch, cl, wh, wl, vh, vl, den, *total)
        total = (solved,)
        modes = exchange(modes)
        if final:
            break
        density, flux_x, flux_y, modes, edge = call(
            functools.partial(middle_body, places - 1), [field] * 3 + [packed(forward_items), edge_shape],
            scratch=[pltpu.VMEM(((steps + 2) * rows, width), f32)] + split,
            scalars=1, n_in=8, cost=(2 * mega, 10 * nbytes), name="middle",
        )(place, modes, density, flux_x, flux_y, source, edge, ch, cl)
    (potential,) = call(
        last_body, [field], scratch=[pltpu.VMEM((steps * rows, width), f32)], n_in=3, cost=(mega, 3 * nbytes), name="last"
    )(modes, ch, cl)
    return density, flux_x, flux_y, potential


def solution(mesh):
    spec = P("tm", "space", None)
    return jax.shard_map(local, mesh=mesh, in_specs=(spec,) * 4, out_specs=(spec,) * 4, check_vma=False)
```

time: 267 us -> 244 us (0.914)
  waiting for transfers between devices: 39.9 us -> 20.2 us
  blocking collectives: 136 us -> 152 us
  starting transfers between devices: 30 us -> 18.6 us
  Pallas kernels: 53 us -> 44.9 us
    ppermute x10 -> x1, waiting for transfers between devices: 21.7 us -> 0.01 us  [local(): edge = lax.ppermute(edge, 'space', [(i, i + 1) for i in range(places - 1)])]
    all_to_all x5, blocking collectives: 136 us -> 152 us  [exchange(): value = lax.all_to_all(value, BOTH, split_axis=0, concat_axis=0, tiled=True)]
    ppermute x10 -> x1, starting transfers between devices: 19.7 us -> 4.58 us  [local(): edge = lax.ppermute(edge, 'space', [(i, i + 1) for i in range(places - 1)])]
    pallas_call x12 -> x8, Pallas kernels: 53 us -> 44.9 us  [the longest x2 17 us: local(): call(functools.partial(middle_body, places - 1), [field] * 3 + [packed(fo...]
    all_to_all x1, starting transfers between devices: 10.3 us -> 14 us  [exchange(): value = lax.all_to_all(value, BOTH, split_axis=0, concat_axis=0, tiled=True)]
    unnamed x26 -> x9, local copies, waits for them, and re-layouts: 5.31 us -> 2.08 us
  transfers between devices with their start and end apart: 11 -> 2, of which waited for: 9 -> 1; matrix products, arithmetic and copies ran while one was open for 0% -> 1% of each run, Pallas kernels for 0% -> 2%
where the time goes in v2:
time: 244 us; the launch traced here: 243 us
  blocking collectives  152 us (62%)
  Pallas kernels  44.9 us (18%)
  waiting for transfers between devices  20.2 us (8%)
  starting transfers between devices  18.6 us (8%)
  local copies, waits for them, and re-layouts  5.4 us (2%)
    all_to_all x5, blocking collectives, exchange(): value = lax.all_to_all(value, BOTH, split_axis=0, concat_axis=0, tiled=True)  152 us
    all_to_all x1, waiting for transfers between devices, exchange(): value = lax.all_to_all(value, BOTH, split_axis=0, concat_axis=0, tiled=True)  20.2 us
    pallas_call x2, Pallas kernels, local(): call(functools.partial(middle_body, places - 1), [field] * 3 + [packed(fo...  17 us
    pallas_call x3, Pallas kernels, local(): call(functools.partial(solve_body, slabs, places, steps, bool(total), not...  15.1 us
    all_to_all x1, starting transfers between devices, exchange(): value = lax.all_to_all(value, BOTH, split_axis=0, concat_axis=0, tiled=True)  14 us
    pallas_call x1, Pallas kernels, local(): call(prox_body, [field] * 3, n_in=3, cost=(density.size * 200, 6 * nbytes...  5.47 us
  transfers between devices with their start and end apart: 2, of which 1 were waited for; matrix products, arithmetic and copies ran while one was open for 1% of the time, Pallas kernels for 2%

profile of v2, /device:TPU:1, one launch (start us, length us, event | category | flops | bytes accessed | tf_op | source)
XLA Modules:
  0.0 243.0 jit_solution(17302995313400116675)
XLA Ops:
  0.6 0.9 slice.9
  1.5 0.9 slice.10
  2.3 0.8 slice.11
  3.2 4.6 %collective-permute-start = (f32[3,4,512]{2,1,0:T(4,128)S(1)}, f32[3,4,512]{2,1,0:T(4,128)S(1)}, u32[]{:S(2)}, u32[]{:S(2)}) collective-permute-start(f32[3,4,512]{2,1,0:T(4,128)S(1)} %pad_maximum_fusion), channel_id=1, source_target_pairs={{0,1},{1,2},{2,3},{3,4},{4,5},{5,6},{6,7},{8,9},{9,10},{10,11},{11... | collective-permute-start | bytes 73736 | tf_op jit(solution)/shard_map/ppermute | solution.py:333
  7.8 5.5 %prox.1 = (f32[4,64,512]{2,1,0:T(8,128)}, f32[4,64,512]{2,1,0:T(8,128)}, f32[4,64,512]{2,1,0:T(8,128)}) custom-call(f32[4,64,512]{2,1,0:T(8,128)} %d.3, f32[4,64,512]{2,1,0:T(8,128)} %fx.3, f32[4,64,512]{2,1,0:T(8,128)} %fy.3), custom_call_target="tpu_custom_call" | custom-call | flops 26214400 | bytes 3145728 | tf_op jit(solution)/shard_map/prox/pallas_call | solution.py:335
  13.3 0.0 collective-permute-done.edge
  13.3 0.0 copy-start.1
  13.3 0.6 copy-done.1
  13.9 4.5 %forward.1 = (f32[1280,128]{1,0:T(8,128)}, f32[3,4,512]{2,1,0:T(4,128)}) custom-call(s32[1]{0:T(128)} %bitcast.place, f32[4,64,512]{2,1,0:T(8,128)} %d.3, f32[4,64,512]{2,1,0:T(8,128)} %fx.3, f32[4,64,512]{2,1,0:T(8,128)} %fy.3, f32[4,64,512]{2,1,0:T(8,128)} %get-tuple-element.23.nd.d, f32[4,64,512]{2,1,0:T(8,128)} %get-tuple-element.24.nx.fx, ...), custom_call_target="tpu_custom_call" | custom-call | flops 402653184 | bytes 4194304 | tf_op jit(solution)/shard_map/forward/pallas_call | solution.py:338
  18.4 14.0 %all-to-all-start = ((f32[256,1,640]{2,1,0:T(1,128)}), f32[256,1,640]{2,1,0:T(1,128)S(1)}, u32[]{:S(2)}, u32[]{:S(2)}) async-start(f32[256,1,640]{2,1,0:T(1,128)} %bitcast.29), calls=%async_computation | async-start | bytes 1310720 | tf_op jit(solution)/shard_map/all_to_all | solution.py:329
  32.4 0.0 copy-start.3
  32.4 0.8 dynamic_slice.3
  33.2 0.0 copy-done.3
  33.2 0.0 copy-start.2
  33.2 0.1 bitcast_add_fusion
  33.2 0.6 copy-done.2
  33.8 0.9 add_add_fusion.refs_7_
  34.7 20.2 %all-to-all-done = f32[256,1,640]{2,1,0:T(1,128)S(1)} async-done(((f32[256,1,640]{2,1,0:T(1,128)}), f32[256,1,640]{2,1,0:T(1,128)S(1)}, u32[]{:S(2)}, u32[]{:S(2)}) %all-to-all-start) | async-done | bytes 655392 | tf_op jit(solution)/shard_map/all_to_all | solution.py:329
  55.0 0.0 copy-start
  55.0 0.8 copy-done
  55.8 5.2 %solve.3 = (f32[1536,128]{1,0:T(8,128)}, f32[256,512]{1,0:T(8,128)}) custom-call(f32[1280,128]{1,0:T(8,128)} %bitcast.28, bf16[512,512]{1,0:T(8,128)(2,1)} %constant.37.clone.ch.refs_1_, bf16[512,512]{1,0:T(8,128)(2,1)} %constant.38.clone.cl.refs_2_, bf16[128,128]{1,0:T(8,128)(2,1)} %constant.39.clone.refs_3_, bf16[128,128]{1,0:T(8,128)(2,1)} %constant.40.clone.refs_4_, ...), custom_call_target="tpu_custom_call" | custom-call | flops 1207959552 | bytes 3145728 | tf_op jit(solution)/shard_map/solve/pallas_call | solution.py:347
  61.0 32.5 %all_to_all.30 = f32[256,1,768]{2,1,0:T(1,128)} all-to-all(f32[256,1,768]{2,1,0:T(1,128)} %bitcast.27), channel_id=1, replica_groups=mesh['tm'=32,'space'=8] {'tm','space'}, dimensions={0} | all-to-all | bytes 1572864 | tf_op jit(solution)/shard_map/all_to_all | solution.py:329
  93.5 8.5 %middle.2 = (f32[4,64,512]{2,1,0:T(8,128)}, f32[4,64,512]{2,1,0:T(8,128)}, f32[4,64,512]{2,1,0:T(8,128)}, f32[1280,128]{1,0:T(8,128)}, f32[3,4,512]{2,1,0:T(4,128)}) custom-call(s32[1]{0:T(128)} %bitcast.place, f32[1536,128]{1,0:T(8,128)} %bitcast.24, f32[4,64,512]{2,1,0:T(8,128)} %get-tuple-element.23.nd.d, f32[4,64,512]{2,1,0:T(8,128)} %get-tuple-element.24.nx.fx, ...), custom_call_target="tpu_custom_call" | custom-call | flops 805306368 | bytes 5242880 | tf_op jit(solution)/shard_map/middle/pallas_call | solution.py:357
  102.0 29.8 %all_to_all.31 = f32[256,1,640]{2,1,0:T(1,128)} all-to-all(f32[256,1,640]{2,1,0:T(1,128)} %bitcast.31), channel_id=1, replica_groups=mesh['tm'=32,'space'=8] {'tm','space'}, dimensions={0} | all-to-all | bytes 1310720 | tf_op jit(solution)/shard_map/all_to_all | solution.py:329
  131.7 5.3 %solve.4 = (f32[1536,128]{1,0:T(8,128)}, f32[256,512]{1,0:T(8,128)}) custom-call(f32[1280,128]{1,0:T(8,128)} %bitcast.33, bf16[512,512]{1,0:T(8,128)(2,1)} %constant.37.clone.ch.refs_1_, bf16[512,512]{1,0:T(8,128)(2,1)} %constant.38.clone.cl.refs_2_, bf16[128,128]{1,0:T(8,128)(2,1)} %constant.39.clone.refs_3_, bf16[128,128]{1,0:T(8,128)(2,1)} %constant.40.clone.refs_4_, ...), custom_call_target="tpu_custom_call" | custom-call | flops 1207959552 | bytes 3145728 | tf_op jit(solution)/shard_map/solve/pallas_call | solution.py:347
  137.0 32.7 %all_to_all.32 = f32[256,1,768]{2,1,0:T(1,128)} all-to-all(f32[256,1,768]{2,1,0:T(1,128)} %bitcast.26), channel_id=1, replica_groups=mesh['tm'=32,'space'=8] {'tm','space'}, dimensions={0} | all-to-all | bytes 1572864 | tf_op jit(solution)/shard_map/all_to_all | solution.py:329
  169.7 8.5 %middle.3 = (f32[4,64,512]{2,1,0:T(8,128)}, f32[4,64,512]{2,1,0:T(8,128)}, f32[4,64,512]{2,1,0:T(8,128)}, f32[1280,128]{1,0:T(8,128)}, f32[3,4,512]{2,1,0:T(4,128)}) custom-call(s32[1]{0:T(128)} %bitcast.place, f32[1536,128]{1,0:T(8,128)} %bitcast.23, f32[4,64,512]{2,1,0:T(8,128)} %get-tuple-element.32.d, f32[4,64,512]{2,1,0:T(8,128)} %get-tuple-element.33.fx, ...), custom_call_target="tpu_custom_call" | custom-call | flops 805306368 | bytes 5242880 | tf_op jit(solution)/shard_map/middle/pallas_call | solution.py:357
  178.2 29.8 %all_to_all.33 = f32[256,1,640]{2,1,0:T(1,128)} all-to-all(f32[256,1,640]{2,1,0:T(1,128)} %bitcast.30), channel_id=1, replica_groups=mesh['tm'=32,'space'=8] {'tm','space'}, dimensions={0} | all-to-all | bytes 1310720 | tf_op jit(solution)/shard_map/all_to_all | solution.py:329
  208.0 4.7 %solve.5 = (f32[1024,128]{1,0:T(8,128)}, f32[256,512]{1,0:T(8,128)}) custom-call(f32[1280,128]{1,0:T(8,128)} %bitcast.32, bf16[512,512]{1,0:T(8,128)(2,1)} %constant.37.clone.ch.refs_1_, bf16[512,512]{1,0:T(8,128)(2,1)} %constant.38.clone.cl.refs_2_, bf16[128,128]{1,0:T(8,128)(2,1)} %constant.39.clone.refs_3_, bf16[128,128]{1,0:T(8,128)(2,1)} %constant.40.clone.refs_4_, ...), custom_call_target="tpu_custom_call" | custom-call | flops 1207959552 | bytes 3145728 | tf_op jit(solution)/shard_map/solve/pallas_call | solution.py:347
  212.7 27.6 %all_to_all.34 = f32[256,1,512]{2,1,0:T(1,128)} all-to-all(f32[256,1,512]{2,1,0:T(1,128)} %bitcast.34), channel_id=1, replica_groups=mesh['tm'=32,'space'=8] {'tm','space'}, dimensions={0} | all-to-all | bytes 1048576 | tf_op jit(solution)/shard_map/all_to_all | solution.py:329
  240.3 2.8 %last.1 = f32[4,64,512]{2,1,0:T(8,128)} custom-call(f32[1024,128]{1,0:T(8,128)} %bitcast.25, bf16[512,512]{1,0:T(8,128)(2,1)} %constant.37.clone.ch.refs_1_, bf16[512,512]{1,0:T(8,128)(2,1)} %constant.38.clone.cl.refs_2_), custom_call_target="tpu_custom_call" | custom-call | flops 402653184 | bytes 1572864 | tf_op jit(solution)/shard_map/last/pallas_call | solution.py:362
  (4 shorter events, 0.0 us)
Async XLA Ops:
  3.2 10.1 %collective-permute-start = (f32[3,4,512]{2,1,0:T(4,128)S(1)}, f32[3,4,512]{2,1,0:T(4,128)S(1)}, u32[]{:S(2)}, u32[]{:S(2)}) collective-permute-start(f32[3,4,512]{2,1,0:T(4,128)S(1)} %pad_maximum_fusion), channel_id=1, source_target_pairs={{0,1},{1,2},{2,3},{3,4},{4,5},{5,6},{6,7},{8,9},{9,10},{10,11},{11... | collective-permute-start | bytes 73736 | tf_op jit(solution)/shard_map/ppermute | solution.py:333
  13.3 0.6 copy-start.1
  18.4 36.6 %all-to-all-start = ((f32[256,1,640]{2,1,0:T(1,128)}), f32[256,1,640]{2,1,0:T(1,128)S(1)}, u32[]{:S(2)}, u32[]{:S(2)}) async-start(f32[256,1,640]{2,1,0:T(1,128)} %bitcast.29), calls=%async_computation | async-start | bytes 1310720 | tf_op jit(solution)/shard_map/all_to_all | solution.py:329
  32.4 0.8 copy-start.3
  33.2 0.7 copy-start.2
  55.0 0.8 copy-start

commit v3 on v2

--- a/solution.py
+++ b/solution.py
@@ -13,6 +13,7 @@
 TAU_STEP = 1.0
 SLOW_LOOP = 2.25
 INTERPRET = False
+GRANT = 20 << 20
 BOTH = ("tm", "space")
 f32 = jnp.float32
 bf16 = jnp.bfloat16
@@ -69,12 +70,13 @@
     smem = pl.BlockSpec(memory_space=pltpu.SMEM)
     return pl.pallas_call(
         body,
-        out_shape=[jax.ShapeDtypeStruct(s, f32) for s in outs],
+        out_shape=[pltpu.VMEM(s, f32) for s in outs],
         in_specs=[smem] * scalars + [vmem] * n_in,
         out_specs=[vmem] * len(outs),
         scratch_shapes=list(scratch),
         cost_estimate=pl.CostEstimate(flops=int(cost[0]), bytes_accessed=int(cost[1]), transcendentals=0),
         interpret=INTERPRET,
+        compiler_params=pltpu.CompilerParams(vmem_limit_bytes=GRANT),
         **kw,
     )
 
@@ -186,6 +188,28 @@
     out[pl.ds(2 * pairs, count, stride=group), :] = jnp.where(low_half, modes[:count, span], modes[count:, span])
 
 
+def edge_body(d, fx, fy, edge):
+    rows = d.shape[1]
+    for k, ref in enumerate((d, fx, fy)):
+        for t in range(d.shape[0]):
+            edge[k, t : t + 1, :] = ref[t, rows - 1 :, :]
+
+
+def last_rows(density, flux_x, flux_y):
+    steps, rows, width = density.shape
+    block = pl.BlockSpec((steps, 8, width), lambda i: (0, rows // 8 - 1, 0))
+    return pl.pallas_call(
+        edge_body,
+        grid=(1,),
+        out_shape=jax.ShapeDtypeStruct((3, steps, width), f32),
+        in_specs=[block] * 3,
+        out_specs=pl.BlockSpec((3, steps, width), lambda i: (0, 0, 0)),
+        compiler_params=pltpu.CompilerParams(vmem_limit_bytes=GRANT),
+        interpret=INTERPRET,
+        name="edges",
+    )(density, flux_x, flux_y)
+
+
 def prox_body(d, fx, fy, nd, nx, ny):
     prox_cells((d, fx, fy), (nd, nx, ny))
 
@@ -329,8 +353,7 @@
         value = lax.all_to_all(value, BOTH, split_axis=0, concat_axis=0, tiled=True)
         return value.reshape(shape)
 
-    edge = jnp.stack([density[:, rows - 1], flux_x[:, rows - 1], flux_y[:, rows - 1]])
-    edge = lax.ppermute(edge, "space", [(i, i + 1) for i in range(places - 1)])
+    edge = lax.ppermute(last_rows(density, flux_x, flux_y), "space", [(i, i + 1) for i in range(places - 1)])
     split = [pltpu.VMEM(((steps + 2) * rows, width), bf16)] * 2
     new_d, new_x, new_y = call(
         prox_body, [field] * 3, n_in=3, cost=(density.size * 200, 6 * nbytes), name="prox"

time: 244 us -> 219 us (0.90)
  blocking collectives: 152 us -> 121 us
  Pallas kernels: 44.9 us -> 23.5 us
  waiting for transfers between devices: 20.2 us -> 39.2 us
  starting transfers between devices: 18.6 us -> 25 us
  local copies, waits for them, and re-layouts: 5.4 us -> 9.4 us
    all_to_all x5 -> x4, blocking collectives: 152 us -> 121 us  [exchange(): value = lax.all_to_all(value, BOTH, split_axis=0, concat_axis=0, tiled=True)]
    all_to_all x1 -> x2, waiting for transfers between devices: 20.2 us -> 39.1 us  [exchange(): value = lax.all_to_all(value, BOTH, split_axis=0, concat_axis=0, tiled=True)]
    pallas_call x3, Pallas kernels: 15.1 us -> 7.41 us  [local(): call(functools.partial(solve_body, slabs, places, steps, bool(total), not...]
    unnamed x9 -> x54, local copies, waits for them, and re-layouts: 2.08 us -> 8.64 us
    all_to_all x1 -> x2, starting transfers between devices: 14 us -> 20.3 us  [exchange(): value = lax.all_to_all(value, BOTH, split_axis=0, concat_axis=0, tiled=True)]
    pallas_call x2, Pallas kernels: 17 us -> 11.1 us  [local(): call(functools.partial(middle_body, places - 1), [field] * 3 + [packed(fo...]
    pallas_call x1, Pallas kernels: 4.5 us -> 1.36 us  [local(): call(functools.partial(forward_body, places - 1), [packed(forward_items),...]
    slice x3 -> x0, local copies, waits for them, and re-layouts: 2.55 us -> none  [the longest x1 0.85 us: local(): density[:, rows - 1]]
  transfers between devices with their start and end apart: 2 -> 3, of which waited for: 1 -> 2; matrix products, arithmetic and copies ran while one was open for 1% -> 2% of each run, Pallas kernels for 2% -> 1%
where the time goes in v3:
time: 219 us
  blocking collectives  121 us (55%)
  waiting for transfers between devices  39.2 us (18%)
  starting transfers between devices  25 us (11%)
  Pallas kernels  23.5 us (11%)
  local copies, waits for them, and re-layouts  9.4 us (4%)
    all_to_all x4, blocking collectives, exchange(): value = lax.all_to_all(value, BOTH, split_axis=0, concat_axis=0, tiled=True)  121 us
    all_to_all x2, waiting for transfers between devices, exchange(): value = lax.all_to_all(value, BOTH, split_axis=0, concat_axis=0, tiled=True)  39.1 us
    all_to_all x2, starting transfers between devices, exchange(): value = lax.all_to_all(value, BOTH, split_axis=0, concat_axis=0, tiled=True)  20.3 us
    pallas_call x2, Pallas kernels, local(): call(functools.partial(middle_body, places - 1), [field] * 3 + [packed(fo...  11.1 us
    unnamed x54, local copies, waits for them, and re-layouts  8.64 us
    pallas_call x3, Pallas kernels, local(): call(functools.partial(solve_body, slabs, places, steps, bool(total), not...  7.41 us
    ppermute x1, starting transfers between devices, local(): lax.ppermute(last_rows(density, flux_x, flux_y), 'space', [(i, i + 1) for...  4.71 us
  transfers between devices with their start and end apart: 3, of which 2 were waited for; matrix products, arithmetic and copies ran while one was open for 2% of the time, Pallas kernels for 1%

profile of v3, /device:TPU:1, one launch (start us, length us, event | category | flops | bytes accessed | tf_op | source)
XLA Modules:
  0.0 218.9 jit_solution(14134524002023057798)
XLA Ops:
  0.6 0.0 copy-start.2
  0.6 1.0 copy-done.2
  1.7 1.0 copy-done.4
  2.7 1.0 copy-done.6
  3.8 4.7 %collective-permute-start = (f32[3,4,512]{2,1,0:T(4,128)S(1)}, f32[3,4,512]{2,1,0:T(4,128)S(1)}, u32[]{:S(2)}, u32[]{:S(2)}) collective-permute-start(f32[3,4,512]{2,1,0:T(4,128)S(1)} %edges.1), channel_id=1, source_target_pairs={{0,1},{1,2},{2,3},{3,4},{4,5},{5,6},{6,7},{8,9},{9,10},{10,11},{11... | collective-permute-start | bytes 73736 | tf_op jit(solution)/shard_map/ppermute | solution.py:356
  8.5 0.0 copy-done.3
  8.5 0.0 copy-done.5
  8.5 0.0 copy-done.7
  8.5 0.0 copy-start
  8.6 0.0 copy-start.1
  8.6 0.0 copy-start.8
  8.6 3.0 %prox.1 = (f32[4,64,512]{2,1,0:T(8,128)S(1)}, f32[4,64,512]{2,1,0:T(8,128)S(1)}, f32[4,64,512]{2,1,0:T(8,128)S(1)}) custom-call(f32[4,64,512]{2,1,0:T(8,128)S(1)} %copy-done.3, f32[4,64,512]{2,1,0:T(8,128)S(1)} %copy-done.5, f32[4,64,512]{2,1,0:T(8,128)S(1)} %copy-done.7), custom_call_target="tpu_custom_call" | custom-call | flops 26214400 | bytes 3145728 | tf_op jit(solution)/shard_map/prox/pallas_call | solution.py:358
  11.6 0.0 copy-start.9
  11.6 0.0 copy-start.11
  11.6 0.0 copy-start.13
  11.6 0.0 collective-permute-done.edge
  11.6 0.0 copy-done
  11.6 0.0 copy-done.1
  11.6 0.0 copy-done.8
  11.6 1.4 forward.1
  13.0 0.0 copy-done.9
  13.0 0.0 copy-done.11
  13.0 0.0 copy-done.13
  13.0 0.0 copy-start.15
  13.0 0.8 copy-done.15
  13.9 14.0 %all-to-all-start = ((f32[256,1,640]{2,1,0:T(1,128)}), f32[256,1,640]{2,1,0:T(1,128)S(1)}, u32[]{:S(2)}, u32[]{:S(2)}) async-start(f32[256,1,640]{2,1,0:T(1,128)} %bitcast.22), calls=%async_computation | async-start | bytes 1310720 | tf_op jit(solution)/shard_map/all_to_all | solution.py:353
  27.9 0.0 copy-start.24
  27.9 0.8 dynamic_slice.3
  28.6 0.0 copy-done.24
  28.7 0.1 bitcast_add_fusion
  28.7 0.6 copy-done.23
  29.3 0.1 add_add_fusion.refs_7_
  29.5 0.0 copy-start.16
  29.5 21.0 %all-to-all-done = f32[256,1,640]{2,1,0:T(1,128)S(1)} async-done(((f32[256,1,640]{2,1,0:T(1,128)}), f32[256,1,640]{2,1,0:T(1,128)S(1)}, u32[]{:S(2)}, u32[]{:S(2)}) %all-to-all-start) | async-done | bytes 655392 | tf_op jit(solution)/shard_map/all_to_all | solution.py:353
  50.5 0.0 copy-done.19
  50.5 0.0 copy-done.20
  50.5 0.0 copy-done.21
  50.5 0.0 copy-done.22
  50.5 2.7 %solve.3 = (f32[1536,128]{1,0:T(8,128)S(1)}, f32[256,512]{1,0:T(8,128)S(1)}) custom-call(f32[1280,128]{1,0:T(8,128)S(1)} %bitcast.21, bf16[512,512]{1,0:T(8,128)(2,1)S(1)} %copy-done.1, bf16[512,512]{1,0:T(8,128)(2,1)S(1)} %copy-done, bf16[128,128]{1,0:T(8,128)(2,1)S(1)} %copy-done.22, bf16[128,128]{1,0:T(8,128)(2,1)S(1)} %copy-done.21, ...), custom_call_target="tpu_custom_call" | custom-call | flops 1207959552 | bytes 3145728 | tf_op jit(solution)/shard_map/solve/pallas_call | solution.py:370
  53.2 0.0 copy-start.10
  53.2 0.0 copy-start.12
  53.2 0.0 copy-start.14
  53.2 31.6 %all_to_all.30 = f32[256,1,768]{2,1,0:T(1,128)S(1)} all-to-all(f32[256,1,768]{2,1,0:T(1,128)S(1)} %bitcast.20), channel_id=1, replica_groups=mesh['tm'=32,'space'=8] {'tm','space'}, dimensions={0} | all-to-all | bytes 1572864 | tf_op jit(solution)/shard_map/all_to_all | solution.py:353
  84.8 0.0 copy-done.10
  84.8 0.0 copy-done.12
  84.8 0.0 copy-done.14
  84.8 5.6 %middle.2 = (f32[4,64,512]{2,1,0:T(8,128)S(1)}, f32[4,64,512]{2,1,0:T(8,128)S(1)}, f32[4,64,512]{2,1,0:T(8,128)S(1)}, f32[1280,128]{1,0:T(8,128)S(1)}, f32[3,4,512]{2,1,0:T(4,128)S(1)}) custom-call(s32[1]{0:T(128)} %bitcast.place, f32[1536,128]{1,0:T(8,128)S(1)} %bitcast.17, f32[4,64,512]{2,1,0:T(8,128)S(1)} %copy-done.10, f32[4,64,512]{2,1,0:T(8,128)S(1)} %copy-done.12, ...), custom_call_target="tpu_custom_call" | custom-call | flops 805306368 | bytes 5242880 | tf_op jit(solution)/shard_map/middle/pallas_call | solution.py:380
  90.4 28.7 %all_to_all.31 = f32[256,1,640]{2,1,0:T(1,128)S(1)} all-to-all(f32[256,1,640]{2,1,0:T(1,128)S(1)} %bitcast.24), channel_id=1, replica_groups=mesh['tm'=32,'space'=8] {'tm','space'}, dimensions={0} | all-to-all | bytes 1310720 | tf_op jit(solution)/shard_map/all_to_all | solution.py:353
  119.1 0.0 copy-done.16
  119.1 2.7 %solve.4 = (f32[1536,128]{1,0:T(8,128)S(1)}, f32[256,512]{1,0:T(8,128)S(1)}) custom-call(f32[1280,128]{1,0:T(8,128)S(1)} %bitcast.26, bf16[512,512]{1,0:T(8,128)(2,1)S(1)} %copy-done.1, bf16[512,512]{1,0:T(8,128)(2,1)S(1)} %copy-done, bf16[128,128]{1,0:T(8,128)(2,1)S(1)} %copy-done.22, bf16[128,128]{1,0:T(8,128)(2,1)S(1)} %copy-done.21, ...), custom_call_target="tpu_custom_call" | custom-call | flops 1207959552 | bytes 3145728 | tf_op jit(solution)/shard_map/solve/pallas_call | solution.py:370
  121.8 31.7 %all_to_all.32 = f32[256,1,768]{2,1,0:T(1,128)S(1)} all-to-all(f32[256,1,768]{2,1,0:T(1,128)S(1)} %bitcast.19), channel_id=1, replica_groups=mesh['tm'=32,'space'=8] {'tm','space'}, dimensions={0} | all-to-all | bytes 1572864 | tf_op jit(solution)/shard_map/all_to_all | solution.py:353
  153.4 5.5 %middle.3 = (f32[4,64,512]{2,1,0:T(8,128)S(1)}, f32[4,64,512]{2,1,0:T(8,128)S(1)}, f32[4,64,512]{2,1,0:T(8,128)S(1)}, f32[1280,128]{1,0:T(8,128)S(1)}, f32[3,4,512]{2,1,0:T(4,128)}) custom-call(s32[1]{0:T(128)} %bitcast.place, f32[1536,128]{1,0:T(8,128)S(1)} %bitcast.16, f32[4,64,512]{2,1,0:T(8,128)S(1)} %get-tuple-element.32.d, ...), custom_call_target="tpu_custom_call" | custom-call | flops 805306368 | bytes 5242880 | tf_op jit(solution)/shard_map/middle/pallas_call | solution.py:380
  159.0 0.0 copy-start.17
  159.0 28.7 %all_to_all.33 = f32[256,1,640]{2,1,0:T(1,128)S(1)} all-to-all(f32[256,1,640]{2,1,0:T(1,128)S(1)} %bitcast.23), channel_id=1, replica_groups=mesh['tm'=32,'space'=8] {'tm','space'}, dimensions={0} | all-to-all | bytes 1310720 | tf_op jit(solution)/shard_map/all_to_all | solution.py:353
  187.7 2.1 solve.5
  189.8 0.0 copy-start.18
  189.8 0.8 copy-done.18
  190.6 6.4 %all-to-all-start.5 = ((f32[256,1,512]{2,1,0:T(1,128)}), f32[256,1,512]{2,1,0:T(1,128)S(1)}, u32[]{:S(2)}, u32[]{:S(2)}) async-start(f32[256,1,512]{2,1,0:T(1,128)} %bitcast.27), calls=%async_computation.5 | async-start | bytes 1048576 | tf_op jit(solution)/shard_map/all_to_all | solution.py:353
  196.9 0.8 copy.23
  197.7 0.8 copy.24
  198.5 0.8 copy.25
  199.3 18.2 %all-to-all-done.5 = f32[256,1,512]{2,1,0:T(1,128)S(1)} async-done(((f32[256,1,512]{2,1,0:T(1,128)}), f32[256,1,512]{2,1,0:T(1,128)S(1)}, u32[]{:S(2)}, u32[]{:S(2)}) %all-to-all-start.5) | async-done | bytes 524320 | tf_op jit(solution)/shard_map/all_to_all | solution.py:353
  217.5 0.6 last.1
  218.1 0.8 copy.26
  (13 shorter events, 0.0 us)
Async XLA Ops:
  0.6 1.0 copy-start.2
  1.7 1.0 copy-start.4
  2.7 1.0 copy-start.6
  3.8 4.8 %copy-start.3 = (f32[4,64,512]{2,1,0:T(8,128)S(1)}, f32[4,64,512]{2,1,0:T(8,128)}, u32[]{:S(2)}) copy-start(f32[4,64,512]{2,1,0:T(8,128)} %d.5) | copy-start | bytes 1572868
  3.8 4.8 %copy-start.5 = (f32[4,64,512]{2,1,0:T(8,128)S(1)}, f32[4,64,512]{2,1,0:T(8,128)}, u32[]{:S(2)}) copy-start(f32[4,64,512]{2,1,0:T(8,128)} %fx.5) | copy-start | bytes 1572868
  3.8 4.8 %copy-start.7 = (f32[4,64,512]{2,1,0:T(8,128)S(1)}, f32[4,64,512]{2,1,0:T(8,128)}, u32[]{:S(2)}) copy-start(f32[4,64,512]{2,1,0:T(8,128)} %fy.5) | copy-start | bytes 1572868
  3.8 7.8 %collective-permute-start = (f32[3,4,512]{2,1,0:T(4,128)S(1)}, f32[3,4,512]{2,1,0:T(4,128)S(1)}, u32[]{:S(2)}, u32[]{:S(2)}) collective-permute-start(f32[3,4,512]{2,1,0:T(4,128)S(1)} %edges.1), channel_id=1, source_target_pairs={{0,1},{1,2},{2,3},{3,4},{4,5},{5,6},{6,7},{8,9},{9,10},{10,11},{11... | collective-permute-start | bytes 73736 | tf_op jit(solution)/shard_map/ppermute | solution.py:356
  8.5 3.1 %copy-start = (bf16[512,512]{1,0:T(8,128)(2,1)S(1)}, bf16[512,512]{1,0:T(8,128)(2,1)}, u32[]{:S(2)}) copy-start(bf16[512,512]{1,0:T(8,128)(2,1)} %constant.38.clone.cl.refs_2_) | copy-start | bytes 1572868
  8.6 3.1 %copy-start.1 = (bf16[512,512]{1,0:T(8,128)(2,1)S(1)}, bf16[512,512]{1,0:T(8,128)(2,1)}, u32[]{:S(2)}) copy-start(bf16[512,512]{1,0:T(8,128)(2,1)} %constant.37.clone.ch.refs_1_) | copy-start | bytes 1572868
  8.6 3.1 %copy-start.8 = (f32[4,64,512]{2,1,0:T(8,128)S(1)}, f32[4,64,512]{2,1,0:T(8,128)}, u32[]{:S(2)}) copy-start(f32[4,64,512]{2,1,0:T(8,128)} %src.5) | copy-start | bytes 1572868
  11.6 1.4 copy-start.9
  11.6 1.4 copy-start.11
  11.6 1.4 copy-start.13
  13.0 0.9 copy-start.15
  13.9 36.6 %all-to-all-start = ((f32[256,1,640]{2,1,0:T(1,128)}), f32[256,1,640]{2,1,0:T(1,128)S(1)}, u32[]{:S(2)}, u32[]{:S(2)}) async-start(f32[256,1,640]{2,1,0:T(1,128)} %bitcast.22), calls=%async_computation | async-start | bytes 1310720 | tf_op jit(solution)/shard_map/all_to_all | solution.py:353
  27.9 0.8 copy-start.24
  28.7 0.7 copy-start.23
  29.3 21.1 %copy-start.19 = (bf16[128,128]{1,0:T(8,128)(2,1)S(1)}, bf16[128,128]{1,0:T(8,128)(2,1)}, u32[]{:S(2)}) copy-start(bf16[128,128]{1,0:T(8,128)(2,1)} %constant.42.clone.refs_6_) | copy-start | bytes 98308
  29.3 21.1 %copy-start.20 = (bf16[128,128]{1,0:T(8,128)(2,1)S(1)}, bf16[128,128]{1,0:T(8,128)(2,1)}, u32[]{:S(2)}) copy-start(bf16[128,128]{1,0:T(8,128)(2,1)} %constant.41.clone.refs_5_) | copy-start | bytes 98308
  29.3 21.1 %copy-start.21 = (bf16[128,128]{1,0:T(8,128)(2,1)S(1)}, bf16[128,128]{1,0:T(8,128)(2,1)}, u32[]{:S(2)}) copy-start(bf16[128,128]{1,0:T(8,128)(2,1)} %constant.40.clone.refs_4_) | copy-start | bytes 98308
  29.3 21.1 %copy-start.22 = (bf16[128,128]{1,0:T(8,128)(2,1)S(1)}, bf16[128,128]{1,0:T(8,128)(2,1)}, u32[]{:S(2)}) copy-start(bf16[128,128]{1,0:T(8,128)(2,1)} %constant.39.clone.refs_3_) | copy-start | bytes 98308
  29.5 89.6 %copy-start.16 = (f32[256,512]{1,0:T(8,128)}, f32[256,512]{1,0:T(8,128)S(1)}, u32[]{:S(2)}) copy-start(f32[256,512]{1,0:T(8,128)S(1)} %add_add_fusion.refs_7_) | copy-start | bytes 1572868
  53.2 31.7 %copy-start.10 = (f32[4,64,512]{2,1,0:T(8,128)S(1)}, f32[4,64,512]{2,1,0:T(8,128)}, u32[]{:S(2)}) copy-start(f32[4,64,512]{2,1,0:T(8,128)} %copy-done.9) | copy-start | bytes 1572868
  53.2 31.7 %copy-start.12 = (f32[4,64,512]{2,1,0:T(8,128)S(1)}, f32[4,64,512]{2,1,0:T(8,128)}, u32[]{:S(2)}) copy-start(f32[4,64,512]{2,1,0:T(8,128)} %copy-done.11) | copy-start | bytes 1572868
  53.2 31.6 %copy-start.14 = (f32[4,64,512]{2,1,0:T(8,128)S(1)}, f32[4,64,512]{2,1,0:T(8,128)}, u32[]{:S(2)}) copy-start(f32[4,64,512]{2,1,0:T(8,128)} %copy-done.13) | copy-start | bytes 1572868
  159.0 28.7 %copy-start.17 = (f32[256,512]{1,0:T(8,128)S(1)}, f32[256,512]{1,0:T(8,128)}, u32[]{:S(2)}) copy-start(f32[256,512]{1,0:T(8,128)} %copy-done.16) | copy-start | bytes 1572868
  189.8 0.8 copy-start.18
  190.6 26.9 %all-to-all-start.5 = ((f32[256,1,512]{2,1,0:T(1,128)}), f32[256,1,512]{2,1,0:T(1,128)S(1)}, u32[]{:S(2)}, u32[]{:S(2)}) async-start(f32[256,1,512]{2,1,0:T(1,128)} %bitcast.27), calls=%async_computation.5 | async-start | bytes 1048576 | tf_op jit(solution)/shard_map/all_to_all | solution.py:353

commit v4 on v3

--- a/solution.py
+++ b/solution.py
@@ -14,6 +14,9 @@
 SLOW_LOOP = 2.25
 INTERPRET = False
 GRANT = 20 << 20
+KEPT = 8
+TAKEN = 9
+BLOCK = 16
 BOTH = ("tm", "space")
 f32 = jnp.float32
 bf16 = jnp.bfloat16
@@ -65,18 +68,19 @@
     return high, (matrix - high.astype(np.float32)).astype(bf16)
 
 
-def call(body, outs, scratch=(), scalars=0, n_in=0, cost=None, **kw):
+def call(body, outs, scratch=(), scalars=0, far=0, n_in=0, far_out=False, cost=None, **kw):
     vmem = pl.BlockSpec(memory_space=pltpu.VMEM)
     smem = pl.BlockSpec(memory_space=pltpu.SMEM)
+    hbm = pl.BlockSpec(memory_space=pltpu.HBM)
     return pl.pallas_call(
         body,
-        out_shape=[pltpu.VMEM(s, f32) for s in outs],
-        in_specs=[smem] * scalars + [vmem] * n_in,
-        out_specs=[vmem] * len(outs),
+        out_shape=[jax.ShapeDtypeStruct(s, f32) if far_out else pltpu.VMEM(s, f32) for s in outs],
+        in_specs=[smem] * scalars + [hbm] * far + [vmem] * n_in,
+        out_specs=[hbm if far_out else vmem] * len(outs),
         scratch_shapes=list(scratch),
         cost_estimate=pl.CostEstimate(flops=int(cost[0]), bytes_accessed=int(cost[1]), transcendentals=0),
+        compiler_params=pltpu.CompilerParams(vmem_limit_bytes=GRANT),
         interpret=INTERPRET,
-        compiler_params=pltpu.CompilerParams(vmem_limit_bytes=GRANT),
         **kw,
     )
 
@@ -97,13 +101,15 @@
     return root, factor * along_x, factor * along_y
 
 
-def prox_cells(source, result):
+def prox_cells(source, result, wait=None):
     steps, rows, width = result[0].shape
-    chunk = 16
+    chunk = 32
     per = rows // chunk
 
     def step(index, carry):
         t = index // per
+        if wait is not None:
+            pl.when(index % per == 0)(lambda: wait(t))
         span = pl.ds(pl.multiple_of((index % per) * chunk, chunk), chunk)
         out = newton(*[ref[t, span, :] for ref in source])
         for ref, value in zip(result, out):
@@ -113,20 +119,40 @@
     lax.fori_loop(0, steps * per, step, 0)
 
 
-def transform_back(y, ch, cl, u, pairs, group):
-    cosine = (ch[...], cl[...])
+def transform_back(y, ch, cl, u, pair, group, packed_edge=False):
     count = y.shape[0] // group
     lanes = y.shape[1]
-    for pair in range(pairs):
+    if packed_edge:
+        both = y[pl.ds(pair * 2, count, stride=group), :]
+        even, odd = both, pltpu.roll(both, lanes // 2, 1)
+        kept = lanes // 2
+    else:
         even = y[pl.ds(pair, count, stride=group), :]
         odd = y[pl.ds(group // 2 + pair, count, stride=group), :]
-        u[pair * lanes : (pair + 1) * lanes, :] = dot3(halves(jnp.concatenate([even, odd], axis=0)), cosine, TN)
+        kept = lanes
+    value = dot3(halves(jnp.concatenate([even, odd], axis=0)), (ch[...], cl[...]), TN)
+    u[pair * lanes : pair * lanes + kept, :] = value[:kept, :]
+
+
+def fill_plane(u, steps, rows, screen, residual_sum):
+    at = (steps - 1) * rows + KEPT
+    here = u[at : at + BLOCK, :]
+    width = here.shape[1]
+    column = lax.broadcasted_iota(jnp.int32, here.shape, 1)
+    right = jnp.where(column == width - 1, here, pltpu.roll(here, width - 1, 1))
+    left = jnp.where(column == 0, here, pltpu.roll(here, 1, 1))
+    earlier = u[at - rows : at - rows + BLOCK, :]
+    value = (here - earlier) + (here - u[at - 1 : at - 1 + BLOCK, :]) + (here - u[at + 1 : at + 1 + BLOCK, :])
+    value = here + (value + (here - right) + (here - left) + screen * here - residual_sum)
+    at = steps * rows + KEPT
+    row = lax.broadcasted_iota(jnp.int32, here.shape, 0)
+    u[at : at + BLOCK, :] = jnp.where(row < TAKEN, value, u[at : at + BLOCK, :])
 
 
 def dual_step(d, fx, fy, edge, u, nd, nx, ny):
     steps, rows, width = d.shape
     below_at = (steps + 1) * rows
-    above_at = below_at + 8
+    above_at = below_at + steps
     end_row = lax.broadcasted_iota(jnp.int32, (rows, width), 0) == rows - 1
     end_column = lax.broadcasted_iota(jnp.int32, (rows, width), 1) == width - 1
     for t in range(steps):
@@ -148,7 +174,7 @@
     )
 
 
-def residual_modes(place, last_place, d, fx, fy, nd, nx, ny, src, edge_x, new_edge_x, ch, cl, out, rh, rl):
+def residual_modes(place, last_place, d, fx, fy, nd, nx, ny, src, edge_x, new_edge_x, ch, cl, out, kept, rh, rl):
     steps, rows, width = d.shape
     shape = (rows, width)
     row = lax.broadcasted_iota(jnp.int32, shape, 0)
@@ -170,6 +196,7 @@
         high, low = halves(value)
         rh[t * rows : (t + 1) * rows, :] = high
         rl[t * rows : (t + 1) * rows, :] = low
+    kept[...] = value[KEPT : KEPT + BLOCK, :]
     high, low = halves(before)
     for t in (steps, steps + 1):
         rh[t * rows : (t + 1) * rows, :] = high
@@ -195,6 +222,10 @@
             edge[k, t : t + 1, :] = ref[t, rows - 1 :, :]
 
 
+def stay(value):
+    return value if INTERPRET else pltpu.with_memory_space_constraint(value, pltpu.HBM)
+
+
 def last_rows(density, flux_x, flux_y):
     steps, rows, width = density.shape
     block = pl.BlockSpec((steps, 8, width), lambda i: (0, rows // 8 - 1, 0))
@@ -207,43 +238,68 @@
         compiler_params=pltpu.CompilerParams(vmem_limit_bytes=GRANT),
         interpret=INTERPRET,
         name="edges",
-    )(density, flux_x, flux_y)
-
-
-def prox_body(d, fx, fy, nd, nx, ny):
-    prox_cells((d, fx, fy), (nd, nx, ny))
-
-
-def forward_body(last_place, place, d, fx, fy, nd, nx, ny, src, edge, ch, cl, out, new_edge, rh, rl):
+    )(*map(stay, (density, flux_x, flux_y)))
+
+
+def prox_body(d, fx, fy, nd, nx, ny, own_d, own_x, own_y, sems):
+    steps = d.shape[0]
+    moves = ((d, own_d), (fx, own_x), (fy, own_y))
+
+    def copy(k, t):
+        return pltpu.make_async_copy(moves[k][0].at[t], moves[k][1].at[t], sems.at[k, t])
+
+    for t in range(steps):
+        for k in range(3):
+            copy(k, t).start()
+
+    def wait(t):
+        for k in range(3):
+            copy(k, t).wait()
+
+    prox_cells((own_d, own_x, own_y), (nd, nx, ny), wait)
+
+
+def forward_body(last_place, place, d, fx, fy, nd, nx, ny, src, edge, ch, cl, out, new_edge, kept, rh, rl):
     fresh = newton(edge[0], edge[1], edge[2])
     for k in range(3):
         new_edge[k] = fresh[k]
-    residual_modes(place[0], last_place, d, fx, fy, nd, nx, ny, src, edge[1], fresh[1], ch, cl, out, rh, rl)
-
-
-def middle_body(last_place, place, y, d, fx, fy, src, edge, ch, cl, nd, nx, ny, out, new_edge, u, rh, rl):
-    steps = d.shape[0]
-    pairs = steps // 2 + 1
-    transform_back(y, ch, cl, u, pairs, 2 * pairs)
+    residual_modes(place[0], last_place, d, fx, fy, nd, nx, ny, src, edge[1], fresh[1], ch, cl, out, kept, rh, rl)
+
+
+def middle_body(last_place, screen, place, y, d, fx, fy, src, edge, kept_sum, ch, cl, nd, nx, ny, out, new_edge, kept, u, rh, rl):
+    steps, rows, _ = d.shape
+    pairs = steps // 2
+    for pair in range(pairs):
+        transform_back(y, ch, cl, u, pair, 2 * pairs + 1)
+    transform_back(y, ch, cl, u, pairs, 2 * pairs + 1, True)
+    at = steps * rows
+    u[at + rows : at + rows + TAKEN, :] = u[at + KEPT : at + KEPT + TAKEN, :]
+    fill_plane(u, steps, rows, screen, kept_sum[...])
     fresh = newton(*dual_step(d, fx, fy, edge, u, nd, nx, ny))
     for k in range(3):
         new_edge[k] = fresh[k]
     prox_cells((nd, nx, ny), (nd, nx, ny))
-    residual_modes(place[0], last_place, d, fx, fy, nd, nx, ny, src, edge[1], fresh[1], ch, cl, out, rh, rl)
-
-
-def last_body(y, ch, cl, u, flat):
+    residual_modes(place[0], last_place, d, fx, fy, nd, nx, ny, src, edge[1], fresh[1], ch, cl, out, kept, rh, rl)
+    kept[...] = kept[...] + kept_sum[...]
+
+
+def last_body(y, ch, cl, u, flat, sems):
     steps, rows, _ = u.shape
-    transform_back(y, ch, cl, flat, steps // 2, steps)
-    for t in range(steps):
-        u[t] = flat[t * rows : (t + 1) * rows, :]
-
-
-def solve_body(slabs, places, steps, with_sum, with_edges, *refs):
+    copies = []
+    for pair in range(steps // 2):
+        transform_back(y, ch, cl, flat, pair, steps)
+        for t in (2 * pair, 2 * pair + 1):
+            copies.append(pltpu.make_async_copy(flat.at[pl.ds(t * rows, rows), :], u.at[t], sems.at[t]))
+            copies[-1].start()
+    for copy in copies:
+        copy.wait()
+
+
+def solve_body(slabs, places, steps, screen, with_sum, with_edges, *refs):
     if with_sum:
-        z, ch, cl, wh, wl, vh, vl, den, so_far, out, total, field = refs
+        place, values, z, ch, cl, wh, wl, vh, vl, across, around, so_far, out, total, field = refs
     else:
-        z, ch, cl, wh, wl, vh, vl, den, out, total, field = refs
+        place, values, z, ch, cl, wh, wl, vh, vl, across, around, out, total, field = refs
     length = slabs * steps
     pairs = steps // 2
     lanes = z.shape[1]
@@ -275,45 +331,48 @@
     for mode in range(2):
         span = slice(mode * length, (mode + 1) * length)
         field[span, :] = dot3((wh[...], wl[...]), halves(field[span, :]), NN)
-    solved = dot3(halves(field[...]), cosine, NT) / den[...]
-    if with_sum:
-        solved = solved + so_far[...]
-    total[...] = solved
-    field[...] = dot3(halves(solved), cosine, NN)
+    modes = dot3(halves(field[...]), cosine, NT)
+    for mode in range(2):
+        span = slice(mode * length, (mode + 1) * length)
+        solved = modes[span, :] / (around[...] + across[...] + (values[place[1] + mode] + screen))
+        if with_sum:
+            solved = solved + so_far[span, :]
+        total[span, :] = solved
+    field[...] = dot3(halves(total[...]), cosine, NN)
     for mode in range(2):
         span = slice(mode * length, (mode + 1) * length)
         field[span, :] = dot3((vh[...], vl[...]), halves(field[span, :]), NN)
-    per_mode = pairs + 1 if with_edges else pairs
-    group_out = 2 * per_mode
+    group_out = 2 * pairs + 1 if with_edges else 2 * pairs
 
     def leaving(place, item):
         return pl.ds(place * group_out + item, slabs, stride=places * group_out)
 
-    for mode in range(2):
-        top = mode * length
-        for q in range(places // 2):
-            span = slice(q * lanes, (q + 1) * lanes)
+    for q in range(places // 2):
+        span = slice(q * lanes, (q + 1) * lanes)
+        for mode in range(2):
             for pair in range(pairs):
-                at = top + 2 * pair * slabs
+                at = mode * length + 2 * pair * slabs
                 first, second = swap(field[at : at + slabs, span], field[at + slabs : at + 2 * slabs, span])
-                out[leaving(2 * q, mode * per_mode + pair), :] = first
-                out[leaving(2 * q + 1, mode * per_mode + pair), :] = second
-            if not with_edges:
-                continue
-            ahead = pltpu.roll(field[top : top + slabs, span], slabs - 1, 0)
-            for place, value in ((2 * q, ahead), (2 * q + 1, pltpu.roll(ahead, rows, 1))):
-                after = (place + 1) * rows if place + 1 < places else (place + 1) * rows - 1
+                out[leaving(2 * q, mode * pairs + pair), :] = first
+                out[leaving(2 * q + 1, mode * pairs + pair), :] = second
+        if not with_edges:
+            continue
+        planes = swap(*[pltpu.roll(field[m * length : m * length + slabs, span], slabs - 1, 0) for m in range(2)])
+        for spot, value in zip((2 * q, 2 * q + 1), planes):
+            after = (spot + 1) * rows if spot + 1 < places else (spot + 1) * rows - 1
+            before = max(spot * rows - 1, 0)
+            for mode in range(2):
+                top = mode * length
+                at = mode * rows + KEPT
                 for t in range(steps):
                     column = field[top + t * slabs : top + (t + 1) * slabs, after : after + 1]
-                    value = jnp.where(lane == rows + t, column, value)
-                if place:
-                    before = place * rows - 1
-                    for t in range(steps + 1):
-                        column = field[top + (t % steps) * slabs : top + (t % steps + 1) * slabs, before : before + 1]
-                        if t == steps:
-                            column = pltpu.roll(jnp.broadcast_to(column, (slabs, lanes)), slabs - 1, 0)
-                        value = jnp.where(lane == rows + 8 + t, column, value)
-                out[leaving(place, mode * per_mode + pairs), :] = value
+                    value = jnp.where(lane == at + t, column, value)
+                for t in range(steps + 1):
+                    column = field[top + (t % steps) * slabs : top + (t % steps + 1) * slabs, before : before + 1]
+                    if t == steps:
+                        column = pltpu.roll(jnp.broadcast_to(column, (slabs, lanes)), slabs - 1, 0)
+                    value = jnp.where(lane == at + steps + t, column, value)
+            out[leaving(spot, 2 * pairs), :] = value
 
 
 def local(density, flux_x, flux_y, source):
@@ -330,10 +389,10 @@
     spectrum = neumann_spectrum(width)
     place = lax.axis_index("space")
     first = 2 * (lax.axis_index("tm") * places + place)
-    own = lax.dynamic_slice_in_dim(jnp.asarray(spectrum), first, 2)
-    den = own[:, None, None] + jnp.asarray(loop_values)[None, :, None] + jnp.asarray(spectrum[order])[None, None, :]
-    den = (den + screen).reshape(2 * length, width)
-    place = place.astype(jnp.int32).reshape(1)
+    values = jnp.asarray(spectrum)
+    across = jnp.asarray(spectrum[order][None, :])
+    around = jnp.asarray(loop_values[:, None])
+    place = jnp.stack([place, first]).astype(jnp.int32)
     nbytes = density.size * 4
     mega = density.size * width * 6
     field = (steps, rows, width)
@@ -344,8 +403,7 @@
     def packed(items):
         return (devices * items, lanes)
 
-    forward_items = steps + 1
-    backward_items = steps + 2
+    items = steps + 1
 
     def exchange(value):
         shape = value.shape
@@ -355,11 +413,13 @@
 
     edge = lax.ppermute(last_rows(density, flux_x, flux_y), "space", [(i, i + 1) for i in range(places - 1)])
     split = [pltpu.VMEM(((steps + 2) * rows, width), bf16)] * 2
-    new_d, new_x, new_y = call(
-        prox_body, [field] * 3, n_in=3, cost=(density.size * 200, 6 * nbytes), name="prox"
-    )(density, flux_x, flux_y)
-    modes, edge = call(
-        functools.partial(forward_body, places - 1), [packed(forward_items), edge_shape],
+    block = (BLOCK, width)
+    new_d, new_x, new_y, density, flux_x, flux_y = call(
+        prox_body, [field] * 6, scratch=[pltpu.SemaphoreType.DMA((3, steps))], far=3,
+        cost=(density.size * 200, 6 * nbytes), name="prox",
+    )(*map(stay, (density, flux_x, flux_y)))
+    modes, edge, kept = call(
+        functools.partial(forward_body, places - 1), [packed(items), edge_shape, block],
         scratch=split, scalars=1, n_in=10, cost=(mega, 8 * nbytes), name="forward",
     )(place, density, flux_x, flux_y, new_d, new_x, new_y, source, edge, ch, cl)
     density, flux_x, flux_y = new_d, new_x, new_y
@@ -368,22 +428,23 @@
         final = iteration + 1 == ITERS
         modes = exchange(modes)
         modes, solved = call(
-            functools.partial(solve_body, slabs, places, steps, bool(total), not final),
-            [packed(steps if final else backward_items), (2 * length, width)],
+            functools.partial(solve_body, slabs, places, steps, screen, bool(total), not final),
+            [packed(steps if final else items), (2 * length, width)],
             scratch=[pltpu.VMEM((2 * length, width), f32)],
-            n_in=8 + len(total), cost=(3 * mega, 6 * nbytes), name="solve",
-        )(modes, ch, cl, wh, wl, vh, vl, den, *total)
+            scalars=2, n_in=9 + len(total), cost=(3 * mega, 6 * nbytes), name="solve",
+        )(place, values, modes, ch, cl, wh, wl, vh, vl, across, around, *total)
         total = (solved,)
         modes = exchange(modes)
         if final:
             break
-        density, flux_x, flux_y, modes, edge = call(
-            functools.partial(middle_body, places - 1), [field] * 3 + [packed(forward_items), edge_shape],
-            scratch=[pltpu.VMEM(((steps + 2) * rows, width), f32)] + split,
-            scalars=1, n_in=8, cost=(2 * mega, 10 * nbytes), name="middle",
-        )(place, modes, density, flux_x, flux_y, source, edge, ch, cl)
+        density, flux_x, flux_y, modes, edge, kept = call(
+            functools.partial(middle_body, places - 1, screen), [field] * 3 + [packed(items), edge_shape, block],
+            scratch=[pltpu.VMEM(((steps + 1) * rows + BLOCK, width), f32)] + split,
+            scalars=1, n_in=9, cost=(2 * mega, 10 * nbytes), name="middle",
+        )(place, modes, density, flux_x, flux_y, source, edge, kept, ch, cl)
     (potential,) = call(
-        last_body, [field], scratch=[pltpu.VMEM((steps * rows, width), f32)], n_in=3, cost=(mega, 3 * nbytes), name="last"
+        last_body, [field], scratch=[pltpu.VMEM((steps * rows, width), f32), pltpu.SemaphoreType.DMA((steps,))],
+        n_in=3, far_out=True, cost=(mega, 3 * nbytes), name="last",
     )(modes, ch, cl)
     return density, flux_x, flux_y, potential
 

time: 219 us -> 214 us (0.977)
  blocking collectives: 121 us -> 151 us
  waiting for transfers between devices: 39.2 us -> 18.2 us
  starting transfers between devices: 25 us -> 10.9 us
  local copies, waits for them, and re-layouts: 9.4 us -> 3.23 us
  Pallas kernels: 23.5 us -> 28.9 us
    all_to_all x4 -> x5, blocking collectives: 121 us -> 151 us  [exchange(): value = lax.all_to_all(value, BOTH, split_axis=0, concat_axis=0, tiled=True)]
    all_to_all x2 -> x1, waiting for transfers between devices: 39.1 us -> 18.2 us  [exchange(): value = lax.all_to_all(value, BOTH, split_axis=0, concat_axis=0, tiled=True)]
    all_to_all x2 -> x1, starting transfers between devices: 20.3 us -> 6.36 us  [exchange(): value = lax.all_to_all(value, BOTH, split_axis=0, concat_axis=0, tiled=True)]
    unnamed x54 -> x25, local copies, waits for them, and re-layouts: 8.64 us -> 3.23 us
    pallas_call x8, Pallas kernels: 23.4 us -> 28 us  [the longest x2 11.5 us: local(): call(functools.partial(middle_body, places - 1, screen), [field] * 3 + [p...]
  transfers between devices with their start and end apart: 3 -> 2, of which waited for: 2 -> 1; matrix products, arithmetic and copies ran while one was open for 2% -> 1% of each run, Pallas kernels for 1% -> 2%
where the time goes in v4:
time: 214 us
  blocking collectives  151 us (71%)
  Pallas kernels  28.9 us (14%)
  waiting for transfers between devices  18.2 us (9%)
  starting transfers between devices  10.9 us (5%)
  local copies, waits for them, and re-layouts  3.23 us (2%)
    all_to_all x5, blocking collectives, exchange(): value = lax.all_to_all(value, BOTH, split_axis=0, concat_axis=0, tiled=True)  151 us
    all_to_all x1, waiting for transfers between devices, exchange(): value = lax.all_to_all(value, BOTH, split_axis=0, concat_axis=0, tiled=True)  18.2 us
    pallas_call x2, Pallas kernels, local(): call(functools.partial(middle_body, places - 1, screen), [field] * 3 + [p...  11.5 us
    pallas_call x3, Pallas kernels, local(): call(functools.partial(solve_body, slabs, places, steps, screen, bool(tot...  9.15 us
    all_to_all x1, starting transfers between devices, exchange(): value = lax.all_to_all(value, BOTH, split_axis=0, concat_axis=0, tiled=True)  6.36 us
    ppermute x1, starting transfers between devices, local(): lax.ppermute(last_rows(density, flux_x, flux_y), 'space', [(i, i + 1) for...  4.57 us
  transfers between devices with their start and end apart: 2, of which 1 were waited for; matrix products, arithmetic and copies ran while one was open for 1% of the time, Pallas kernels for 2%

profile of v4, /device:TPU:1, one launch (start us, length us, event | category | flops | bytes accessed | tf_op | source)
XLA Modules:
  0.0 213.7 jit_solution(585653320475926866)
XLA Ops:
  0.6 0.9 edges.1
  1.5 4.6 %collective-permute-start = (f32[3,4,512]{2,1,0:T(4,128)S(1)}, f32[3,4,512]{2,1,0:T(4,128)S(1)}, u32[]{:S(2)}, u32[]{:S(2)}) collective-permute-start(f32[3,4,512]{2,1,0:T(4,128)S(1)} %edges.1), channel_id=1, source_target_pairs={{0,1},{1,2},{2,3},{3,4},{4,5},{5,6},{6,7},{8,9},{9,10},{10,11},{11... | collective-permute-start | bytes 73736 | tf_op jit(solution)/shard_map/ppermute | solution.py:414
  6.1 0.1 pad_add_fusion.place.refs_0_
  6.2 0.0 copy-start
  6.2 0.0 copy-start.1
  6.2 0.0 copy-start.2
  6.2 4.1 %prox.1 = (f32[4,64,512]{2,1,0:T(8,128)S(1)}, f32[4,64,512]{2,1,0:T(8,128)S(1)}, f32[4,64,512]{2,1,0:T(8,128)S(1)}, f32[4,64,512]{2,1,0:T(8,128)S(1)}, f32[4,64,...) custom-call(f32[4,64,512]{2,1,0:T(8,128)} %d.3, f32[4,64,512]{2,1,0:T(8,128)} %fx.3, f32[4,64,512]{2,1,0:T(8,128)} %fy.3), custom_call_target="tpu_custom_call" | custom-call | flops 26214400 | bytes 3145728 | tf_op jit(solution)/shard_map/prox/pallas_call | solution.py:417
  10.3 0.0 collective-permute-done.edge
  10.3 0.0 copy-done
  10.3 0.0 copy-done.1
  10.3 0.0 copy-done.2
  10.3 1.9 forward.1
  12.2 0.0 copy-start.4
  12.2 0.0 copy-start.5
  12.2 0.0 copy-start.6
  12.3 0.0 copy-start.7
  12.3 0.0 copy-start.8
  12.3 0.0 copy-start.9
  12.3 0.0 copy-start.10
  12.3 36.4 %all_to_all.30 = f32[256,1,640]{2,1,0:T(1,128)S(1)} all-to-all(f32[256,1,640]{2,1,0:T(1,128)S(1)} %bitcast.20), channel_id=1, replica_groups=mesh['tm'=32,'space'=8] {'tm','space'}, dimensions={0} | all-to-all | bytes 1310720 | tf_op jit(solution)/shard_map/all_to_all | solution.py:411
  48.7 0.0 copy-done.4
  48.7 0.0 copy-done.5
  48.7 0.0 copy-done.6
  48.7 0.0 copy-done.7
  48.7 0.0 copy-done.8
  48.7 0.0 copy-done.9
  48.7 0.0 copy-done.10
  48.7 3.2 %solve.3 = (f32[1280,128]{1,0:T(8,128)S(1)}, f32[256,512]{1,0:T(8,128)S(1)}) custom-call(s32[2]{0:T(128)S(1)} %pad_add_fusion.place.refs_0_, f32[512]{0:T(512)S(1)} %copy-done.10, f32[1280,128]{1,0:T(8,128)S(1)} %bitcast.23, bf16[512,512]{1,0:T(8,128)(2,1)S(1)} %copy-done.1, bf16[512,512]{1,0:T(8,128)(2,1)S(1)} %copy-done, bf16[128,128]{1,0:T(8,128)(2,1)S(1)} %copy-done.8, ...), custom_call_target="tpu_custom_call" | custom-call | flops 1207959552 | bytes 3145728 | tf_op jit(solution)/shard_map/solve/pallas_call | solution.py:430
  52.0 28.8 %all_to_all.31 = f32[256,1,640]{2,1,0:T(1,128)S(1)} all-to-all(f32[256,1,640]{2,1,0:T(1,128)S(1)} %bitcast.24), channel_id=1, replica_groups=mesh['tm'=32,'space'=8] {'tm','space'}, dimensions={0} | all-to-all | bytes 1310720 | tf_op jit(solution)/shard_map/all_to_all | solution.py:411
  80.8 5.7 %middle.2 = (f32[4,64,512]{2,1,0:T(8,128)S(1)}, f32[4,64,512]{2,1,0:T(8,128)S(1)}, f32[4,64,512]{2,1,0:T(8,128)S(1)}, f32[1280,128]{1,0:T(8,128)S(1)}, f32[3,4,512]{2,1,0:T(4,128)S(1)}, /*index=5*/f32[16,512]{1,0:T(8,128)S(1)}) custom-call(s32[2]{0:T(128)S(1)} %pad_add_fusion.place.refs_0_, f32[1280,128]{1,0:T(8,128)S(1)} %bitcast.14, ...), custom_call_target="tpu_custom_call" | custom-call | flops 805306368 | bytes 5242880 | tf_op jit(solution)/shard_map/middle/pallas_call | solution.py:440
  86.5 28.8 %all_to_all.32 = f32[256,1,640]{2,1,0:T(1,128)S(1)} all-to-all(f32[256,1,640]{2,1,0:T(1,128)S(1)} %bitcast.18), channel_id=1, replica_groups=mesh['tm'=32,'space'=8] {'tm','space'}, dimensions={0} | all-to-all | bytes 1310720 | tf_op jit(solution)/shard_map/all_to_all | solution.py:411
  115.2 3.3 %solve.4 = (f32[1280,128]{1,0:T(8,128)S(1)}, f32[256,512]{1,0:T(8,128)S(1)}) custom-call(s32[2]{0:T(128)S(1)} %pad_add_fusion.place.refs_0_, f32[512]{0:T(512)S(1)} %copy-done.10, f32[1280,128]{1,0:T(8,128)S(1)} %bitcast.21, bf16[512,512]{1,0:T(8,128)(2,1)S(1)} %copy-done.1, bf16[512,512]{1,0:T(8,128)(2,1)S(1)} %copy-done, bf16[128,128]{1,0:T(8,128)(2,1)S(1)} %copy-done.8, ...), custom_call_target="tpu_custom_call" | custom-call | flops 1207959552 | bytes 3145728 | tf_op jit(solution)/shard_map/solve/pallas_call | solution.py:430
  118.5 28.8 %all_to_all.33 = f32[256,1,640]{2,1,0:T(1,128)S(1)} all-to-all(f32[256,1,640]{2,1,0:T(1,128)S(1)} %bitcast.22), channel_id=1, replica_groups=mesh['tm'=32,'space'=8] {'tm','space'}, dimensions={0} | all-to-all | bytes 1310720 | tf_op jit(solution)/shard_map/all_to_all | solution.py:411
  147.3 5.8 %middle.3 = (f32[4,64,512]{2,1,0:T(8,128)S(1)}, f32[4,64,512]{2,1,0:T(8,128)S(1)}, f32[4,64,512]{2,1,0:T(8,128)S(1)}, f32[1280,128]{1,0:T(8,128)S(1)}, f32[3,4,512]{2,1,0:T(4,128)}, /*index=5*/f32[16,512]{1,0:T(8,128)}) custom-call(s32[2]{0:T(128)S(1)} %pad_add_fusion.place.refs_0_, f32[1280,128]{1,0:T(8,128)S(1)} %bitcast.15, ...), custom_call_target="tpu_custom_call" | custom-call | flops 805306368 | bytes 5242880 | tf_op jit(solution)/shard_map/middle/pallas_call | solution.py:440
  153.1 28.8 %all_to_all.34 = f32[256,1,640]{2,1,0:T(1,128)S(1)} all-to-all(f32[256,1,640]{2,1,0:T(1,128)S(1)} %bitcast.19), channel_id=1, replica_groups=mesh['tm'=32,'space'=8] {'tm','space'}, dimensions={0} | all-to-all | bytes 1310720 | tf_op jit(solution)/shard_map/all_to_all | solution.py:411
  181.8 2.7 %solve.5 = (f32[1024,128]{1,0:T(8,128)S(1)}, f32[256,512]{1,0:T(8,128)}) custom-call(s32[2]{0:T(128)S(1)} %pad_add_fusion.place.refs_0_, f32[512]{0:T(512)S(1)} %copy-done.10, f32[1280,128]{1,0:T(8,128)S(1)} %bitcast.17, bf16[512,512]{1,0:T(8,128)(2,1)S(1)} %copy-done.1, bf16[512,512]{1,0:T(8,128)(2,1)S(1)} %copy-done, bf16[128,128]{1,0:T(8,128)(2,1)S(1)} %copy-done.8, ...), custom_call_target="tpu_custom_call" | custom-call | flops 1207959552 | bytes 3145728 | tf_op jit(solution)/shard_map/solve/pallas_call | solution.py:430
  184.5 0.0 copy-start.3
  184.5 0.8 copy-done.3
  185.3 6.4 %all-to-all-start.5 = ((f32[256,1,512]{2,1,0:T(1,128)}), f32[256,1,512]{2,1,0:T(1,128)S(1)}, u32[]{:S(2)}, u32[]{:S(2)}) async-start(f32[256,1,512]{2,1,0:T(1,128)} %bitcast.25), calls=%async_computation.5 | async-start | bytes 1048576 | tf_op jit(solution)/shard_map/all_to_all | solution.py:411
  191.7 0.8 copy.23
  192.5 0.8 copy.24
  193.3 0.8 copy.25
  194.1 18.2 %all-to-all-done.5 = f32[256,1,512]{2,1,0:T(1,128)S(1)} async-done(((f32[256,1,512]{2,1,0:T(1,128)}), f32[256,1,512]{2,1,0:T(1,128)S(1)}, u32[]{:S(2)}, u32[]{:S(2)}) %all-to-all-start.5) | async-done | bytes 524320 | tf_op jit(solution)/shard_map/all_to_all | solution.py:411
  212.2 1.3 last.1
Async XLA Ops:
  1.5 8.7 %collective-permute-start = (f32[3,4,512]{2,1,0:T(4,128)S(1)}, f32[3,4,512]{2,1,0:T(4,128)S(1)}, u32[]{:S(2)}, u32[]{:S(2)}) collective-permute-start(f32[3,4,512]{2,1,0:T(4,128)S(1)} %edges.1), channel_id=1, source_target_pairs={{0,1},{1,2},{2,3},{3,4},{4,5},{5,6},{6,7},{8,9},{9,10},{10,11},{11... | collective-permute-start | bytes 73736 | tf_op jit(solution)/shard_map/ppermute | solution.py:414
  6.2 4.1 %copy-start = (bf16[512,512]{1,0:T(8,128)(2,1)S(1)}, bf16[512,512]{1,0:T(8,128)(2,1)}, u32[]{:S(2)}) copy-start(bf16[512,512]{1,0:T(8,128)(2,1)} %constant.32.clone.cl.refs_4_) | copy-start | bytes 1572868
  6.2 4.1 %copy-start.1 = (bf16[512,512]{1,0:T(8,128)(2,1)S(1)}, bf16[512,512]{1,0:T(8,128)(2,1)}, u32[]{:S(2)}) copy-start(bf16[512,512]{1,0:T(8,128)(2,1)} %constant.31.clone.ch.refs_3_) | copy-start | bytes 1572868
  6.2 4.1 %copy-start.2 = (f32[4,64,512]{2,1,0:T(8,128)S(1)}, f32[4,64,512]{2,1,0:T(8,128)}, u32[]{:S(2)}) copy-start(f32[4,64,512]{2,1,0:T(8,128)} %src.5) | copy-start | bytes 1572868
  12.2 36.5 %copy-start.4 = (f32[128,1]{1,0:T(8,128)S(1)}, f32[128,1]{1,0:T(8,128)}, u32[]{:S(2)}) copy-start(f32[128,1]{1,0:T(8,128)} %constant.39.clone.refs_10_) | copy-start | bytes 1540
  12.2 36.5 %copy-start.5 = (bf16[128,128]{1,0:T(8,128)(2,1)S(1)}, bf16[128,128]{1,0:T(8,128)(2,1)}, u32[]{:S(2)}) copy-start(bf16[128,128]{1,0:T(8,128)(2,1)} %constant.36.clone.refs_8_) | copy-start | bytes 98308
  12.2 36.4 %copy-start.6 = (bf16[128,128]{1,0:T(8,128)(2,1)S(1)}, bf16[128,128]{1,0:T(8,128)(2,1)}, u32[]{:S(2)}) copy-start(bf16[128,128]{1,0:T(8,128)(2,1)} %constant.35.clone.refs_7_) | copy-start | bytes 98308
  12.3 36.4 %copy-start.7 = (bf16[128,128]{1,0:T(8,128)(2,1)S(1)}, bf16[128,128]{1,0:T(8,128)(2,1)}, u32[]{:S(2)}) copy-start(bf16[128,128]{1,0:T(8,128)(2,1)} %constant.34.clone.refs_6_) | copy-start | bytes 98308
  12.3 36.4 %copy-start.8 = (bf16[128,128]{1,0:T(8,128)(2,1)S(1)}, bf16[128,128]{1,0:T(8,128)(2,1)}, u32[]{:S(2)}) copy-start(bf16[128,128]{1,0:T(8,128)(2,1)} %constant.33.clone.refs_5_) | copy-start | bytes 98308
  12.3 36.4 %copy-start.9 = (f32[1,512]{1,0:T(1,128)S(1)}, f32[1,512]{1,0:T(1,128)}, u32[]{:S(2)}) copy-start(f32[1,512]{1,0:T(1,128)} %constant.38.clone.refs_9_) | copy-start | bytes 6148
  12.3 36.4 %copy-start.10 = (f32[512]{0:T(512)S(1)}, f32[512]{0:T(512)}, u32[]{:S(2)}) copy-start(f32[512]{0:T(512)} %constant.37.clone.refs_1_) | copy-start | bytes 6148
  184.5 0.8 copy-start.3
  185.3 26.9 %all-to-all-start.5 = ((f32[256,1,512]{2,1,0:T(1,128)}), f32[256,1,512]{2,1,0:T(1,128)S(1)}, u32[]{:S(2)}, u32[]{:S(2)}) async-start(f32[256,1,512]{2,1,0:T(1,128)} %bitcast.25), calls=%async_computation.5 | async-start | bytes 1048576 | tf_op jit(solution)/shard_map/all_to_all | solution.py:411

commit v5 on v4

--- a/solution.py
+++ b/solution.py
@@ -89,13 +89,12 @@
     target = 0.5 * TAU_STEP * (along_x * along_x + along_y * along_y)
     root = jnp.maximum(mass, 0.0) + jnp.exp(jnp.log(target) * (1.0 / 3.0))
     shifted = root + TAU_STEP
-    base = mass + TAU_STEP
-    base_twice = base + base
+    half_base = 0.5 * (mass + TAU_STEP)
+    quarter = 0.25 * target
     for _ in range(NEWTON):
-        twice = shifted + shifted
-        above = (shifted * shifted) * (twice - base) + target
-        below = shifted * ((twice + shifted) - base_twice)
-        shifted = jnp.maximum(above / below, TAU_STEP)
+        half = 0.5 * shifted
+        product = shifted * (shifted - half_base)
+        shifted = jnp.maximum((half * product + quarter) / (product - half * half), TAU_STEP)
     root = shifted - TAU_STEP
     factor = root / shifted
     return root, factor * along_x, factor * along_y
@@ -119,34 +118,40 @@
     lax.fori_loop(0, steps * per, step, 0)
 
 
-def transform_back(y, ch, cl, u, pair, group, packed_edge=False):
+def transform_back(y, ch, cl, u, pair, group):
     count = y.shape[0] // group
     lanes = y.shape[1]
-    if packed_edge:
-        both = y[pl.ds(pair * 2, count, stride=group), :]
-        even, odd = both, pltpu.roll(both, lanes // 2, 1)
-        kept = lanes // 2
-    else:
-        even = y[pl.ds(pair, count, stride=group), :]
-        odd = y[pl.ds(group // 2 + pair, count, stride=group), :]
-        kept = lanes
-    value = dot3(halves(jnp.concatenate([even, odd], axis=0)), (ch[...], cl[...]), TN)
-    u[pair * lanes : pair * lanes + kept, :] = value[:kept, :]
-
-
-def fill_plane(u, steps, rows, screen, residual_sum):
-    at = (steps - 1) * rows + KEPT
-    here = u[at : at + BLOCK, :]
+    even = y[pl.ds(pair, count, stride=group), :]
+    odd = y[pl.ds(group // 2 + pair, count, stride=group), :]
+    u[pair * lanes : (pair + 1) * lanes, :] = dot3(halves(jnp.concatenate([even, odd], axis=0)), (ch[...], cl[...]), TN)
+
+
+def other_step(here, beyond, above, below, screen, residual_sum):
     width = here.shape[1]
     column = lax.broadcasted_iota(jnp.int32, here.shape, 1)
     right = jnp.where(column == width - 1, here, pltpu.roll(here, width - 1, 1))
     left = jnp.where(column == 0, here, pltpu.roll(here, 1, 1))
-    earlier = u[at - rows : at - rows + BLOCK, :]
-    value = (here - earlier) + (here - u[at - 1 : at - 1 + BLOCK, :]) + (here - u[at + 1 : at + 1 + BLOCK, :])
-    value = here + (value + (here - right) + (here - left) + screen * here - residual_sum)
-    at = steps * rows + KEPT
+    value = (here - beyond) + (here - above) + (here - below) + (here - right) + (here - left)
+    return here + (value + (screen * here - residual_sum))
+
+
+def fill_steps(u, steps, rows, screen, kept_sum):
+    edge = (steps + 1) * rows
+    u[edge : edge + TAKEN, :] = u[KEPT : KEPT + TAKEN, :]
+    at = rows + KEPT
+    value = other_step(
+        u[at : at + BLOCK, :], u[at + rows : at + rows + BLOCK, :], u[at - 1 : at - 1 + BLOCK, :],
+        u[at + 1 : at + 1 + BLOCK, :], screen, kept_sum[:BLOCK, :],
+    )
+    row = lax.broadcasted_iota(jnp.int32, value.shape, 0)
+    u[KEPT : KEPT + BLOCK, :] = jnp.where(row < TAKEN, value, u[KEPT : KEPT + BLOCK, :])
+    at = (steps - 1) * rows
+    here = u[at : at + rows, :]
     row = lax.broadcasted_iota(jnp.int32, here.shape, 0)
-    u[at : at + BLOCK, :] = jnp.where(row < TAKEN, value, u[at : at + BLOCK, :])
+    above = jnp.where(row == 0, u[edge + 2 * steps - 1 : edge + 2 * steps, :], pltpu.roll(here, 1, 0))
+    below = jnp.where(row == rows - 1, u[edge + steps - 1 : edge + steps, :], pltpu.roll(here, rows - 1, 0))
+    value = other_step(here, u[at - rows : at, :], above, below, screen, kept_sum[BLOCK:, :])
+    u[at + rows : at + 2 * rows, :] = value
 
 
 def dual_step(d, fx, fy, edge, u, nd, nx, ny):
@@ -196,7 +201,10 @@
         high, low = halves(value)
         rh[t * rows : (t + 1) * rows, :] = high
         rl[t * rows : (t + 1) * rows, :] = low
-    kept[...] = value[KEPT : KEPT + BLOCK, :]
+        if t == 1:
+            kept[:BLOCK, :] = value[KEPT : KEPT + BLOCK, :]
+        if t == steps - 1:
+            kept[BLOCK:, :] = value
     high, low = halves(before)
     for t in (steps, steps + 1):
         rh[t * rows : (t + 1) * rows, :] = high
@@ -268,13 +276,9 @@
 
 def middle_body(last_place, screen, place, y, d, fx, fy, src, edge, kept_sum, ch, cl, nd, nx, ny, out, new_edge, kept, u, rh, rl):
     steps, rows, _ = d.shape
-    pairs = steps // 2
-    for pair in range(pairs):
-        transform_back(y, ch, cl, u, pair, 2 * pairs + 1)
-    transform_back(y, ch, cl, u, pairs, 2 * pairs + 1, True)
-    at = steps * rows
-    u[at + rows : at + rows + TAKEN, :] = u[at + KEPT : at + KEPT + TAKEN, :]
-    fill_plane(u, steps, rows, screen, kept_sum[...])
+    for pair in range(steps // 2):
+        transform_back(y, ch, cl, u, pair, steps)
+    fill_steps(u, steps, rows, screen, kept_sum)
     fresh = newton(*dual_step(d, fx, fy, edge, u, nd, nx, ny))
     for k in range(3):
         new_edge[k] = fresh[k]
@@ -297,9 +301,13 @@
 
 def solve_body(slabs, places, steps, screen, with_sum, with_edges, *refs):
     if with_sum:
-        place, values, z, ch, cl, wh, wl, vh, vl, across, around, so_far, out, total, field = refs
+        z, ch, cl, wh, wl, vh, vl, inverse, so_far, out, total, field = refs
     else:
-        place, values, z, ch, cl, wh, wl, vh, vl, across, around, out, total, field = refs
+        place, values, z, ch, cl, wh, wl, vh, vl, across, around, out, total, inverse, field = refs
+        for mode in range(2):
+            inverse[mode * slabs * steps : (mode + 1) * slabs * steps, :] = 1.0 / (
+                around[...] + across[...] + (values[place[1] + mode] + screen)
+            )
     length = slabs * steps
     pairs = steps // 2
     lanes = z.shape[1]
@@ -331,48 +339,40 @@
     for mode in range(2):
         span = slice(mode * length, (mode + 1) * length)
         field[span, :] = dot3((wh[...], wl[...]), halves(field[span, :]), NN)
-    modes = dot3(halves(field[...]), cosine, NT)
-    for mode in range(2):
-        span = slice(mode * length, (mode + 1) * length)
-        solved = modes[span, :] / (around[...] + across[...] + (values[place[1] + mode] + screen))
-        if with_sum:
-            solved = solved + so_far[span, :]
-        total[span, :] = solved
-    field[...] = dot3(halves(total[...]), cosine, NN)
+    solved = dot3(halves(field[...]), cosine, NT) * inverse[...]
+    if with_sum:
+        solved = solved + so_far[...]
+    total[...] = solved
+    field[...] = dot3(halves(solved), cosine, NN)
     for mode in range(2):
         span = slice(mode * length, (mode + 1) * length)
         field[span, :] = dot3((vh[...], vl[...]), halves(field[span, :]), NN)
-    group_out = 2 * pairs + 1 if with_edges else 2 * pairs
-
     def leaving(place, item):
-        return pl.ds(place * group_out + item, slabs, stride=places * group_out)
+        return pl.ds(place * steps + item, slabs, stride=places * steps)
+
+    def with_row_values(value, top, spot):
+        after = (spot + 1) * rows if spot + 1 < places else (spot + 1) * rows - 1
+        before = max(spot * rows - 1, 0)
+        for t in range(steps):
+            column = field[top + t * slabs : top + (t + 1) * slabs, after : after + 1]
+            value = jnp.where(lane == KEPT + t, column, value)
+        for t in range(steps + 1):
+            column = field[top + (t % steps) * slabs : top + (t % steps + 1) * slabs, before : before + 1]
+            if t == steps:
+                column = pltpu.roll(jnp.broadcast_to(column, (slabs, lanes)), slabs - 1, 0)
+            value = jnp.where(lane == KEPT + steps + t, column, value)
+        return value
 
     for q in range(places // 2):
         span = slice(q * lanes, (q + 1) * lanes)
         for mode in range(2):
             for pair in range(pairs):
                 at = mode * length + 2 * pair * slabs
-                first, second = swap(field[at : at + slabs, span], field[at + slabs : at + 2 * slabs, span])
-                out[leaving(2 * q, mode * pairs + pair), :] = first
-                out[leaving(2 * q + 1, mode * pairs + pair), :] = second
-        if not with_edges:
-            continue
-        planes = swap(*[pltpu.roll(field[m * length : m * length + slabs, span], slabs - 1, 0) for m in range(2)])
-        for spot, value in zip((2 * q, 2 * q + 1), planes):
-            after = (spot + 1) * rows if spot + 1 < places else (spot + 1) * rows - 1
-            before = max(spot * rows - 1, 0)
-            for mode in range(2):
-                top = mode * length
-                at = mode * rows + KEPT
-                for t in range(steps):
-                    column = field[top + t * slabs : top + (t + 1) * slabs, after : after + 1]
-                    value = jnp.where(lane == at + t, column, value)
-                for t in range(steps + 1):
-                    column = field[top + (t % steps) * slabs : top + (t % steps + 1) * slabs, before : before + 1]
-                    if t == steps:
-                        column = pltpu.roll(jnp.broadcast_to(column, (slabs, lanes)), slabs - 1, 0)
-                    value = jnp.where(lane == at + steps + t, column, value)
-            out[leaving(spot, 2 * pairs), :] = value
+                both = swap(field[at : at + slabs, span], field[at + slabs : at + 2 * slabs, span])
+                for spot, value in zip((2 * q, 2 * q + 1), both):
+                    if with_edges and pair == 0:
+                        value = with_row_values(value, mode * length, spot)
+                    out[leaving(spot, mode * pairs + pair), :] = value
 
 
 def local(density, flux_x, flux_y, source):
@@ -413,7 +413,8 @@
 
     edge = lax.ppermute(last_rows(density, flux_x, flux_y), "space", [(i, i + 1) for i in range(places - 1)])
     split = [pltpu.VMEM(((steps + 2) * rows, width), bf16)] * 2
-    block = (BLOCK, width)
+    block = (BLOCK + rows, width)
+    square = (2 * length, width)
     new_d, new_x, new_y, density, flux_x, flux_y = call(
         prox_body, [field] * 6, scratch=[pltpu.SemaphoreType.DMA((3, steps))], far=3,
         cost=(density.size * 200, 6 * nbytes), name="prox",
@@ -423,17 +424,19 @@
         scratch=split, scalars=1, n_in=10, cost=(mega, 8 * nbytes), name="forward",
     )(place, density, flux_x, flux_y, new_d, new_x, new_y, source, edge, ch, cl)
     density, flux_x, flux_y = new_d, new_x, new_y
-    total = ()
     for iteration in range(ITERS):
         final = iteration + 1 == ITERS
         modes = exchange(modes)
-        modes, solved = call(
-            functools.partial(solve_body, slabs, places, steps, screen, bool(total), not final),
-            [packed(steps if final else items), (2 * length, width)],
-            scratch=[pltpu.VMEM((2 * length, width), f32)],
-            scalars=2, n_in=9 + len(total), cost=(3 * mega, 6 * nbytes), name="solve",
-        )(place, values, modes, ch, cl, wh, wl, vh, vl, across, around, *total)
-        total = (solved,)
+        body = functools.partial(solve_body, slabs, places, steps, screen, iteration > 0, not final)
+        settings = dict(scratch=[pltpu.VMEM(square, f32)], n_in=9, cost=(3 * mega, 6 * nbytes), name="solve")
+        shapes = [packed(steps), square]
+        matrices = (ch, cl, wh, wl, vh, vl)
+        if iteration:
+            modes, total = call(body, shapes, **settings)(modes, *matrices, inverse, total)
+        else:
+            modes, total, inverse = call(body, shapes + [square], scalars=2, **settings)(
+                place, values, modes, *matrices, across, around
+            )
         modes = exchange(modes)
         if final:
             break

time: 214 us -> 206 us (0.963)
  blocking collectives: 151 us -> 146 us
  Pallas kernels: 28.9 us -> 26.3 us
    all_to_all x5, blocking collectives: 151 us -> 146 us  [exchange(): value = lax.all_to_all(value, BOTH, split_axis=0, concat_axis=0, tiled=True)]
where the time goes in v5:
time: 206 us
  blocking collectives  146 us (71%)
  Pallas kernels  26.3 us (13%)
  waiting for transfers between devices  18.2 us (9%)
  starting transfers between devices  10.9 us (5%)
  local copies, waits for them, and re-layouts  3.23 us (2%)
    all_to_all x5, blocking collectives, exchange(): value = lax.all_to_all(value, BOTH, split_axis=0, concat_axis=0, tiled=True)  146 us
    all_to_all x1, waiting for transfers between devices, exchange(): value = lax.all_to_all(value, BOTH, split_axis=0, concat_axis=0, tiled=True)  18.2 us
    pallas_call x2, Pallas kernels, local(): call(functools.partial(middle_body, places - 1, screen), [field] * 3 + [p...  10.2 us
    all_to_all x1, starting transfers between devices, exchange(): value = lax.all_to_all(value, BOTH, split_axis=0, concat_axis=0, tiled=True)  6.37 us
    pallas_call x2, Pallas kernels, local(): call(body, shapes, **settings)(modes, *matrices, inverse, total)  4.85 us
    ppermute x1, starting transfers between devices, local(): lax.ppermute(last_rows(density, flux_x, flux_y), 'space', [(i, i + 1) for...  4.57 us
  transfers between devices with their start and end apart: 2, of which 1 were waited for; matrix products, arithmetic and copies ran while one was open for 1% of the time, Pallas kernels for 2%

profile of v5, /device:TPU:1, one launch (start us, length us, event | category | flops | bytes accessed | tf_op | source)
XLA Modules:
  0.0 205.6 jit_solution(13188981651712423637)
XLA Ops:
  0.6 0.9 edges.1
  1.5 4.6 %collective-permute-start = (f32[3,4,512]{2,1,0:T(4,128)S(1)}, f32[3,4,512]{2,1,0:T(4,128)S(1)}, u32[]{:S(2)}, u32[]{:S(2)}) collective-permute-start(f32[3,4,512]{2,1,0:T(4,128)S(1)} %edges.1), channel_id=1, source_target_pairs={{0,1},{1,2},{2,3},{3,4},{4,5},{5,6},{6,7},{8,9},{9,10},{10,11},{11... | collective-permute-start | bytes 73736 | tf_op jit(solution)/shard_map/ppermute | solution.py:414
  6.1 0.1 pad_add_fusion.place.refs_0_
  6.2 0.0 copy-start
  6.2 0.0 copy-start.1
  6.2 0.0 copy-start.2
  6.2 3.7 %prox.1 = (f32[4,64,512]{2,1,0:T(8,128)S(1)}, f32[4,64,512]{2,1,0:T(8,128)S(1)}, f32[4,64,512]{2,1,0:T(8,128)S(1)}, f32[4,64,512]{2,1,0:T(8,128)S(1)}, f32[4,64,...) custom-call(f32[4,64,512]{2,1,0:T(8,128)} %d.3, f32[4,64,512]{2,1,0:T(8,128)} %fx.3, f32[4,64,512]{2,1,0:T(8,128)} %fy.3), custom_call_target="tpu_custom_call" | custom-call | flops 26214400 | bytes 3145728 | tf_op jit(solution)/shard_map/prox/pallas_call | solution.py:418
  10.0 0.0 collective-permute-done.edge
  10.0 0.0 copy-done
  10.0 0.0 copy-done.1
  10.0 0.0 copy-done.2
  10.0 1.9 forward.1
  11.9 0.0 copy-start.4
  11.9 0.0 copy-start.5
  11.9 0.0 copy-start.6
  12.0 0.0 copy-start.7
  12.0 0.0 copy-start.8
  12.0 0.0 copy-start.9
  12.0 0.0 copy-start.10
  12.0 36.4 %all_to_all.30 = f32[256,1,640]{2,1,0:T(1,128)S(1)} all-to-all(f32[256,1,640]{2,1,0:T(1,128)S(1)} %bitcast.20), channel_id=1, replica_groups=mesh['tm'=32,'space'=8] {'tm','space'}, dimensions={0} | all-to-all | bytes 1310720 | tf_op jit(solution)/shard_map/all_to_all | solution.py:411
  48.4 0.0 copy-done.4
  48.4 0.0 copy-done.5
  48.4 0.0 copy-done.6
  48.4 0.0 copy-done.7
  48.4 0.0 copy-done.8
  48.4 0.0 copy-done.9
  48.4 0.0 copy-done.10
  48.4 3.3 %solve.3 = (f32[1024,128]{1,0:T(8,128)S(1)}, f32[256,512]{1,0:T(8,128)S(1)}, f32[256,512]{1,0:T(8,128)S(1)}) custom-call(s32[2]{0:T(128)S(1)} %pad_add_fusion.place.refs_0_, f32[512]{0:T(512)S(1)} %copy-done.10, f32[1280,128]{1,0:T(8,128)S(1)} %bitcast.21, bf16[512,512]{1,0:T(8,128)(2,1)S(1)} %copy-done.1, bf16[512,512]{1,0:T(8,128)(2,1)S(1)} %copy-done, ...), custom_call_target="tpu_custom_call" | custom-call | flops 1207959552 | bytes 3145728 | tf_op jit(solution)/shard_map/solve/pallas_call | solution.py:437
  51.8 26.7 %all_to_all.31 = f32[256,1,512]{2,1,0:T(1,128)S(1)} all-to-all(f32[256,1,512]{2,1,0:T(1,128)S(1)} %bitcast.24), channel_id=1, replica_groups=mesh['tm'=32,'space'=8] {'tm','space'}, dimensions={0} | all-to-all | bytes 1048576 | tf_op jit(solution)/shard_map/all_to_all | solution.py:411
  78.5 5.1 %middle.2 = (f32[4,64,512]{2,1,0:T(8,128)S(1)}, f32[4,64,512]{2,1,0:T(8,128)S(1)}, f32[4,64,512]{2,1,0:T(8,128)S(1)}, f32[1280,128]{1,0:T(8,128)S(1)}, f32[3,4,512]{2,1,0:T(4,128)S(1)}, /*index=5*/f32[80,512]{1,0:T(8,128)S(1)}) custom-call(s32[2]{0:T(128)S(1)} %pad_add_fusion.place.refs_0_, f32[1024,128]{1,0:T(8,128)S(1)} %bitcast.16, ...), custom_call_target="tpu_custom_call" | custom-call | flops 805306368 | bytes 5242880 | tf_op jit(solution)/shard_map/middle/pallas_call | solution.py:443
  83.6 28.0 %all_to_all.32 = f32[256,1,640]{2,1,0:T(1,128)S(1)} all-to-all(f32[256,1,640]{2,1,0:T(1,128)S(1)} %bitcast.18), channel_id=1, replica_groups=mesh['tm'=32,'space'=8] {'tm','space'}, dimensions={0} | all-to-all | bytes 1310720 | tf_op jit(solution)/shard_map/all_to_all | solution.py:411
  111.6 2.8 %solve.4 = (f32[1024,128]{1,0:T(8,128)S(1)}, f32[256,512]{1,0:T(8,128)S(1)}) custom-call(f32[1280,128]{1,0:T(8,128)S(1)} %bitcast.22, bf16[512,512]{1,0:T(8,128)(2,1)S(1)} %copy-done.1, bf16[512,512]{1,0:T(8,128)(2,1)S(1)} %copy-done, bf16[128,128]{1,0:T(8,128)(2,1)S(1)} %copy-done.8, bf16[128,128]{1,0:T(8,128)(2,1)S(1)} %copy-done.7, ...), custom_call_target="tpu_custom_call" | custom-call | flops 1207959552 | bytes 3145728 | tf_op jit(solution)/shard_map/solve/pallas_call | solution.py:435
  114.4 26.7 %all_to_all.33 = f32[256,1,512]{2,1,0:T(1,128)S(1)} all-to-all(f32[256,1,512]{2,1,0:T(1,128)S(1)} %bitcast.25), channel_id=1, replica_groups=mesh['tm'=32,'space'=8] {'tm','space'}, dimensions={0} | all-to-all | bytes 1048576 | tf_op jit(solution)/shard_map/all_to_all | solution.py:411
  141.1 5.1 %middle.3 = (f32[4,64,512]{2,1,0:T(8,128)S(1)}, f32[4,64,512]{2,1,0:T(8,128)S(1)}, f32[4,64,512]{2,1,0:T(8,128)S(1)}, f32[1280,128]{1,0:T(8,128)S(1)}, f32[3,4,512]{2,1,0:T(4,128)}, /*index=5*/f32[80,512]{1,0:T(8,128)}) custom-call(s32[2]{0:T(128)S(1)} %pad_add_fusion.place.refs_0_, f32[1024,128]{1,0:T(8,128)S(1)} %bitcast.15, ...), custom_call_target="tpu_custom_call" | custom-call | flops 805306368 | bytes 5242880 | tf_op jit(solution)/shard_map/middle/pallas_call | solution.py:443
  146.2 28.0 %all_to_all.34 = f32[256,1,640]{2,1,0:T(1,128)S(1)} all-to-all(f32[256,1,640]{2,1,0:T(1,128)S(1)} %bitcast.17), channel_id=1, replica_groups=mesh['tm'=32,'space'=8] {'tm','space'}, dimensions={0} | all-to-all | bytes 1310720 | tf_op jit(solution)/shard_map/all_to_all | solution.py:411
  174.3 2.1 %solve.5 = (f32[1024,128]{1,0:T(8,128)S(1)}, f32[256,512]{1,0:T(8,128)}) custom-call(f32[1280,128]{1,0:T(8,128)S(1)} %bitcast.19, bf16[512,512]{1,0:T(8,128)(2,1)S(1)} %copy-done.1, bf16[512,512]{1,0:T(8,128)(2,1)S(1)} %copy-done, bf16[128,128]{1,0:T(8,128)(2,1)S(1)} %copy-done.8, bf16[128,128]{1,0:T(8,128)(2,1)S(1)} %copy-done.7, ...), custom_call_target="tpu_custom_call" | custom-call | flops 1207959552 | bytes 3145728 | tf_op jit(solution)/shard_map/solve/pallas_call | solution.py:435
  176.4 0.0 copy-start.3
  176.4 0.8 copy-done.3
  177.1 6.4 %all-to-all-start.5 = ((f32[256,1,512]{2,1,0:T(1,128)}), f32[256,1,512]{2,1,0:T(1,128)S(1)}, u32[]{:S(2)}, u32[]{:S(2)}) async-start(f32[256,1,512]{2,1,0:T(1,128)} %bitcast.23), calls=%async_computation.5 | async-start | bytes 1048576 | tf_op jit(solution)/shard_map/all_to_all | solution.py:411
  183.5 0.8 copy.23
  184.3 0.8 copy.24
  185.1 0.8 copy.25
  185.9 18.2 %all-to-all-done.5 = f32[256,1,512]{2,1,0:T(1,128)S(1)} async-done(((f32[256,1,512]{2,1,0:T(1,128)}), f32[256,1,512]{2,1,0:T(1,128)S(1)}, u32[]{:S(2)}, u32[]{:S(2)}) %all-to-all-start.5) | async-done | bytes 524320 | tf_op jit(solution)/shard_map/all_to_all | solution.py:411
  204.1 1.3 last.1
Async XLA Ops:
  1.5 8.4 %collective-permute-start = (f32[3,4,512]{2,1,0:T(4,128)S(1)}, f32[3,4,512]{2,1,0:T(4,128)S(1)}, u32[]{:S(2)}, u32[]{:S(2)}) collective-permute-start(f32[3,4,512]{2,1,0:T(4,128)S(1)} %edges.1), channel_id=1, source_target_pairs={{0,1},{1,2},{2,3},{3,4},{4,5},{5,6},{6,7},{8,9},{9,10},{10,11},{11... | collective-permute-start | bytes 73736 | tf_op jit(solution)/shard_map/ppermute | solution.py:414
  6.2 3.8 %copy-start = (bf16[512,512]{1,0:T(8,128)(2,1)S(1)}, bf16[512,512]{1,0:T(8,128)(2,1)}, u32[]{:S(2)}) copy-start(bf16[512,512]{1,0:T(8,128)(2,1)} %constant.32.clone.cl.refs_4_.refs_2_) | copy-start | bytes 1572868
  6.2 3.8 %copy-start.1 = (bf16[512,512]{1,0:T(8,128)(2,1)S(1)}, bf16[512,512]{1,0:T(8,128)(2,1)}, u32[]{:S(2)}) copy-start(bf16[512,512]{1,0:T(8,128)(2,1)} %constant.31.clone.ch.refs_3_.refs_1_) | copy-start | bytes 1572868
  6.2 3.8 %copy-start.2 = (f32[4,64,512]{2,1,0:T(8,128)S(1)}, f32[4,64,512]{2,1,0:T(8,128)}, u32[]{:S(2)}) copy-start(f32[4,64,512]{2,1,0:T(8,128)} %src.5) | copy-start | bytes 1572868
  11.9 36.5 %copy-start.4 = (f32[128,1]{1,0:T(8,128)S(1)}, f32[128,1]{1,0:T(8,128)}, u32[]{:S(2)}) copy-start(f32[128,1]{1,0:T(8,128)} %constant.39.clone.refs_10_) | copy-start | bytes 1540
  11.9 36.5 %copy-start.5 = (bf16[128,128]{1,0:T(8,128)(2,1)S(1)}, bf16[128,128]{1,0:T(8,128)(2,1)}, u32[]{:S(2)}) copy-start(bf16[128,128]{1,0:T(8,128)(2,1)} %constant.36.clone.refs_8_.refs_6_) | copy-start | bytes 98308
  11.9 36.4 %copy-start.6 = (bf16[128,128]{1,0:T(8,128)(2,1)S(1)}, bf16[128,128]{1,0:T(8,128)(2,1)}, u32[]{:S(2)}) copy-start(bf16[128,128]{1,0:T(8,128)(2,1)} %constant.35.clone.refs_7_.refs_5_) | copy-start | bytes 98308
  12.0 36.4 %copy-start.7 = (bf16[128,128]{1,0:T(8,128)(2,1)S(1)}, bf16[128,128]{1,0:T(8,128)(2,1)}, u32[]{:S(2)}) copy-start(bf16[128,128]{1,0:T(8,128)(2,1)} %constant.34.clone.refs_6_.refs_4_) | copy-start | bytes 98308
  12.0 36.4 %copy-start.8 = (bf16[128,128]{1,0:T(8,128)(2,1)S(1)}, bf16[128,128]{1,0:T(8,128)(2,1)}, u32[]{:S(2)}) copy-start(bf16[128,128]{1,0:T(8,128)(2,1)} %constant.33.clone.refs_5_.refs_3_) | copy-start | bytes 98308
  12.0 36.4 %copy-start.9 = (f32[1,512]{1,0:T(1,128)S(1)}, f32[1,512]{1,0:T(1,128)}, u32[]{:S(2)}) copy-start(f32[1,512]{1,0:T(1,128)} %constant.38.clone.refs_9_) | copy-start | bytes 6148
  12.0 36.4 %copy-start.10 = (f32[512]{0:T(512)S(1)}, f32[512]{0:T(512)}, u32[]{:S(2)}) copy-start(f32[512]{0:T(512)} %constant.37.clone.refs_1_) | copy-start | bytes 6148
  176.4 0.8 copy-start.3
  177.1 26.9 %all-to-all-start.5 = ((f32[256,1,512]{2,1,0:T(1,128)}), f32[256,1,512]{2,1,0:T(1,128)S(1)}, u32[]{:S(2)}, u32[]{:S(2)}) async-start(f32[256,1,512]{2,1,0:T(1,128)} %bitcast.23), calls=%async_computation.5 | async-start | bytes 1048576 | tf_op jit(solution)/shard_map/all_to_all | solution.py:411

commit v6 on v4

--- a/solution.py
+++ b/solution.py
@@ -15,8 +15,9 @@
 INTERPRET = False
 GRANT = 20 << 20
 KEPT = 8
-TAKEN = 9
+TAKEN = 13
 BLOCK = 16
+ORDER = (1, 2, 0, 3)
 BOTH = ("tm", "space")
 f32 = jnp.float32
 bf16 = jnp.bfloat16
@@ -89,13 +90,12 @@
     target = 0.5 * TAU_STEP * (along_x * along_x + along_y * along_y)
     root = jnp.maximum(mass, 0.0) + jnp.exp(jnp.log(target) * (1.0 / 3.0))
     shifted = root + TAU_STEP
-    base = mass + TAU_STEP
-    base_twice = base + base
+    half_base = 0.5 * (mass + TAU_STEP)
+    quarter = 0.25 * target
     for _ in range(NEWTON):
-        twice = shifted + shifted
-        above = (shifted * shifted) * (twice - base) + target
-        below = shifted * ((twice + shifted) - base_twice)
-        shifted = jnp.maximum(above / below, TAU_STEP)
+        half = 0.5 * shifted
+        product = shifted * (shifted - half_base)
+        shifted = jnp.maximum((half * product + quarter) / (product - half * half), TAU_STEP)
     root = shifted - TAU_STEP
     factor = root / shifted
     return root, factor * along_x, factor * along_y
@@ -103,7 +103,7 @@
 
 def prox_cells(source, result, wait=None):
     steps, rows, width = result[0].shape
-    chunk = 32
+    chunk = 16
     per = rows // chunk
 
     def step(index, carry):
@@ -119,19 +119,28 @@
     lax.fori_loop(0, steps * per, step, 0)
 
 
-def transform_back(y, ch, cl, u, pair, group, packed_edge=False):
-    count = y.shape[0] // group
+def send_values(y, hat_sum, qh, ql, pick, scale):
+    count = y.shape[0] // 3
     lanes = y.shape[1]
-    if packed_edge:
-        both = y[pl.ds(pair * 2, count, stride=group), :]
-        even, odd = both, pltpu.roll(both, lanes // 2, 1)
-        kept = lanes // 2
-    else:
-        even = y[pl.ds(pair, count, stride=group), :]
-        odd = y[pl.ds(group // 2 + pair, count, stride=group), :]
-        kept = lanes
-    value = dot3(halves(jnp.concatenate([even, odd], axis=0)), (ch[...], cl[...]), TN)
-    u[pair * lanes : pair * lanes + kept, :] = value[:kept, :]
+    both = y[pl.ds(2, count, stride=3), :]
+    outer = jnp.concatenate([y[pl.ds(0, count, stride=3), :], y[pl.ds(1, count, stride=3), :]], axis=0)
+    edge = jnp.concatenate([both, pltpu.roll(both, lanes // 2, 1)], axis=0)
+    sine = (qh[...], ql[...])
+    high, low = (lax.dot_general(part, pick[...], NN, preferred_element_type=f32) for part in halves(edge))
+    moved = high + low
+    modes = dot3(halves(outer + hat_sum[...] + moved[:, lanes:]), sine, NN)
+    inner = dot3(halves(modes * scale[...]), sine, NN) + moved[:, :lanes]
+    return outer, inner, edge
+
+
+def fill_slab(u, rows, outer, inner, edge, ch, cl):
+    cosine = (ch[...], cl[...])
+    value = dot3(halves(outer), cosine, TN)
+    u[:rows, :] = value[:rows, :]
+    u[3 * rows : 4 * rows, :] = value[rows:, :]
+    u[rows : 3 * rows, :] = dot3(halves(inner), cosine, TN)
+    if edge is not None:
+        u[4 * rows : 5 * rows, :] = dot3(halves(edge), cosine, TN)[:rows, :]
 
 
 def fill_plane(u, steps, rows, screen, residual_sum):
@@ -174,7 +183,7 @@
     )
 
 
-def residual_modes(place, last_place, d, fx, fy, nd, nx, ny, src, edge_x, new_edge_x, ch, cl, out, kept, rh, rl):
+def residual_modes(place, last_place, d, fx, fy, nd, nx, ny, src, edge_x, new_edge_x, ch, cl, out, kept, hat, rh, rl):
     steps, rows, width = d.shape
     shape = (rows, width)
     row = lax.broadcasted_iota(jnp.int32, shape, 0)
@@ -194,8 +203,9 @@
         value = value - src[t]
         before = mass
         high, low = halves(value)
-        rh[t * rows : (t + 1) * rows, :] = high
-        rl[t * rows : (t + 1) * rows, :] = low
+        at = ORDER.index(t) * rows
+        rh[at : at + rows, :] = high
+        rl[at : at + rows, :] = low
     kept[...] = value[KEPT : KEPT + BLOCK, :]
     high, low = halves(before)
     for t in (steps, steps + 1):
@@ -203,6 +213,7 @@
         rl[t * rows : (t + 1) * rows, :] = low
     modes = dot3((ch[...], cl[...]), (rh[...], rl[...]), NT)
     lanes = 2 * rows
+    hat[...] = modes[:, :lanes]
     pairs = steps // 2
     count = width // 2
     group = 2 * pairs + 1
@@ -241,7 +252,7 @@
     )(*map(stay, (density, flux_x, flux_y)))
 
 
-def prox_body(d, fx, fy, nd, nx, ny, own_d, own_x, own_y, sems):
+def prox_body(d, fx, fy, across, along, nd, nx, ny, own_d, own_x, own_y, scale, sems):
     steps = d.shape[0]
     moves = ((d, own_d), (fx, own_x), (fy, own_y))
 
@@ -252,6 +263,8 @@
         for k in range(3):
             copy(k, t).start()
 
+    scale[...] = 1.0 / (jnp.broadcast_to(across[...], scale.shape[::-1]).T + along[...])
+
     def wait(t):
         for k in range(3):
             copy(k, t).wait()
@@ -259,19 +272,19 @@
     prox_cells((own_d, own_x, own_y), (nd, nx, ny), wait)
 
 
-def forward_body(last_place, place, d, fx, fy, nd, nx, ny, src, edge, ch, cl, out, new_edge, kept, rh, rl):
+def forward_body(last_place, place, d, fx, fy, nd, nx, ny, src, edge, ch, cl, out, new_edge, kept, hat, rh, rl):
     fresh = newton(edge[0], edge[1], edge[2])
     for k in range(3):
         new_edge[k] = fresh[k]
-    residual_modes(place[0], last_place, d, fx, fy, nd, nx, ny, src, edge[1], fresh[1], ch, cl, out, kept, rh, rl)
-
-
-def middle_body(last_place, screen, place, y, d, fx, fy, src, edge, kept_sum, ch, cl, nd, nx, ny, out, new_edge, kept, u, rh, rl):
+    residual_modes(place[0], last_place, d, fx, fy, nd, nx, ny, src, edge[1], fresh[1], ch, cl, out, kept, hat, rh, rl)
+
+
+def middle_body(
+    last_place, screen, place, y, d, fx, fy, src, edge, kept_sum, hat_sum, ch, cl, qh, ql, pick, scale,
+    nd, nx, ny, out, new_edge, kept, hat, u, rh, rl,
+):
     steps, rows, _ = d.shape
-    pairs = steps // 2
-    for pair in range(pairs):
-        transform_back(y, ch, cl, u, pair, 2 * pairs + 1)
-    transform_back(y, ch, cl, u, pairs, 2 * pairs + 1, True)
+    fill_slab(u, rows, *send_values(y, hat_sum, qh, ql, pick, scale), ch, cl)
     at = steps * rows
     u[at + rows : at + rows + TAKEN, :] = u[at + KEPT : at + KEPT + TAKEN, :]
     fill_plane(u, steps, rows, screen, kept_sum[...])
@@ -279,27 +292,32 @@
     for k in range(3):
         new_edge[k] = fresh[k]
     prox_cells((nd, nx, ny), (nd, nx, ny))
-    residual_modes(place[0], last_place, d, fx, fy, nd, nx, ny, src, edge[1], fresh[1], ch, cl, out, kept, rh, rl)
+    residual_modes(place[0], last_place, d, fx, fy, nd, nx, ny, src, edge[1], fresh[1], ch, cl, out, kept, hat, rh, rl)
     kept[...] = kept[...] + kept_sum[...]
-
-
-def last_body(y, ch, cl, u, flat, sems):
+    hat[...] = hat[...] + hat_sum[...]
+
+
+def last_body(y, hat_sum, ch, cl, qh, ql, pick, scale, u, flat, sems):
     steps, rows, _ = u.shape
-    copies = []
-    for pair in range(steps // 2):
-        transform_back(y, ch, cl, flat, pair, steps)
-        for t in (2 * pair, 2 * pair + 1):
-            copies.append(pltpu.make_async_copy(flat.at[pl.ds(t * rows, rows), :], u.at[t], sems.at[t]))
-            copies[-1].start()
+    outer, inner, _ = send_values(y, hat_sum, qh, ql, pick, scale)
+    fill_slab(flat, rows, outer, inner, None, ch, cl)
+    copies = [pltpu.make_async_copy(flat.at[pl.ds(t * rows, rows), :], u.at[t], sems.at[t]) for t in range(steps)]
+    for copy in copies:
+        copy.start()
     for copy in copies:
         copy.wait()
 
 
-def solve_body(slabs, places, steps, screen, with_sum, with_edges, *refs):
+def solve_body(slabs, places, steps, screen, with_sum, *refs):
     if with_sum:
-        place, values, z, ch, cl, wh, wl, vh, vl, across, around, so_far, out, total, field = refs
+        z, ch, cl, wh, wl, inverse, so_far, out, total, field = refs
     else:
-        place, values, z, ch, cl, wh, wl, vh, vl, across, around, out, total, field = refs
+        place, values, z, ch, cl, wh, wl, across, around, out, total, inverse, field = refs
+        turned = jnp.broadcast_to(around[...], across.shape[1:] + around.shape[1:]).T
+        for mode in range(2):
+            inverse[mode * slabs * steps : (mode + 1) * slabs * steps, :] = 1.0 / (
+                turned + across[...] + (values[place[1] + mode] + screen)
+            )
     length = slabs * steps
     pairs = steps // 2
     lanes = z.shape[1]
@@ -322,27 +340,24 @@
             for pair in range(pairs):
                 item = mode * pairs + pair
                 first, second = swap(arrived(2 * q, item), arrived(2 * q + 1, item))
-                if pair == 0:
-                    first = first - pltpu.roll(planes[mode], 1, 0)
-                top = mode * length + 2 * pair * slabs
-                field[top : top + slabs, span] = first
-                field[top + slabs : top + 2 * slabs, span] = second
+                for t, value in zip(ORDER[2 * pair : 2 * pair + 2], (first, second)):
+                    if t == 0:
+                        value = value - pltpu.roll(planes[mode], 1, 0)
+                    top = mode * length + t * slabs
+                    field[top : top + slabs, span] = value
     cosine = (ch[...], cl[...])
     for mode in range(2):
         span = slice(mode * length, (mode + 1) * length)
         field[span, :] = dot3((wh[...], wl[...]), halves(field[span, :]), NN)
-    modes = dot3(halves(field[...]), cosine, NT)
+    solved = dot3(halves(field[...]), cosine, NT) * inverse[...]
+    if with_sum:
+        solved = solved + so_far[...]
+    total[...] = solved
+    field[...] = dot3(halves(solved), cosine, NN)
     for mode in range(2):
         span = slice(mode * length, (mode + 1) * length)
-        solved = modes[span, :] / (around[...] + across[...] + (values[place[1] + mode] + screen))
-        if with_sum:
-            solved = solved + so_far[span, :]
-        total[span, :] = solved
-    field[...] = dot3(halves(total[...]), cosine, NN)
-    for mode in range(2):
-        span = slice(mode * length, (mode + 1) * length)
-        field[span, :] = dot3((vh[...], vl[...]), halves(field[span, :]), NN)
-    group_out = 2 * pairs + 1 if with_edges else 2 * pairs
+        field[span, :] = dot3((wh[...], wl[...]), halves(field[span, :]), TN)
+    group_out = 3
 
     def leaving(place, item):
         return pl.ds(place * group_out + item, slabs, stride=places * group_out)
@@ -350,13 +365,11 @@
     for q in range(places // 2):
         span = slice(q * lanes, (q + 1) * lanes)
         for mode in range(2):
-            for pair in range(pairs):
-                at = mode * length + 2 * pair * slabs
-                first, second = swap(field[at : at + slabs, span], field[at + slabs : at + 2 * slabs, span])
-                out[leaving(2 * q, mode * pairs + pair), :] = first
-                out[leaving(2 * q + 1, mode * pairs + pair), :] = second
-        if not with_edges:
-            continue
+            at = mode * length
+            end = at + (steps - 1) * slabs
+            first, second = swap(field[at : at + slabs, span], field[end : end + slabs, span])
+            out[leaving(2 * q, mode), :] = first
+            out[leaving(2 * q + 1, mode), :] = second
         planes = swap(*[pltpu.roll(field[m * length : m * length + slabs, span], slabs - 1, 0) for m in range(2)])
         for spot, value in zip((2 * q, 2 * q + 1), planes):
             after = (spot + 1) * rows if spot + 1 < places else (spot + 1) * rows - 1
@@ -372,7 +385,11 @@
                     if t == steps:
                         column = pltpu.roll(jnp.broadcast_to(column, (slabs, lanes)), slabs - 1, 0)
                     value = jnp.where(lane == at + steps + t, column, value)
-            out[leaving(spot, 2 * pairs), :] = value
+                for k, (t, line) in enumerate(((1, 0), (1, rows - 1), (2, 0), (2, rows - 1))):
+                    line = spot * rows + line
+                    column = field[top + t * slabs : top + (t + 1) * slabs, line : line + 1]
+                    value = jnp.where(lane == at + 2 * steps + 1 + k, column, value)
+            out[leaving(spot, 2), :] = value
 
 
 def local(density, flux_x, flux_y, source):
@@ -385,13 +402,25 @@
     ch, cl = (jnp.asarray(m) for m in np_halves(cosine_matrix(width)[order]))
     basis, loop_values = loop_basis(length, slabs)
     wh, wl = (jnp.asarray(m) for m in np_halves(basis))
-    vh, vl = (jnp.asarray(m) for m in np_halves(np.ascontiguousarray(basis.T)))
     spectrum = neumann_spectrum(width)
     place = lax.axis_index("space")
     first = 2 * (lax.axis_index("tm") * places + place)
     values = jnp.asarray(spectrum)
+    count = np.arange(rows)
+    gaps = rows - 1
+    sine = np.sqrt(2.0 / gaps) * np.sin(np.pi * (np.outer(count, count) % (2 * gaps)) / gaps)
+    sine[0] = sine[-1] = sine[:, 0] = sine[:, -1] = 0.0
+    lines = np.sqrt(0.5) * np.block([[sine, sine], [sine, -sine]])
+    lanes_of = 2 * rows
+    pick = np.zeros((lanes_of, 2 * lanes_of), np.float32)
+    for spot, place_of, line in ((0, 0, 1), (1, rows - 1, rows - 2), (2, rows, rows + 1), (3, 2 * rows - 1, 2 * rows - 2)):
+        pick[KEPT + 2 * steps + 1 + spot, (place_of, lanes_of + line)] = 1.0
+    inner = [jnp.asarray(m) for m in np_halves(lines.astype(np.float32))]
+    inner.append(jnp.asarray(pick.astype(bf16)))
+    stiffness = 2.0 - 2.0 * np.cos(np.pi * count / gaps)
+    along = jnp.asarray((np.concatenate([1.0 + stiffness, 3.0 + stiffness]) + screen).astype(np.float32)[None, :])
     across = jnp.asarray(spectrum[order][None, :])
-    around = jnp.asarray(loop_values[:, None])
+    around = jnp.asarray(loop_values[None, :])
     place = jnp.stack([place, first]).astype(jnp.int32)
     nbytes = density.size * 4
     mega = density.size * width * 6
@@ -414,38 +443,41 @@
     edge = lax.ppermute(last_rows(density, flux_x, flux_y), "space", [(i, i + 1) for i in range(places - 1)])
     split = [pltpu.VMEM(((steps + 2) * rows, width), bf16)] * 2
     block = (BLOCK, width)
-    new_d, new_x, new_y, density, flux_x, flux_y = call(
-        prox_body, [field] * 6, scratch=[pltpu.SemaphoreType.DMA((3, steps))], far=3,
+    square = (2 * length, width)
+    hat_shape = (width, lanes)
+    new_d, new_x, new_y, density, flux_x, flux_y, scale = call(
+        prox_body, [field] * 6 + [hat_shape], scratch=[pltpu.SemaphoreType.DMA((3, steps))], far=3, n_in=2,
         cost=(density.size * 200, 6 * nbytes), name="prox",
-    )(*map(stay, (density, flux_x, flux_y)))
-    modes, edge, kept = call(
-        functools.partial(forward_body, places - 1), [packed(items), edge_shape, block],
+    )(*map(stay, (density, flux_x, flux_y)), across, along)
+    modes, edge, kept, hat = call(
+        functools.partial(forward_body, places - 1), [packed(items), edge_shape, block, hat_shape],
         scratch=split, scalars=1, n_in=10, cost=(mega, 8 * nbytes), name="forward",
     )(place, density, flux_x, flux_y, new_d, new_x, new_y, source, edge, ch, cl)
     density, flux_x, flux_y = new_d, new_x, new_y
-    total = ()
     for iteration in range(ITERS):
-        final = iteration + 1 == ITERS
         modes = exchange(modes)
-        modes, solved = call(
-            functools.partial(solve_body, slabs, places, steps, screen, bool(total), not final),
-            [packed(steps if final else items), (2 * length, width)],
-            scratch=[pltpu.VMEM((2 * length, width), f32)],
-            scalars=2, n_in=9 + len(total), cost=(3 * mega, 6 * nbytes), name="solve",
-        )(place, values, modes, ch, cl, wh, wl, vh, vl, across, around, *total)
-        total = (solved,)
+        body = functools.partial(solve_body, slabs, places, steps, screen, iteration > 0)
+        settings = dict(scratch=[pltpu.VMEM(square, f32)], n_in=7, cost=(3 * mega, 6 * nbytes), name="solve")
+        shapes = [packed(3), square]
+        matrices = (ch, cl, wh, wl)
+        if iteration:
+            modes, total = call(body, shapes, **settings)(modes, *matrices, inverse, total)
+        else:
+            modes, total, inverse = call(body, shapes + [square], scalars=2, **settings)(
+                place, values, modes, *matrices, across, around
+            )
         modes = exchange(modes)
-        if final:
+        if iteration + 1 == ITERS:
             break
-        density, flux_x, flux_y, modes, edge, kept = call(
-            functools.partial(middle_body, places - 1, screen), [field] * 3 + [packed(items), edge_shape, block],
+        density, flux_x, flux_y, modes, edge, kept, hat = call(
+            functools.partial(middle_body, places - 1, screen), [field] * 3 + [packed(items), edge_shape, block, hat_shape],
             scratch=[pltpu.VMEM(((steps + 1) * rows + BLOCK, width), f32)] + split,
-            scalars=1, n_in=9, cost=(2 * mega, 10 * nbytes), name="middle",
-        )(place, modes, density, flux_x, flux_y, source, edge, kept, ch, cl)
+            scalars=1, n_in=14, cost=(2 * mega, 10 * nbytes), name="middle",
+        )(place, modes, density, flux_x, flux_y, source, edge, kept, hat, ch, cl, *inner, scale)
     (potential,) = call(
         last_body, [field], scratch=[pltpu.VMEM((steps * rows, width), f32), pltpu.SemaphoreType.DMA((steps,))],
-        n_in=3, far_out=True, cost=(mega, 3 * nbytes), name="last",
-    )(modes, ch, cl)
+        n_in=8, far_out=True, cost=(mega, 3 * nbytes), name="last",
+    )(modes, hat, ch, cl, *inner, scale)
     return density, flux_x, flux_y, potential
 
 

time: 214 us -> 204 us (0.953)
  blocking collectives: 151 us -> 140 us
  waiting for transfers between devices: 18.2 us -> 15.8 us
  Pallas kernels: 28.9 us -> 31.1 us
    all_to_all x5, blocking collectives: 151 us -> 140 us  [exchange(): value = lax.all_to_all(value, BOTH, split_axis=0, concat_axis=0, tiled=True)]
    all_to_all x1, waiting for transfers between devices: 18.2 us -> 15.8 us  [exchange(): value = lax.all_to_all(value, BOTH, split_axis=0, concat_axis=0, tiled=True)]
    unnamed x25 -> x33, local copies, waits for them, and re-layouts: 3.23 us -> 4.42 us
where the time goes in v6:
time: 204 us
  blocking collectives  140 us (69%)
  Pallas kernels  31.1 us (15%)
  waiting for transfers between devices  15.8 us (8%)
  starting transfers between devices  10.9 us (5%)
  local copies, waits for them, and re-layouts  4.42 us (2%)
    all_to_all x5, blocking collectives, exchange(): value = lax.all_to_all(value, BOTH, split_axis=0, concat_axis=0, tiled=True)  140 us
    all_to_all x1, waiting for transfers between devices, exchange(): value = lax.all_to_all(value, BOTH, split_axis=0, concat_axis=0, tiled=True)  15.8 us
    pallas_call x2, Pallas kernels, local(): call(functools.partial(middle_body, places - 1, screen), [field] * 3 + [p...  12.5 us
    all_to_all x1, starting transfers between devices, exchange(): value = lax.all_to_all(value, BOTH, split_axis=0, concat_axis=0, tiled=True)  6.37 us
    pallas_call x2, Pallas kernels, local(): call(body, shapes, **settings)(modes, *matrices, inverse, total)  5.88 us
    ppermute x1, starting transfers between devices, local(): lax.ppermute(last_rows(density, flux_x, flux_y), 'space', [(i, i + 1) for...  4.57 us
    unnamed x33, local copies, waits for them, and re-layouts  4.42 us
    pallas_call x1, Pallas kernels, local(): call(prox_body, [field] * 6 + [hat_shape], scratch=[pltpu.SemaphoreType.D...  4.17 us
  transfers between devices with their start and end apart: 2, of which 1 were waited for; matrix products, arithmetic and copies ran while one was open for 1% of the time, Pallas kernels for 2%

profile of v6, /device:TPU:1, one launch (start us, length us, event | category | flops | bytes accessed | tf_op | source)
XLA Modules:
  0.0 203.6 jit_solution(1015896704395455433)
XLA Ops:
  0.6 0.9 edges.1
  1.5 4.6 %collective-permute-start = (f32[3,4,512]{2,1,0:T(4,128)S(1)}, f32[3,4,512]{2,1,0:T(4,128)S(1)}, u32[]{:S(2)}, u32[]{:S(2)}) collective-permute-start(f32[3,4,512]{2,1,0:T(4,128)S(1)} %edges.1), channel_id=1, source_target_pairs={{0,1},{1,2},{2,3},{3,4},{4,5},{5,6},{6,7},{8,9},{9,10},{10,11},{11... | collective-permute-start | bytes 73736 | tf_op jit(solution)/shard_map/ppermute | solution.py:443
  6.1 0.0 copy-start.9
  6.1 0.0 copy-start.10
  6.2 0.1 pad_add_fusion.place.refs_0_
  6.2 0.6 copy-done.9
  6.8 0.0 copy-done.10
  6.8 0.0 copy-start
  6.8 0.0 copy-start.1
  6.8 0.0 copy-start.2
  6.8 4.2 %prox.1 = (f32[4,64,512]{2,1,0:T(8,128)S(1)}, f32[4,64,512]{2,1,0:T(8,128)S(1)}, f32[4,64,512]{2,1,0:T(8,128)S(1)}, f32[4,64,512]{2,1,0:T(8,128)S(1)}, f32[4,64,...) custom-call(f32[4,64,512]{2,1,0:T(8,128)} %d.3, f32[4,64,512]{2,1,0:T(8,128)} %fx.3, ...), custom_call_target="tpu_custom_call" | custom-call | flops 26214400 | bytes 3145728 | tf_op jit(solution)/shard_map/prox/pallas_call | solution.py:448
  11.0 0.0 collective-permute-done.edge
  11.0 0.0 copy-done
  11.0 0.0 copy-done.1
  11.0 0.0 copy-done.2
  11.0 1.9 forward.1
  12.9 0.0 copy-start.11
  12.9 0.0 copy-start.12
  13.0 0.0 copy-start.13
  13.0 36.4 %all_to_all.30 = f32[256,1,640]{2,1,0:T(1,128)S(1)} all-to-all(f32[256,1,640]{2,1,0:T(1,128)S(1)} %bitcast.19), channel_id=1, replica_groups=mesh['tm'=32,'space'=8] {'tm','space'}, dimensions={0} | all-to-all | bytes 1310720 | tf_op jit(solution)/shard_map/all_to_all | solution.py:440
  49.4 0.0 copy-start.14
  49.4 0.0 copy-done.11
  49.4 0.0 copy-done.12
  49.4 0.0 copy-done.13
  49.4 0.6 copy-done.14
  50.0 3.5 %solve.3 = (f32[768,128]{1,0:T(8,128)S(1)}, f32[256,512]{1,0:T(8,128)S(1)}, f32[256,512]{1,0:T(8,128)S(1)}) custom-call(s32[2]{0:T(128)S(1)} %pad_add_fusion.place.refs_0_, f32[512]{0:T(512)S(1)} %copy-done.13, f32[1280,128]{1,0:T(8,128)S(1)} %bitcast.21, bf16[512,512]{1,0:T(8,128)(2,1)S(1)} %copy-done.1, bf16[512,512]{1,0:T(8,128)(2,1)S(1)} %copy-done, ...), custom_call_target="tpu_custom_call" | custom-call | flops 1207959552 | bytes 3145728 | tf_op jit(solution)/shard_map/solve/pallas_call | solution.py:466
  53.6 0.0 copy-start.3
  53.6 0.0 copy-start.5
  53.6 0.0 copy-start.6
  53.6 24.3 %all_to_all.31 = f32[256,1,384]{2,1,0:T(1,128)S(1)} all-to-all(f32[256,1,384]{2,1,0:T(1,128)S(1)} %bitcast.24), channel_id=1, replica_groups=mesh['tm'=32,'space'=8] {'tm','space'}, dimensions={0} | all-to-all | bytes 786432 | tf_op jit(solution)/shard_map/all_to_all | solution.py:440
  77.9 0.0 copy-done.3
  77.9 0.0 copy-done.5
  77.9 0.0 copy-done.6
  77.9 6.2 %middle.2 = (f32[4,64,512]{2,1,0:T(8,128)S(1)}, f32[4,64,512]{2,1,0:T(8,128)S(1)}, f32[4,64,512]{2,1,0:T(8,128)S(1)}, f32[1280,128]{1,0:T(8,128)S(1)}, f32[3,4,5...) custom-call(s32[2]{0:T(128)S(1)} %pad_add_fusion.place.refs_0_, f32[768,128]{1,0:T(8,128)S(1)} %bitcast.15, ...), custom_call_target="tpu_custom_call" | custom-call | flops 805306368 | bytes 5242880 | tf_op jit(solution)/shard_map/middle/pallas_call | solution.py:472
  84.2 27.6 %all_to_all.32 = f32[256,1,640]{2,1,0:T(1,128)S(1)} all-to-all(f32[256,1,640]{2,1,0:T(1,128)S(1)} %bitcast.18), channel_id=1, replica_groups=mesh['tm'=32,'space'=8] {'tm','space'}, dimensions={0} | all-to-all | bytes 1310720 | tf_op jit(solution)/shard_map/all_to_all | solution.py:440
  111.8 2.9 %solve.4 = (f32[768,128]{1,0:T(8,128)S(1)}, f32[256,512]{1,0:T(8,128)S(1)}) custom-call(f32[1280,128]{1,0:T(8,128)S(1)} %bitcast.22, bf16[512,512]{1,0:T(8,128)(2,1)S(1)} %copy-done.1, bf16[512,512]{1,0:T(8,128)(2,1)S(1)} %copy-done, bf16[128,128]{1,0:T(8,128)(2,1)S(1)} %copy-done.12, bf16[128,128]{1,0:T(8,128)(2,1)S(1)} %copy-done.11, ...), custom_call_target="tpu_custom_call" | custom-call | flops 1207959552 | bytes 3145728 | tf_op jit(solution)/shard_map/solve/pallas_call | solution.py:464
  114.7 24.3 %all_to_all.33 = f32[256,1,384]{2,1,0:T(1,128)S(1)} all-to-all(f32[256,1,384]{2,1,0:T(1,128)S(1)} %bitcast.25), channel_id=1, replica_groups=mesh['tm'=32,'space'=8] {'tm','space'}, dimensions={0} | all-to-all | bytes 786432 | tf_op jit(solution)/shard_map/all_to_all | solution.py:440
  139.1 6.2 %middle.3 = (f32[4,64,512]{2,1,0:T(8,128)S(1)}, f32[4,64,512]{2,1,0:T(8,128)S(1)}, f32[4,64,512]{2,1,0:T(8,128)S(1)}, f32[1280,128]{1,0:T(8,128)S(1)}, f32[3,4,5...) custom-call(s32[2]{0:T(128)S(1)} %pad_add_fusion.place.refs_0_, f32[768,128]{1,0:T(8,128)S(1)} %bitcast.16, ...), custom_call_target="tpu_custom_call" | custom-call | flops 805306368 | bytes 5242880 | tf_op jit(solution)/shard_map/middle/pallas_call | solution.py:472
  145.3 0.0 copy-start.7
  145.3 27.6 %all_to_all.34 = f32[256,1,640]{2,1,0:T(1,128)S(1)} all-to-all(f32[256,1,640]{2,1,0:T(1,128)S(1)} %bitcast.17), channel_id=1, replica_groups=mesh['tm'=32,'space'=8] {'tm','space'}, dimensions={0} | all-to-all | bytes 1310720 | tf_op jit(solution)/shard_map/all_to_all | solution.py:440
  172.9 0.0 copy-done.7
  172.9 2.9 %solve.5 = (f32[768,128]{1,0:T(8,128)S(1)}, f32[256,512]{1,0:T(8,128)}) custom-call(f32[1280,128]{1,0:T(8,128)S(1)} %bitcast.20, bf16[512,512]{1,0:T(8,128)(2,1)S(1)} %copy-done.1, bf16[512,512]{1,0:T(8,128)(2,1)S(1)} %copy-done, bf16[128,128]{1,0:T(8,128)(2,1)S(1)} %copy-done.12, bf16[128,128]{1,0:T(8,128)(2,1)S(1)} %copy-done.11, ...), custom_call_target="tpu_custom_call" | custom-call | flops 1207959552 | bytes 3145728 | tf_op jit(solution)/shard_map/solve/pallas_call | solution.py:464
  175.9 0.0 copy-start.4
  175.9 0.7 copy-done.4
  176.6 6.4 %all-to-all-start.5 = ((f32[256,1,384]{2,1,0:T(1,128)}), f32[256,1,384]{2,1,0:T(1,128)S(1)}, u32[]{:S(2)}, u32[]{:S(2)}) async-start(f32[256,1,384]{2,1,0:T(1,128)} %bitcast.23), calls=%async_computation.5 | async-start | bytes 786432 | tf_op jit(solution)/shard_map/all_to_all | solution.py:440
  183.0 0.8 copy.25
  183.8 0.8 copy.26
  184.6 0.0 copy-start.8
  184.6 0.8 copy.27
  185.4 15.8 %all-to-all-done.5 = f32[256,1,384]{2,1,0:T(1,128)S(1)} async-done(((f32[256,1,384]{2,1,0:T(1,128)}), f32[256,1,384]{2,1,0:T(1,128)S(1)}, u32[]{:S(2)}, u32[]{:S(2)}) %all-to-all-start.5) | async-done | bytes 393248 | tf_op jit(solution)/shard_map/all_to_all | solution.py:440
  201.2 0.0 copy-done.8
  201.2 2.2 %last.1 = f32[4,64,512]{2,1,0:T(8,128)} custom-call(f32[768,128]{1,0:T(8,128)S(1)} %bitcast.14, f32[512,128]{1,0:T(8,128)S(1)} %copy-done.8, bf16[512,512]{1,0:T(8,128)(2,1)S(1)} %copy-done.1, bf16[512,512]{1,0:T(8,128)(2,1)S(1)} %copy-done, bf16[128,128]{1,0:T(8,128)(2,1)S(1)} %copy-done.6, bf16[128,128]{1,0:T(8,128)(2,1)S(1)} %copy-done.5, ...), custom_call_target="tpu_custom_call" | custom-call | flops 402653184 | bytes 1572864 | tf_op jit(solution)/shard_map/last/pallas_call | solution.py:477
Async XLA Ops:
  1.5 9.5 %collective-permute-start = (f32[3,4,512]{2,1,0:T(4,128)S(1)}, f32[3,4,512]{2,1,0:T(4,128)S(1)}, u32[]{:S(2)}, u32[]{:S(2)}) collective-permute-start(f32[3,4,512]{2,1,0:T(4,128)S(1)} %edges.1), channel_id=1, source_target_pairs={{0,1},{1,2},{2,3},{3,4},{4,5},{5,6},{6,7},{8,9},{9,10},{10,11},{11... | collective-permute-start | bytes 73736 | tf_op jit(solution)/shard_map/ppermute | solution.py:443
  6.1 0.7 copy-start.9
  6.1 0.7 copy-start.10
  6.8 4.2 %copy-start = (bf16[512,512]{1,0:T(8,128)(2,1)S(1)}, bf16[512,512]{1,0:T(8,128)(2,1)}, u32[]{:S(2)}) copy-start(bf16[512,512]{1,0:T(8,128)(2,1)} %constant.36.clone.cl.refs_4_.refs_2_) | copy-start | bytes 1572868
  6.8 4.2 %copy-start.1 = (bf16[512,512]{1,0:T(8,128)(2,1)S(1)}, bf16[512,512]{1,0:T(8,128)(2,1)}, u32[]{:S(2)}) copy-start(bf16[512,512]{1,0:T(8,128)(2,1)} %constant.35.clone.ch.refs_3_.refs_1_) | copy-start | bytes 1572868
  6.8 4.2 %copy-start.2 = (f32[4,64,512]{2,1,0:T(8,128)S(1)}, f32[4,64,512]{2,1,0:T(8,128)}, u32[]{:S(2)}) copy-start(f32[4,64,512]{2,1,0:T(8,128)} %src.5) | copy-start | bytes 1572868
  12.9 36.4 %copy-start.11 = (bf16[128,128]{1,0:T(8,128)(2,1)S(1)}, bf16[128,128]{1,0:T(8,128)(2,1)}, u32[]{:S(2)}) copy-start(bf16[128,128]{1,0:T(8,128)(2,1)} %constant.38.clone.refs_6_.refs_4_) | copy-start | bytes 98308
  12.9 36.4 %copy-start.12 = (bf16[128,128]{1,0:T(8,128)(2,1)S(1)}, bf16[128,128]{1,0:T(8,128)(2,1)}, u32[]{:S(2)}) copy-start(bf16[128,128]{1,0:T(8,128)(2,1)} %constant.37.clone.refs_5_.refs_3_) | copy-start | bytes 98308
  13.0 36.4 %copy-start.13 = (f32[512]{0:T(512)S(1)}, f32[512]{0:T(512)}, u32[]{:S(2)}) copy-start(f32[512]{0:T(512)} %constant.39.clone.refs_1_) | copy-start | bytes 6148
  49.4 0.7 copy-start.14
  53.6 24.4 %copy-start.3 = (bf16[128,256]{1,0:T(8,128)(2,1)S(1)}, bf16[128,256]{1,0:T(8,128)(2,1)}, u32[]{:S(2)}) copy-start(bf16[128,256]{1,0:T(8,128)(2,1)} %constant.42.clone.pick) | copy-start | bytes 196612
  53.6 24.4 %copy-start.5 = (bf16[128,128]{1,0:T(8,128)(2,1)S(1)}, bf16[128,128]{1,0:T(8,128)(2,1)}, u32[]{:S(2)}) copy-start(bf16[128,128]{1,0:T(8,128)(2,1)} %constant.41.clone.ql) | copy-start | bytes 98308
  53.6 24.4 %copy-start.6 = (bf16[128,128]{1,0:T(8,128)(2,1)S(1)}, bf16[128,128]{1,0:T(8,128)(2,1)}, u32[]{:S(2)}) copy-start(bf16[128,128]{1,0:T(8,128)(2,1)} %constant.40.clone.qh) | copy-start | bytes 98308
  145.3 27.6 %copy-start.7 = (f32[512,128]{1,0:T(8,128)}, f32[512,128]{1,0:T(8,128)S(1)}, u32[]{:S(2)}) copy-start(f32[512,128]{1,0:T(8,128)S(1)} %get-tuple-element.61.hat_sum) | copy-start | bytes 786436
  175.9 0.7 copy-start.4
  176.6 24.5 %all-to-all-start.5 = ((f32[256,1,384]{2,1,0:T(1,128)}), f32[256,1,384]{2,1,0:T(1,128)S(1)}, u32[]{:S(2)}, u32[]{:S(2)}) async-start(f32[256,1,384]{2,1,0:T(1,128)} %bitcast.23), calls=%async_computation.5 | async-start | bytes 786432 | tf_op jit(solution)/shard_map/all_to_all | solution.py:440
  184.6 16.6 %copy-start.8 = (f32[512,128]{1,0:T(8,128)S(1)}, f32[512,128]{1,0:T(8,128)}, u32[]{:S(2)}) copy-start(f32[512,128]{1,0:T(8,128)} %copy-done.7) | copy-start | bytes 786436

commit v7 on v6

--- a/solution.py
+++ b/solution.py
@@ -134,13 +134,13 @@
 
 
 def fill_slab(u, rows, outer, inner, edge, ch, cl):
-    cosine = (ch[...], cl[...])
-    value = dot3(halves(outer), cosine, TN)
-    u[:rows, :] = value[:rows, :]
-    u[3 * rows : 4 * rows, :] = value[rows:, :]
-    u[rows : 3 * rows, :] = dot3(halves(inner), cosine, TN)
+    parts = [inner, outer] + ([] if edge is None else [edge])
+    value = dot3(halves(jnp.concatenate(parts, axis=1)), (ch[...], cl[...]), TN)
+    u[rows : 3 * rows, :] = value[: 2 * rows, :]
+    u[:rows, :] = value[2 * rows : 3 * rows, :]
+    u[3 * rows : 4 * rows, :] = value[3 * rows : 4 * rows, :]
     if edge is not None:
-        u[4 * rows : 5 * rows, :] = dot3(halves(edge), cosine, TN)[:rows, :]
+        u[4 * rows : 5 * rows, :] = value[4 * rows : 5 * rows, :]
 
 
 def fill_plane(u, steps, rows, screen, residual_sum):
@@ -252,18 +252,36 @@
     )(*map(stay, (density, flux_x, flux_y)))
 
 
-def prox_body(d, fx, fy, across, along, nd, nx, ny, own_d, own_x, own_y, scale, sems):
+def prox_body(
+    screen, place, d, fx, fy, across, along, around, nd, nx, ny, own_d, own_x, own_y, scale, inverse, table, sems, small,
+):
     steps = d.shape[0]
+    width = across.shape[1]
+    lanes = along.shape[1]
+    length = around.shape[1]
     moves = ((d, own_d), (fx, own_x), (fy, own_y))
+    tables = [
+        pltpu.make_async_copy(ref, table.at[pl.ds(k, 1), pl.ds(0, ref.shape[1])], small.at[k])
+        for k, ref in enumerate((across, along, around))
+    ]
 
     def copy(k, t):
         return pltpu.make_async_copy(moves[k][0].at[t], moves[k][1].at[t], sems.at[k, t])
 
+    for move in tables:
+        move.start()
     for t in range(steps):
         for k in range(3):
             copy(k, t).start()
-
-    scale[...] = 1.0 / (jnp.broadcast_to(across[...], scale.shape[::-1]).T + along[...])
+    for move in tables:
+        move.wait()
+    values = table[0:1, :]
+    scale[...] = 1.0 / (jnp.broadcast_to(values, (lanes, width)).T + table[1:2, :lanes])
+    turned = jnp.broadcast_to(table[2:3, :length], (width, length)).T
+    lane = lax.broadcasted_iota(jnp.int32, values.shape, 1)
+    for mode in range(2):
+        own = jnp.sum(jnp.where(lane == place[1] + mode * (width // 2), values, 0.0), axis=1, keepdims=True)
+        inverse[mode * length : (mode + 1) * length, :] = 1.0 / (turned + (values + (own + screen)))
 
     def wait(t):
         for k in range(3):
@@ -308,16 +326,11 @@
         copy.wait()
 
 
-def solve_body(slabs, places, steps, screen, with_sum, *refs):
+def solve_body(slabs, places, steps, with_sum, *refs):
     if with_sum:
         z, ch, cl, wh, wl, inverse, so_far, out, total, field = refs
     else:
-        place, values, z, ch, cl, wh, wl, across, around, out, total, inverse, field = refs
-        turned = jnp.broadcast_to(around[...], across.shape[1:] + around.shape[1:]).T
-        for mode in range(2):
-            inverse[mode * slabs * steps : (mode + 1) * slabs * steps, :] = 1.0 / (
-                turned + across[...] + (values[place[1] + mode] + screen)
-            )
+        z, ch, cl, wh, wl, inverse, out, total, field = refs
     length = slabs * steps
     pairs = steps // 2
     lanes = z.shape[1]
@@ -404,8 +417,7 @@
     wh, wl = (jnp.asarray(m) for m in np_halves(basis))
     spectrum = neumann_spectrum(width)
     place = lax.axis_index("space")
-    first = 2 * (lax.axis_index("tm") * places + place)
-    values = jnp.asarray(spectrum)
+    first = lax.axis_index("tm") * places + place
     count = np.arange(rows)
     gaps = rows - 1
     sine = np.sqrt(2.0 / gaps) * np.sin(np.pi * (np.outer(count, count) % (2 * gaps)) / gaps)
@@ -445,10 +457,11 @@
     block = (BLOCK, width)
     square = (2 * length, width)
     hat_shape = (width, lanes)
-    new_d, new_x, new_y, density, flux_x, flux_y, scale = call(
-        prox_body, [field] * 6 + [hat_shape], scratch=[pltpu.SemaphoreType.DMA((3, steps))], far=3, n_in=2,
-        cost=(density.size * 200, 6 * nbytes), name="prox",
-    )(*map(stay, (density, flux_x, flux_y)), across, along)
+    new_d, new_x, new_y, density, flux_x, flux_y, scale, inverse = call(
+        functools.partial(prox_body, screen), [field] * 6 + [hat_shape, square],
+        scratch=[pltpu.VMEM((8, width), f32), pltpu.SemaphoreType.DMA((3, steps)), pltpu.SemaphoreType.DMA((3,))],
+        scalars=1, far=6, cost=(density.size * 200, 6 * nbytes), name="prox",
+    )(place, *map(stay, (density, flux_x, flux_y, across, along, around)))
     modes, edge, kept, hat = call(
         functools.partial(forward_body, places - 1), [packed(items), edge_shape, block, hat_shape],
         scratch=split, scalars=1, n_in=10, cost=(mega, 8 * nbytes), name="forward",
@@ -456,16 +469,11 @@
     density, flux_x, flux_y = new_d, new_x, new_y
     for iteration in range(ITERS):
         modes = exchange(modes)
-        body = functools.partial(solve_body, slabs, places, steps, screen, iteration > 0)
-        settings = dict(scratch=[pltpu.VMEM(square, f32)], n_in=7, cost=(3 * mega, 6 * nbytes), name="solve")
-        shapes = [packed(3), square]
-        matrices = (ch, cl, wh, wl)
-        if iteration:
-            modes, total = call(body, shapes, **settings)(modes, *matrices, inverse, total)
-        else:
-            modes, total, inverse = call(body, shapes + [square], scalars=2, **settings)(
-                place, values, modes, *matrices, across, around
-            )
+        carried = (total,) if iteration else ()
+        modes, total = call(
+            functools.partial(solve_body, slabs, places, steps, iteration > 0), [packed(3), square],
+            scratch=[pltpu.VMEM(square, f32)], n_in=6 + len(carried), cost=(3 * mega, 6 * nbytes), name="solve",
+        )(modes, ch, cl, wh, wl, inverse, *carried)
         modes = exchange(modes)
         if iteration + 1 == ITERS:
             break

time: 204 us -> 204 us (level)
    unnamed x33 -> x25, local copies, waits for them, and re-layouts: 4.42 us -> 3.17 us
where the time goes in v7:
time: 204 us; the launch traced here: 203 us
  blocking collectives  140 us (69%)
  Pallas kernels  32.2 us (16%)
  waiting for transfers between devices  15.8 us (8%)
  starting transfers between devices  10.9 us (5%)
  local copies, waits for them, and re-layouts  3.17 us (2%)
    all_to_all x5, blocking collectives, exchange(): value = lax.all_to_all(value, BOTH, split_axis=0, concat_axis=0, tiled=True)  140 us
    all_to_all x1, waiting for transfers between devices, exchange(): value = lax.all_to_all(value, BOTH, split_axis=0, concat_axis=0, tiled=True)  15.8 us
    pallas_call x2, Pallas kernels, local(): call(functools.partial(middle_body, places - 1, screen), [field] * 3 + [p...  12.9 us
    pallas_call x3, Pallas kernels, local(): call(functools.partial(solve_body, slabs, places, steps, iteration > 0),...  8.83 us
    all_to_all x1, starting transfers between devices, exchange(): value = lax.all_to_all(value, BOTH, split_axis=0, concat_axis=0, tiled=True)  6.36 us
    pallas_call x1, Pallas kernels, local(): call(functools.partial(prox_body, screen), [field] * 6 + [hat_shape, squa...  5 us
    ppermute x1, starting transfers between devices, local(): lax.ppermute(last_rows(density, flux_x, flux_y), 'space', [(i, i + 1) for...  4.57 us
  transfers between devices with their start and end apart: 2, of which 1 were waited for; matrix products, arithmetic and copies ran while one was open for 1% of the time, Pallas kernels for 2%

profile of v7, /device:TPU:1, one launch (start us, length us, event | category | flops | bytes accessed | tf_op | source)
XLA Modules:
  0.0 203.4 jit_solution(1629292338892124316)
XLA Ops:
  0.6 0.9 edges.1
  1.5 4.6 %collective-permute-start = (f32[3,4,512]{2,1,0:T(4,128)S(1)}, f32[3,4,512]{2,1,0:T(4,128)S(1)}, u32[]{:S(2)}, u32[]{:S(2)}) collective-permute-start(f32[3,4,512]{2,1,0:T(4,128)S(1)} %edges.1), channel_id=1, source_target_pairs={{0,1},{1,2},{2,3},{3,4},{4,5},{5,6},{6,7},{8,9},{9,10},{10,11},{11... | collective-permute-start | bytes 73736 | tf_op jit(solution)/shard_map/ppermute | solution.py:455
  6.1 0.1 pad_add_fusion.place
  6.2 0.0 copy-start
  6.2 0.0 copy-start.1
  6.2 0.0 copy-start.2
  6.2 5.0 %prox.1 = (f32[4,64,512]{2,1,0:T(8,128)S(1)}, f32[4,64,512]{2,1,0:T(8,128)S(1)}, f32[4,64,512]{2,1,0:T(8,128)S(1)}, f32[4,64,512]{2,1,0:T(8,128)S(1)}, f32[4,64,...) custom-call(s32[2]{0:T(128)S(1)} %pad_add_fusion.place, ...), custom_call_target="tpu_custom_call" | custom-call | flops 26214400 | bytes 3145728 | tf_op jit(solution)/shard_map/prox/pallas_call | solution.py:460
  11.2 0.0 collective-permute-done.edge
  11.2 0.0 copy-done
  11.2 0.0 copy-done.1
  11.3 0.0 copy-done.2
  11.3 1.9 forward.1
  13.1 0.0 copy-start.9
  13.2 0.0 copy-start.10
  13.2 36.4 %all_to_all.30 = f32[256,1,640]{2,1,0:T(1,128)S(1)} all-to-all(f32[256,1,640]{2,1,0:T(1,128)S(1)} %bitcast.19), channel_id=1, replica_groups=mesh['tm'=32,'space'=8] {'tm','space'}, dimensions={0} | all-to-all | bytes 1310720 | tf_op jit(solution)/shard_map/all_to_all | solution.py:452
  49.6 0.0 copy-done.9
  49.6 0.0 copy-done.10
  49.6 2.9 %solve.3 = (f32[768,128]{1,0:T(8,128)S(1)}, f32[256,512]{1,0:T(8,128)S(1)}) custom-call(f32[1280,128]{1,0:T(8,128)S(1)} %bitcast.22, bf16[512,512]{1,0:T(8,128)(2,1)S(1)} %copy-done.1, bf16[512,512]{1,0:T(8,128)(2,1)S(1)} %copy-done, bf16[128,128]{1,0:T(8,128)(2,1)S(1)} %copy-done.10, bf16[128,128]{1,0:T(8,128)(2,1)S(1)} %copy-done.9, ...), custom_call_target="tpu_custom_call" | custom-call | flops 1207959552 | bytes 3145728 | tf_op jit(solution)/shard_map/solve/pallas_call | solution.py:473
  52.5 0.0 copy-start.3
  52.5 0.0 copy-start.5
  52.5 0.0 copy-start.6
  52.6 24.3 %all_to_all.31 = f32[256,1,384]{2,1,0:T(1,128)S(1)} all-to-all(f32[256,1,384]{2,1,0:T(1,128)S(1)} %bitcast.25), channel_id=1, replica_groups=mesh['tm'=32,'space'=8] {'tm','space'}, dimensions={0} | all-to-all | bytes 786432 | tf_op jit(solution)/shard_map/all_to_all | solution.py:452
  76.9 0.0 copy-done.3
  76.9 0.0 copy-done.5
  76.9 0.0 copy-done.6
  76.9 6.5 %middle.2 = (f32[4,64,512]{2,1,0:T(8,128)S(1)}, f32[4,64,512]{2,1,0:T(8,128)S(1)}, f32[4,64,512]{2,1,0:T(8,128)S(1)}, f32[1280,128]{1,0:T(8,128)S(1)}, f32[3,4,5...) custom-call(s32[2]{0:T(128)S(1)} %pad_add_fusion.place, f32[768,128]{1,0:T(8,128)S(1)} %bitcast.15, ...), custom_call_target="tpu_custom_call" | custom-call | flops 805306368 | bytes 5242880 | tf_op jit(solution)/shard_map/middle/pallas_call | solution.py:480
  83.4 27.6 %all_to_all.32 = f32[256,1,640]{2,1,0:T(1,128)S(1)} all-to-all(f32[256,1,640]{2,1,0:T(1,128)S(1)} %bitcast.18), channel_id=1, replica_groups=mesh['tm'=32,'space'=8] {'tm','space'}, dimensions={0} | all-to-all | bytes 1310720 | tf_op jit(solution)/shard_map/all_to_all | solution.py:452
  111.0 2.9 %solve.4 = (f32[768,128]{1,0:T(8,128)S(1)}, f32[256,512]{1,0:T(8,128)S(1)}) custom-call(f32[1280,128]{1,0:T(8,128)S(1)} %bitcast.21, bf16[512,512]{1,0:T(8,128)(2,1)S(1)} %copy-done.1, bf16[512,512]{1,0:T(8,128)(2,1)S(1)} %copy-done, bf16[128,128]{1,0:T(8,128)(2,1)S(1)} %copy-done.10, bf16[128,128]{1,0:T(8,128)(2,1)S(1)} %copy-done.9, ...), custom_call_target="tpu_custom_call" | custom-call | flops 1207959552 | bytes 3145728 | tf_op jit(solution)/shard_map/solve/pallas_call | solution.py:473
  113.9 24.3 %all_to_all.33 = f32[256,1,384]{2,1,0:T(1,128)S(1)} all-to-all(f32[256,1,384]{2,1,0:T(1,128)S(1)} %bitcast.24), channel_id=1, replica_groups=mesh['tm'=32,'space'=8] {'tm','space'}, dimensions={0} | all-to-all | bytes 786432 | tf_op jit(solution)/shard_map/all_to_all | solution.py:452
  138.3 6.5 %middle.3 = (f32[4,64,512]{2,1,0:T(8,128)S(1)}, f32[4,64,512]{2,1,0:T(8,128)S(1)}, f32[4,64,512]{2,1,0:T(8,128)S(1)}, f32[1280,128]{1,0:T(8,128)S(1)}, f32[3,4,5...) custom-call(s32[2]{0:T(128)S(1)} %pad_add_fusion.place, f32[768,128]{1,0:T(8,128)S(1)} %bitcast.16, ...), custom_call_target="tpu_custom_call" | custom-call | flops 805306368 | bytes 5242880 | tf_op jit(solution)/shard_map/middle/pallas_call | solution.py:480
  144.8 0.0 copy-start.7
  144.8 27.6 %all_to_all.34 = f32[256,1,640]{2,1,0:T(1,128)S(1)} all-to-all(f32[256,1,640]{2,1,0:T(1,128)S(1)} %bitcast.17), channel_id=1, replica_groups=mesh['tm'=32,'space'=8] {'tm','space'}, dimensions={0} | all-to-all | bytes 1310720 | tf_op jit(solution)/shard_map/all_to_all | solution.py:452
  172.4 0.0 copy-done.7
  172.4 2.9 %solve.5 = (f32[768,128]{1,0:T(8,128)S(1)}, f32[256,512]{1,0:T(8,128)}) custom-call(f32[1280,128]{1,0:T(8,128)S(1)} %bitcast.20, bf16[512,512]{1,0:T(8,128)(2,1)S(1)} %copy-done.1, bf16[512,512]{1,0:T(8,128)(2,1)S(1)} %copy-done, bf16[128,128]{1,0:T(8,128)(2,1)S(1)} %copy-done.10, bf16[128,128]{1,0:T(8,128)(2,1)S(1)} %copy-done.9, ...), custom_call_target="tpu_custom_call" | custom-call | flops 1207959552 | bytes 3145728 | tf_op jit(solution)/shard_map/solve/pallas_call | solution.py:473
  175.3 0.0 copy-start.4
  175.3 0.7 copy-done.4
  176.1 6.4 %all-to-all-start.5 = ((f32[256,1,384]{2,1,0:T(1,128)}), f32[256,1,384]{2,1,0:T(1,128)S(1)}, u32[]{:S(2)}, u32[]{:S(2)}) async-start(f32[256,1,384]{2,1,0:T(1,128)} %bitcast.23), calls=%async_computation.5 | async-start | bytes 786432 | tf_op jit(solution)/shard_map/all_to_all | solution.py:452
  182.4 0.8 copy.24
  183.2 0.8 copy.25
  184.0 0.0 copy-start.8
  184.0 0.8 copy.26
  184.8 15.8 %all-to-all-done.5 = f32[256,1,384]{2,1,0:T(1,128)S(1)} async-done(((f32[256,1,384]{2,1,0:T(1,128)}), f32[256,1,384]{2,1,0:T(1,128)S(1)}, u32[]{:S(2)}, u32[]{:S(2)}) %all-to-all-start.5) | async-done | bytes 393248 | tf_op jit(solution)/shard_map/all_to_all | solution.py:452
  200.6 0.0 copy-done.8
  200.6 2.7 %last.1 = f32[4,64,512]{2,1,0:T(8,128)} custom-call(f32[768,128]{1,0:T(8,128)S(1)} %bitcast.14, f32[512,128]{1,0:T(8,128)S(1)} %copy-done.8, bf16[512,512]{1,0:T(8,128)(2,1)S(1)} %copy-done.1, bf16[512,512]{1,0:T(8,128)(2,1)S(1)} %copy-done, bf16[128,128]{1,0:T(8,128)(2,1)S(1)} %copy-done.6, bf16[128,128]{1,0:T(8,128)(2,1)S(1)} %copy-done.5, ...), custom_call_target="tpu_custom_call" | custom-call | flops 402653184 | bytes 1572864 | tf_op jit(solution)/shard_map/last/pallas_call | solution.py:485
Async XLA Ops:
  1.5 9.7 %collective-permute-start = (f32[3,4,512]{2,1,0:T(4,128)S(1)}, f32[3,4,512]{2,1,0:T(4,128)S(1)}, u32[]{:S(2)}, u32[]{:S(2)}) collective-permute-start(f32[3,4,512]{2,1,0:T(4,128)S(1)} %edges.1), channel_id=1, source_target_pairs={{0,1},{1,2},{2,3},{3,4},{4,5},{5,6},{6,7},{8,9},{9,10},{10,11},{11... | collective-permute-start | bytes 73736 | tf_op jit(solution)/shard_map/ppermute | solution.py:455
  6.2 5.0 %copy-start = (bf16[512,512]{1,0:T(8,128)(2,1)S(1)}, bf16[512,512]{1,0:T(8,128)(2,1)}, u32[]{:S(2)}) copy-start(bf16[512,512]{1,0:T(8,128)(2,1)} %constant.32.clone.cl.refs_2_) | copy-start | bytes 1572868
  6.2 5.0 %copy-start.1 = (bf16[512,512]{1,0:T(8,128)(2,1)S(1)}, bf16[512,512]{1,0:T(8,128)(2,1)}, u32[]{:S(2)}) copy-start(bf16[512,512]{1,0:T(8,128)(2,1)} %constant.31.clone.ch.refs_1_) | copy-start | bytes 1572868
  6.2 5.0 %copy-start.2 = (f32[4,64,512]{2,1,0:T(8,128)S(1)}, f32[4,64,512]{2,1,0:T(8,128)}, u32[]{:S(2)}) copy-start(f32[4,64,512]{2,1,0:T(8,128)} %src.5) | copy-start | bytes 1572868
  13.1 36.4 %copy-start.9 = (bf16[128,128]{1,0:T(8,128)(2,1)S(1)}, bf16[128,128]{1,0:T(8,128)(2,1)}, u32[]{:S(2)}) copy-start(bf16[128,128]{1,0:T(8,128)(2,1)} %constant.34.clone.refs_4_) | copy-start | bytes 98308
  13.2 36.4 %copy-start.10 = (bf16[128,128]{1,0:T(8,128)(2,1)S(1)}, bf16[128,128]{1,0:T(8,128)(2,1)}, u32[]{:S(2)}) copy-start(bf16[128,128]{1,0:T(8,128)(2,1)} %constant.33.clone.refs_3_) | copy-start | bytes 98308
  52.5 24.4 %copy-start.3 = (bf16[128,256]{1,0:T(8,128)(2,1)S(1)}, bf16[128,256]{1,0:T(8,128)(2,1)}, u32[]{:S(2)}) copy-start(bf16[128,256]{1,0:T(8,128)(2,1)} %constant.37.clone.pick) | copy-start | bytes 196612
  52.5 24.4 %copy-start.5 = (bf16[128,128]{1,0:T(8,128)(2,1)S(1)}, bf16[128,128]{1,0:T(8,128)(2,1)}, u32[]{:S(2)}) copy-start(bf16[128,128]{1,0:T(8,128)(2,1)} %constant.36.clone.ql) | copy-start | bytes 98308
  52.5 24.4 %copy-start.6 = (bf16[128,128]{1,0:T(8,128)(2,1)S(1)}, bf16[128,128]{1,0:T(8,128)(2,1)}, u32[]{:S(2)}) copy-start(bf16[128,128]{1,0:T(8,128)(2,1)} %constant.35.clone.qh) | copy-start | bytes 98308
  144.8 27.6 %copy-start.7 = (f32[512,128]{1,0:T(8,128)}, f32[512,128]{1,0:T(8,128)S(1)}, u32[]{:S(2)}) copy-start(f32[512,128]{1,0:T(8,128)S(1)} %get-tuple-element.61.hat_sum) | copy-start | bytes 786436
  175.3 0.7 copy-start.4
  176.1 24.5 %all-to-all-start.5 = ((f32[256,1,384]{2,1,0:T(1,128)}), f32[256,1,384]{2,1,0:T(1,128)S(1)}, u32[]{:S(2)}, u32[]{:S(2)}) async-start(f32[256,1,384]{2,1,0:T(1,128)} %bitcast.23), calls=%async_computation.5 | async-start | bytes 786432 | tf_op jit(solution)/shard_map/all_to_all | solution.py:452
  184.0 16.6 %copy-start.8 = (f32[512,128]{1,0:T(8,128)S(1)}, f32[512,128]{1,0:T(8,128)}, u32[]{:S(2)}) copy-start(f32[512,128]{1,0:T(8,128)} %copy-done.7) | copy-start | bytes 786436

commit v8 on v7

--- a/solution.py
+++ b/solution.py
@@ -69,15 +69,15 @@
     return high, (matrix - high.astype(np.float32)).astype(bf16)
 
 
-def call(body, outs, scratch=(), scalars=0, far=0, n_in=0, far_out=False, cost=None, **kw):
+def call(body, outs, scratch=(), scalars=0, far=0, n_in=0, far_out=0, cost=None, **kw):
     vmem = pl.BlockSpec(memory_space=pltpu.VMEM)
     smem = pl.BlockSpec(memory_space=pltpu.SMEM)
     hbm = pl.BlockSpec(memory_space=pltpu.HBM)
     return pl.pallas_call(
         body,
-        out_shape=[jax.ShapeDtypeStruct(s, f32) if far_out else pltpu.VMEM(s, f32) for s in outs],
+        out_shape=[jax.ShapeDtypeStruct(s, f32) if k < far_out else pltpu.VMEM(s, f32) for k, s in enumerate(outs)],
         in_specs=[smem] * scalars + [hbm] * far + [vmem] * n_in,
-        out_specs=[hbm if far_out else vmem] * len(outs),
+        out_specs=[hbm] * far_out + [vmem] * (len(outs) - far_out),
         scratch_shapes=list(scratch),
         cost_estimate=pl.CostEstimate(flops=int(cost[0]), bytes_accessed=int(cost[1]), transcendentals=0),
         compiler_params=pltpu.CompilerParams(vmem_limit_bytes=GRANT),
@@ -101,7 +101,7 @@
     return root, factor * along_x, factor * along_y
 
 
-def prox_cells(source, result, wait=None):
+def prox_cells(source, result, wait=None, ready=None):
     steps, rows, width = result[0].shape
     chunk = 16
     per = rows // chunk
@@ -114,6 +114,8 @@
         out = newton(*[ref[t, span, :] for ref in source])
         for ref, value in zip(result, out):
             ref[t, span, :] = value
+        if ready is not None:
+            pl.when(index % per == per - 1)(lambda: ready(t))
         return carry
 
     lax.fori_loop(0, steps * per, step, 0)
@@ -133,14 +135,16 @@
     return outer, inner, edge
 
 
-def fill_slab(u, rows, outer, inner, edge, ch, cl):
-    parts = [inner, outer] + ([] if edge is None else [edge])
-    value = dot3(halves(jnp.concatenate(parts, axis=1)), (ch[...], cl[...]), TN)
-    u[rows : 3 * rows, :] = value[: 2 * rows, :]
-    u[:rows, :] = value[2 * rows : 3 * rows, :]
-    u[3 * rows : 4 * rows, :] = value[3 * rows : 4 * rows, :]
+def fill_slab(u, rows, outer, inner, edge, ch, cl, ready=lambda *steps: None):
+    cosine = (ch[...], cl[...])
+    value = dot3(halves(outer), cosine, TN)
+    u[:rows, :] = value[:rows, :]
+    u[3 * rows : 4 * rows, :] = value[rows:, :]
+    ready(0, 3)
+    u[rows : 3 * rows, :] = dot3(halves(inner), cosine, TN)
+    ready(1, 2)
     if edge is not None:
-        u[4 * rows : 5 * rows, :] = value[4 * rows : 5 * rows, :]
+        u[4 * rows : 5 * rows, :] = dot3(halves(edge), cosine, TN)[:rows, :]
 
 
 def fill_plane(u, steps, rows, screen, residual_sum):
@@ -299,8 +303,9 @@
 
 def middle_body(
     last_place, screen, place, y, d, fx, fy, src, edge, kept_sum, hat_sum, ch, cl, qh, ql, pick, scale,
-    nd, nx, ny, out, new_edge, kept, hat, u, rh, rl,
+    out_d, out_x, out_y, out, new_edge, kept, hat, u, rh, rl, *leave,
 ):
+    nd, nx, ny = leave[:3] if leave else (out_d, out_x, out_y)
     steps, rows, _ = d.shape
     fill_slab(u, rows, *send_values(y, hat_sum, qh, ql, pick, scale), ch, cl)
     at = steps * rows
@@ -309,21 +314,38 @@
     fresh = newton(*dual_step(d, fx, fy, edge, u, nd, nx, ny))
     for k in range(3):
         new_edge[k] = fresh[k]
-    prox_cells((nd, nx, ny), (nd, nx, ny))
+
+    def move(k, t):
+        return pltpu.make_async_copy((nd, nx, ny)[k].at[t], (out_d, out_x, out_y)[k].at[t], leave[3].at[k, t])
+
+    def ready(t):
+        for k in range(3):
+            move(k, t).start()
+
+    prox_cells((nd, nx, ny), (nd, nx, ny), ready=ready if leave else None)
     residual_modes(place[0], last_place, d, fx, fy, nd, nx, ny, src, edge[1], fresh[1], ch, cl, out, kept, hat, rh, rl)
     kept[...] = kept[...] + kept_sum[...]
     hat[...] = hat[...] + hat_sum[...]
+    if leave:
+        for t in range(steps):
+            for k in range(3):
+                move(k, t).wait()
 
 
 def last_body(y, hat_sum, ch, cl, qh, ql, pick, scale, u, flat, sems):
     steps, rows, _ = u.shape
     outer, inner, _ = send_values(y, hat_sum, qh, ql, pick, scale)
-    fill_slab(flat, rows, outer, inner, None, ch, cl)
-    copies = [pltpu.make_async_copy(flat.at[pl.ds(t * rows, rows), :], u.at[t], sems.at[t]) for t in range(steps)]
-    for copy in copies:
-        copy.start()
-    for copy in copies:
-        copy.wait()
+
+    def move(t):
+        return pltpu.make_async_copy(flat.at[pl.ds(t * rows, rows), :], u.at[t], sems.at[t])
+
+    def ready(*which):
+        for t in which:
+            move(t).start()
+
+    fill_slab(flat, rows, outer, inner, None, ch, cl, ready)
+    for t in range(steps):
+        move(t).wait()
 
 
 def solve_body(slabs, places, steps, with_sum, *refs):
@@ -477,14 +499,17 @@
         modes = exchange(modes)
         if iteration + 1 == ITERS:
             break
+        leave = []
+        if iteration + 2 == ITERS:
+            leave = [pltpu.VMEM(field, f32)] * 3 + [pltpu.SemaphoreType.DMA((3, steps))]
         density, flux_x, flux_y, modes, edge, kept, hat = call(
             functools.partial(middle_body, places - 1, screen), [field] * 3 + [packed(items), edge_shape, block, hat_shape],
-            scratch=[pltpu.VMEM(((steps + 1) * rows + BLOCK, width), f32)] + split,
-            scalars=1, n_in=14, cost=(2 * mega, 10 * nbytes), name="middle",
+            scratch=[pltpu.VMEM(((steps + 1) * rows + BLOCK, width), f32)] + split + leave,
+            scalars=1, n_in=14, far_out=3 if leave else 0, cost=(2 * mega, 10 * nbytes), name="middle",
         )(place, modes, density, flux_x, flux_y, source, edge, kept, hat, ch, cl, *inner, scale)
     (potential,) = call(
         last_body, [field], scratch=[pltpu.VMEM((steps * rows, width), f32), pltpu.SemaphoreType.DMA((steps,))],
-        n_in=8, far_out=True, cost=(mega, 3 * nbytes), name="last",
+        n_in=8, far_out=1, cost=(mega, 3 * nbytes), name="last",
     )(modes, hat, ch, cl, *inner, scale)
     return density, flux_x, flux_y, potential
 

time: 204 us -> 203 us (level)
  blocking collectives: 140 us -> 165 us
  waiting for transfers between devices: 15.8 us -> 0.01 us
  starting transfers between devices: 10.9 us -> 4.57 us
  local copies, waits for them, and re-layouts: 3.17 us -> 0.05 us
    all_to_all x5 -> x6, blocking collectives: 140 us -> 165 us  [exchange(): value = lax.all_to_all(value, BOTH, split_axis=0, concat_axis=0, tiled=True)]
    all_to_all x1 -> x0, waiting for transfers between devices: 15.8 us -> none  [exchange(): value = lax.all_to_all(value, BOTH, split_axis=0, concat_axis=0, tiled=True)]
    all_to_all x1 -> x0, starting transfers between devices: 6.36 us -> none  [exchange(): value = lax.all_to_all(value, BOTH, split_axis=0, concat_axis=0, tiled=True)]
    unnamed x25 -> x16, local copies, waits for them, and re-layouts: 3.17 us -> 0.05 us
  transfers between devices with their start and end apart: 2 -> 1, of which waited for: 1 -> 0; matrix products, arithmetic and copies ran while one was open for 1% -> 0% of each run, Pallas kernels for 2% -> 2%
where the time goes in v8:
time: 203 us
  blocking collectives  165 us (81%)
  Pallas kernels  32.5 us (16%)
  starting transfers between devices  4.57 us (2%)
    all_to_all x6, blocking collectives, exchange(): value = lax.all_to_all(value, BOTH, split_axis=0, concat_axis=0, tiled=True)  165 us
    pallas_call x2, Pallas kernels, local(): call(functools.partial(middle_body, places - 1, screen), [field] * 3 + [p...  13.5 us
    pallas_call x3, Pallas kernels, local(): call(functools.partial(solve_body, slabs, places, steps, iteration > 0),...  8.86 us
    pallas_call x1, Pallas kernels, local(): call(functools.partial(prox_body, screen), [field] * 6 + [hat_shape, squa...  5 us
    ppermute x1, starting transfers between devices, local(): lax.ppermute(last_rows(density, flux_x, flux_y), 'space', [(i, i + 1) for...  4.57 us
  transfers between devices with their start and end apart: 1, of which 0 were waited for; matrix products, arithmetic and copies ran while one was open for 0% of the time, Pallas kernels for 2%

profile of v8, /device:TPU:1, one launch (start us, length us, event | category | flops | bytes accessed | tf_op | source)
XLA Modules:
  0.0 202.7 jit_solution(7411051903362841933)
XLA Ops:
  0.6 0.9 edges.1
  1.5 4.6 %collective-permute-start = (f32[3,4,512]{2,1,0:T(4,128)S(1)}, f32[3,4,512]{2,1,0:T(4,128)S(1)}, u32[]{:S(2)}, u32[]{:S(2)}) collective-permute-start(f32[3,4,512]{2,1,0:T(4,128)S(1)} %edges.1), channel_id=1, source_target_pairs={{0,1},{1,2},{2,3},{3,4},{4,5},{5,6},{6,7},{8,9},{9,10},{10,11},{11... | collective-permute-start | bytes 73736 | tf_op jit(solution)/shard_map/ppermute | solution.py:477
  6.1 0.1 pad_add_fusion.place
  6.2 0.0 copy-start
  6.2 0.0 copy-start.1
  6.2 0.0 copy-start.2
  6.2 5.0 %prox.1 = (f32[4,64,512]{2,1,0:T(8,128)S(1)}, f32[4,64,512]{2,1,0:T(8,128)S(1)}, f32[4,64,512]{2,1,0:T(8,128)S(1)}, f32[4,64,512]{2,1,0:T(8,128)S(1)}, f32[4,64,...) custom-call(s32[2]{0:T(128)S(1)} %pad_add_fusion.place, ...), custom_call_target="tpu_custom_call" | custom-call | flops 26214400 | bytes 3145728 | tf_op jit(solution)/shard_map/prox/pallas_call | solution.py:482
  11.2 0.0 collective-permute-done.edge
  11.2 0.0 copy-done
  11.2 0.0 copy-done.1
  11.3 0.0 copy-done.2
  11.3 2.0 forward.1
  13.3 0.0 copy-start.6
  13.3 0.0 copy-start.7
  13.3 36.4 %all_to_all.30 = f32[256,1,640]{2,1,0:T(1,128)S(1)} all-to-all(f32[256,1,640]{2,1,0:T(1,128)S(1)} %bitcast.19), channel_id=1, replica_groups=mesh['tm'=32,'space'=8] {'tm','space'}, dimensions={0} | all-to-all | bytes 1310720 | tf_op jit(solution)/shard_map/all_to_all | solution.py:474
  49.7 0.0 copy-done.6
  49.7 0.0 copy-done.7
  49.7 2.9 %solve.3 = (f32[768,128]{1,0:T(8,128)S(1)}, f32[256,512]{1,0:T(8,128)S(1)}) custom-call(f32[1280,128]{1,0:T(8,128)S(1)} %bitcast.22, bf16[512,512]{1,0:T(8,128)(2,1)S(1)} %copy-done.1, bf16[512,512]{1,0:T(8,128)(2,1)S(1)} %copy-done, bf16[128,128]{1,0:T(8,128)(2,1)S(1)} %copy-done.7, bf16[128,128]{1,0:T(8,128)(2,1)S(1)} %copy-done.6, ...), custom_call_target="tpu_custom_call" | custom-call | flops 1207959552 | bytes 3145728 | tf_op jit(solution)/shard_map/solve/pallas_call | solution.py:495
  52.6 0.0 copy-start.3
  52.6 0.0 copy-start.4
  52.6 0.0 copy-start.5
  52.7 24.4 %all_to_all.31 = f32[256,1,384]{2,1,0:T(1,128)S(1)} all-to-all(f32[256,1,384]{2,1,0:T(1,128)S(1)} %bitcast.25), channel_id=1, replica_groups=mesh['tm'=32,'space'=8] {'tm','space'}, dimensions={0} | all-to-all | bytes 786432 | tf_op jit(solution)/shard_map/all_to_all | solution.py:474
  77.0 0.0 copy-done.3
  77.0 0.0 copy-done.4
  77.0 0.0 copy-done.5
  77.0 6.4 %middle.2 = (f32[4,64,512]{2,1,0:T(8,128)S(1)}, f32[4,64,512]{2,1,0:T(8,128)S(1)}, f32[4,64,512]{2,1,0:T(8,128)S(1)}, f32[1280,128]{1,0:T(8,128)S(1)}, f32[3,4,5...) custom-call(s32[2]{0:T(128)S(1)} %pad_add_fusion.place, f32[768,128]{1,0:T(8,128)S(1)} %bitcast.14, ...), custom_call_target="tpu_custom_call" | custom-call | flops 805306368 | bytes 5242880 | tf_op jit(solution)/shard_map/middle/pallas_call | solution.py:505
  83.4 27.6 %all_to_all.32 = f32[256,1,640]{2,1,0:T(1,128)S(1)} all-to-all(f32[256,1,640]{2,1,0:T(1,128)S(1)} %bitcast.18), channel_id=1, replica_groups=mesh['tm'=32,'space'=8] {'tm','space'}, dimensions={0} | all-to-all | bytes 1310720 | tf_op jit(solution)/shard_map/all_to_all | solution.py:474
  111.0 3.0 %solve.4 = (f32[768,128]{1,0:T(8,128)S(1)}, f32[256,512]{1,0:T(8,128)S(1)}) custom-call(f32[1280,128]{1,0:T(8,128)S(1)} %bitcast.21, bf16[512,512]{1,0:T(8,128)(2,1)S(1)} %copy-done.1, bf16[512,512]{1,0:T(8,128)(2,1)S(1)} %copy-done, bf16[128,128]{1,0:T(8,128)(2,1)S(1)} %copy-done.7, bf16[128,128]{1,0:T(8,128)(2,1)S(1)} %copy-done.6, ...), custom_call_target="tpu_custom_call" | custom-call | flops 1207959552 | bytes 3145728 | tf_op jit(solution)/shard_map/solve/pallas_call | solution.py:495
  114.0 24.3 %all_to_all.33 = f32[256,1,384]{2,1,0:T(1,128)S(1)} all-to-all(f32[256,1,384]{2,1,0:T(1,128)S(1)} %bitcast.24), channel_id=1, replica_groups=mesh['tm'=32,'space'=8] {'tm','space'}, dimensions={0} | all-to-all | bytes 786432 | tf_op jit(solution)/shard_map/all_to_all | solution.py:474
  138.3 7.1 %middle.3 = (f32[4,64,512]{2,1,0:T(8,128)}, f32[4,64,512]{2,1,0:T(8,128)}, f32[4,64,512]{2,1,0:T(8,128)}, f32[1280,128]{1,0:T(8,128)S(1)}, f32[3,4,512]{2,1,0:T(...) custom-call(s32[2]{0:T(128)S(1)} %pad_add_fusion.place, f32[768,128]{1,0:T(8,128)S(1)} %bitcast.15, ...), custom_call_target="tpu_custom_call" | custom-call | flops 805306368 | bytes 5242880 | tf_op jit(solution)/shard_map/middle/pallas_call | solution.py:505
  145.5 27.6 %all_to_all.34 = f32[256,1,640]{2,1,0:T(1,128)S(1)} all-to-all(f32[256,1,640]{2,1,0:T(1,128)S(1)} %bitcast.17), channel_id=1, replica_groups=mesh['tm'=32,'space'=8] {'tm','space'}, dimensions={0} | all-to-all | bytes 1310720 | tf_op jit(solution)/shard_map/all_to_all | solution.py:474
  173.0 2.9 %solve.5 = (f32[768,128]{1,0:T(8,128)S(1)}, f32[256,512]{1,0:T(8,128)}) custom-call(f32[1280,128]{1,0:T(8,128)S(1)} %bitcast.20, bf16[512,512]{1,0:T(8,128)(2,1)S(1)} %copy-done.1, bf16[512,512]{1,0:T(8,128)(2,1)S(1)} %copy-done, bf16[128,128]{1,0:T(8,128)(2,1)S(1)} %copy-done.7, bf16[128,128]{1,0:T(8,128)(2,1)S(1)} %copy-done.6, ...), custom_call_target="tpu_custom_call" | custom-call | flops 1207959552 | bytes 3145728 | tf_op jit(solution)/shard_map/solve/pallas_call | solution.py:495
  176.0 24.3 %all_to_all.35 = f32[256,1,384]{2,1,0:T(1,128)S(1)} all-to-all(f32[256,1,384]{2,1,0:T(1,128)S(1)} %bitcast.23), channel_id=1, replica_groups=mesh['tm'=32,'space'=8] {'tm','space'}, dimensions={0} | all-to-all | bytes 786432 | tf_op jit(solution)/shard_map/all_to_all | solution.py:474
  200.3 2.2 %last.1 = f32[4,64,512]{2,1,0:T(8,128)} custom-call(f32[768,128]{1,0:T(8,128)S(1)} %bitcast.16, f32[512,128]{1,0:T(8,128)S(1)} %get-tuple-element.61.hat_sum, bf16[512,512]{1,0:T(8,128)(2,1)S(1)} %copy-done.1, bf16[512,512]{1,0:T(8,128)(2,1)S(1)} %copy-done, bf16[128,128]{1,0:T(8,128)(2,1)S(1)} %copy-done.5, bf16[128,128]{1,0:T(8,128)(2,1)S(1)} %copy-done.4, ...), custom_call_target="tpu_custom_call" | custom-call | flops 402653184 | bytes 1572864 | tf_op jit(solution)/shard_map/last/pallas_call | solution.py:510
Async XLA Ops:
  1.5 9.7 %collective-permute-start = (f32[3,4,512]{2,1,0:T(4,128)S(1)}, f32[3,4,512]{2,1,0:T(4,128)S(1)}, u32[]{:S(2)}, u32[]{:S(2)}) collective-permute-start(f32[3,4,512]{2,1,0:T(4,128)S(1)} %edges.1), channel_id=1, source_target_pairs={{0,1},{1,2},{2,3},{3,4},{4,5},{5,6},{6,7},{8,9},{9,10},{10,11},{11... | collective-permute-start | bytes 73736 | tf_op jit(solution)/shard_map/ppermute | solution.py:477
  6.2 5.0 %copy-start = (bf16[512,512]{1,0:T(8,128)(2,1)S(1)}, bf16[512,512]{1,0:T(8,128)(2,1)}, u32[]{:S(2)}) copy-start(bf16[512,512]{1,0:T(8,128)(2,1)} %constant.32.clone.cl.refs_2_) | copy-start | bytes 1572868
  6.2 5.0 %copy-start.1 = (bf16[512,512]{1,0:T(8,128)(2,1)S(1)}, bf16[512,512]{1,0:T(8,128)(2,1)}, u32[]{:S(2)}) copy-start(bf16[512,512]{1,0:T(8,128)(2,1)} %constant.31.clone.ch.refs_1_) | copy-start | bytes 1572868
  6.2 5.0 %copy-start.2 = (f32[4,64,512]{2,1,0:T(8,128)S(1)}, f32[4,64,512]{2,1,0:T(8,128)}, u32[]{:S(2)}) copy-start(f32[4,64,512]{2,1,0:T(8,128)} %src.5) | copy-start | bytes 1572868
  13.3 36.4 %copy-start.6 = (bf16[128,128]{1,0:T(8,128)(2,1)S(1)}, bf16[128,128]{1,0:T(8,128)(2,1)}, u32[]{:S(2)}) copy-start(bf16[128,128]{1,0:T(8,128)(2,1)} %constant.34.clone.refs_4_) | copy-start | bytes 98308
  13.3 36.4 %copy-start.7 = (bf16[128,128]{1,0:T(8,128)(2,1)S(1)}, bf16[128,128]{1,0:T(8,128)(2,1)}, u32[]{:S(2)}) copy-start(bf16[128,128]{1,0:T(8,128)(2,1)} %constant.33.clone.refs_3_) | copy-start | bytes 98308
  52.6 24.4 %copy-start.3 = (bf16[128,256]{1,0:T(8,128)(2,1)S(1)}, bf16[128,256]{1,0:T(8,128)(2,1)}, u32[]{:S(2)}) copy-start(bf16[128,256]{1,0:T(8,128)(2,1)} %constant.37.clone.pick) | copy-start | bytes 196612
  52.6 24.4 %copy-start.4 = (bf16[128,128]{1,0:T(8,128)(2,1)S(1)}, bf16[128,128]{1,0:T(8,128)(2,1)}, u32[]{:S(2)}) copy-start(bf16[128,128]{1,0:T(8,128)(2,1)} %constant.36.clone.ql) | copy-start | bytes 98308
  52.6 24.4 %copy-start.5 = (bf16[128,128]{1,0:T(8,128)(2,1)S(1)}, bf16[128,128]{1,0:T(8,128)(2,1)}, u32[]{:S(2)}) copy-start(bf16[128,128]{1,0:T(8,128)(2,1)} %constant.35.clone.qh) | copy-start | bytes 98308

commit v9 on v8

--- a/solution.py
+++ b/solution.py
@@ -492,10 +492,12 @@
     for iteration in range(ITERS):
         modes = exchange(modes)
         carried = (total,) if iteration else ()
-        modes, total = call(
-            functools.partial(solve_body, slabs, places, steps, iteration > 0), [packed(3), square],
-            scratch=[pltpu.VMEM(square, f32)], n_in=6 + len(carried), cost=(3 * mega, 6 * nbytes), name="solve",
+        kept_total = [square] if iteration + 1 < ITERS else []
+        modes, *rest = call(
+            functools.partial(solve_body, slabs, places, steps, iteration > 0), [packed(3)] + kept_total,
+            scratch=[pltpu.VMEM(square, f32)] * (3 - len(kept_total) - 1), n_in=6 + len(carried), cost=(3 * mega, 6 * nbytes), name="solve",
         )(modes, ch, cl, wh, wl, inverse, *carried)
+        total = rest[0] if rest else None
         modes = exchange(modes)
         if iteration + 1 == ITERS:
             break

time: 203 us -> 203 us (level)
  no operation moved by 1% of the time
where the time goes in v9:
time: 203 us
  blocking collectives  165 us (81%)
  Pallas kernels  32.5 us (16%)
  starting transfers between devices  4.57 us (2%)
    all_to_all x6, blocking collectives, exchange(): value = lax.all_to_all(value, BOTH, split_axis=0, concat_axis=0, tiled=True)  165 us
    pallas_call x2, Pallas kernels, local(): call(functools.partial(middle_body, places - 1, screen), [field] * 3 + [p...  13.5 us
    pallas_call x3, Pallas kernels, local(): call(functools.partial(solve_body, slabs, places, steps, iteration > 0),...  8.84 us
    pallas_call x1, Pallas kernels, local(): call(functools.partial(prox_body, screen), [field] * 6 + [hat_shape, squa...  5 us
    ppermute x1, starting transfers between devices, local(): lax.ppermute(last_rows(density, flux_x, flux_y), 'space', [(i, i + 1) for...  4.57 us
  transfers between devices with their start and end apart: 1, of which 0 were waited for; matrix products, arithmetic and copies ran while one was open for 0% of the time, Pallas kernels for 2%

profile of v9, /device:TPU:1, one launch (start us, length us, event | category | flops | bytes accessed | tf_op | source)
XLA Modules:
  0.0 202.7 jit_solution(9440280681706578572)
XLA Ops:
  0.6 0.9 edges.1
  1.5 4.6 %collective-permute-start = (f32[3,4,512]{2,1,0:T(4,128)S(1)}, f32[3,4,512]{2,1,0:T(4,128)S(1)}, u32[]{:S(2)}, u32[]{:S(2)}) collective-permute-start(f32[3,4,512]{2,1,0:T(4,128)S(1)} %edges.1), channel_id=1, source_target_pairs={{0,1},{1,2},{2,3},{3,4},{4,5},{5,6},{6,7},{8,9},{9,10},{10,11},{11... | collective-permute-start | bytes 73736 | tf_op jit(solution)/shard_map/ppermute | solution.py:477
  6.1 0.1 pad_add_fusion.place
  6.2 0.0 copy-start
  6.2 0.0 copy-start.1
  6.2 0.0 copy-start.2
  6.2 5.0 %prox.1 = (f32[4,64,512]{2,1,0:T(8,128)S(1)}, f32[4,64,512]{2,1,0:T(8,128)S(1)}, f32[4,64,512]{2,1,0:T(8,128)S(1)}, f32[4,64,512]{2,1,0:T(8,128)S(1)}, f32[4,64,...) custom-call(s32[2]{0:T(128)S(1)} %pad_add_fusion.place, ...), custom_call_target="tpu_custom_call" | custom-call | flops 26214400 | bytes 3145728 | tf_op jit(solution)/shard_map/prox/pallas_call | solution.py:482
  11.2 0.0 collective-permute-done.edge
  11.2 0.0 copy-done
  11.2 0.0 copy-done.1
  11.3 0.0 copy-done.2
  11.3 2.0 forward.1
  13.3 0.0 copy-start.6
  13.3 0.0 copy-start.7
  13.3 36.4 %all_to_all.30 = f32[256,1,640]{2,1,0:T(1,128)S(1)} all-to-all(f32[256,1,640]{2,1,0:T(1,128)S(1)} %bitcast.19), channel_id=1, replica_groups=mesh['tm'=32,'space'=8] {'tm','space'}, dimensions={0} | all-to-all | bytes 1310720 | tf_op jit(solution)/shard_map/all_to_all | solution.py:474
  49.7 0.0 copy-done.6
  49.7 0.0 copy-done.7
  49.7 2.9 %solve.3 = (f32[768,128]{1,0:T(8,128)S(1)}, f32[256,512]{1,0:T(8,128)S(1)}) custom-call(f32[1280,128]{1,0:T(8,128)S(1)} %bitcast.22, bf16[512,512]{1,0:T(8,128)(2,1)S(1)} %copy-done.1, bf16[512,512]{1,0:T(8,128)(2,1)S(1)} %copy-done, bf16[128,128]{1,0:T(8,128)(2,1)S(1)} %copy-done.7, bf16[128,128]{1,0:T(8,128)(2,1)S(1)} %copy-done.6, ...), custom_call_target="tpu_custom_call" | custom-call | flops 1207959552 | bytes 3145728 | tf_op jit(solution)/shard_map/solve/pallas_call | solution.py:496
  52.6 0.0 copy-start.3
  52.6 0.0 copy-start.4
  52.6 0.0 copy-start.5
  52.6 24.3 %all_to_all.31 = f32[256,1,384]{2,1,0:T(1,128)S(1)} all-to-all(f32[256,1,384]{2,1,0:T(1,128)S(1)} %bitcast.25), channel_id=1, replica_groups=mesh['tm'=32,'space'=8] {'tm','space'}, dimensions={0} | all-to-all | bytes 786432 | tf_op jit(solution)/shard_map/all_to_all | solution.py:474
  77.0 0.0 copy-done.3
  77.0 0.0 copy-done.4
  77.0 0.0 copy-done.5
  77.0 6.4 %middle.2 = (f32[4,64,512]{2,1,0:T(8,128)S(1)}, f32[4,64,512]{2,1,0:T(8,128)S(1)}, f32[4,64,512]{2,1,0:T(8,128)S(1)}, f32[1280,128]{1,0:T(8,128)S(1)}, f32[3,4,5...) custom-call(s32[2]{0:T(128)S(1)} %pad_add_fusion.place, f32[768,128]{1,0:T(8,128)S(1)} %bitcast.14, ...), custom_call_target="tpu_custom_call" | custom-call | flops 805306368 | bytes 5242880 | tf_op jit(solution)/shard_map/middle/pallas_call | solution.py:507
  83.4 27.6 %all_to_all.32 = f32[256,1,640]{2,1,0:T(1,128)S(1)} all-to-all(f32[256,1,640]{2,1,0:T(1,128)S(1)} %bitcast.18), channel_id=1, replica_groups=mesh['tm'=32,'space'=8] {'tm','space'}, dimensions={0} | all-to-all | bytes 1310720 | tf_op jit(solution)/shard_map/all_to_all | solution.py:474
  111.0 3.0 %solve.4 = (f32[768,128]{1,0:T(8,128)S(1)}, f32[256,512]{1,0:T(8,128)S(1)}) custom-call(f32[1280,128]{1,0:T(8,128)S(1)} %bitcast.21, bf16[512,512]{1,0:T(8,128)(2,1)S(1)} %copy-done.1, bf16[512,512]{1,0:T(8,128)(2,1)S(1)} %copy-done, bf16[128,128]{1,0:T(8,128)(2,1)S(1)} %copy-done.7, bf16[128,128]{1,0:T(8,128)(2,1)S(1)} %copy-done.6, ...), custom_call_target="tpu_custom_call" | custom-call | flops 1207959552 | bytes 3145728 | tf_op jit(solution)/shard_map/solve/pallas_call | solution.py:496
  114.0 24.4 %all_to_all.33 = f32[256,1,384]{2,1,0:T(1,128)S(1)} all-to-all(f32[256,1,384]{2,1,0:T(1,128)S(1)} %bitcast.24), channel_id=1, replica_groups=mesh['tm'=32,'space'=8] {'tm','space'}, dimensions={0} | all-to-all | bytes 786432 | tf_op jit(solution)/shard_map/all_to_all | solution.py:474
  138.3 7.1 %middle.3 = (f32[4,64,512]{2,1,0:T(8,128)}, f32[4,64,512]{2,1,0:T(8,128)}, f32[4,64,512]{2,1,0:T(8,128)}, f32[1280,128]{1,0:T(8,128)S(1)}, f32[3,4,512]{2,1,0:T(...) custom-call(s32[2]{0:T(128)S(1)} %pad_add_fusion.place, f32[768,128]{1,0:T(8,128)S(1)} %bitcast.15, ...), custom_call_target="tpu_custom_call" | custom-call | flops 805306368 | bytes 5242880 | tf_op jit(solution)/shard_map/middle/pallas_call | solution.py:507
  145.4 27.6 %all_to_all.34 = f32[256,1,640]{2,1,0:T(1,128)S(1)} all-to-all(f32[256,1,640]{2,1,0:T(1,128)S(1)} %bitcast.17), channel_id=1, replica_groups=mesh['tm'=32,'space'=8] {'tm','space'}, dimensions={0} | all-to-all | bytes 1310720 | tf_op jit(solution)/shard_map/all_to_all | solution.py:474
  173.0 2.9 %solve.5 = f32[768,128]{1,0:T(8,128)S(1)} custom-call(f32[1280,128]{1,0:T(8,128)S(1)} %bitcast.20, bf16[512,512]{1,0:T(8,128)(2,1)S(1)} %copy-done.1, bf16[512,512]{1,0:T(8,128)(2,1)S(1)} %copy-done, bf16[128,128]{1,0:T(8,128)(2,1)S(1)} %copy-done.7, bf16[128,128]{1,0:T(8,128)(2,1)S(1)} %copy-done.6, f32[256,512]{1,0:T(8,128)S(1)} %get-tuple-element.39.refs_5_, ...), custom_call_target="tpu_custom_call" | custom-call | flops 1207959552 | bytes 3145728 | tf_op jit(solution)/shard_map/solve/pallas_call | solution.py:496
  176.0 24.3 %all_to_all.35 = f32[256,1,384]{2,1,0:T(1,128)S(1)} all-to-all(f32[256,1,384]{2,1,0:T(1,128)S(1)} %bitcast.23), channel_id=1, replica_groups=mesh['tm'=32,'space'=8] {'tm','space'}, dimensions={0} | all-to-all | bytes 786432 | tf_op jit(solution)/shard_map/all_to_all | solution.py:474
  200.3 2.2 %last.1 = f32[4,64,512]{2,1,0:T(8,128)} custom-call(f32[768,128]{1,0:T(8,128)S(1)} %bitcast.16, f32[512,128]{1,0:T(8,128)S(1)} %get-tuple-element.59.hat_sum, bf16[512,512]{1,0:T(8,128)(2,1)S(1)} %copy-done.1, bf16[512,512]{1,0:T(8,128)(2,1)S(1)} %copy-done, bf16[128,128]{1,0:T(8,128)(2,1)S(1)} %copy-done.5, bf16[128,128]{1,0:T(8,128)(2,1)S(1)} %copy-done.4, ...), custom_call_target="tpu_custom_call" | custom-call | flops 402653184 | bytes 1572864 | tf_op jit(solution)/shard_map/last/pallas_call | solution.py:512
Async XLA Ops:
  1.5 9.7 %collective-permute-start = (f32[3,4,512]{2,1,0:T(4,128)S(1)}, f32[3,4,512]{2,1,0:T(4,128)S(1)}, u32[]{:S(2)}, u32[]{:S(2)}) collective-permute-start(f32[3,4,512]{2,1,0:T(4,128)S(1)} %edges.1), channel_id=1, source_target_pairs={{0,1},{1,2},{2,3},{3,4},{4,5},{5,6},{6,7},{8,9},{9,10},{10,11},{11... | collective-permute-start | bytes 73736 | tf_op jit(solution)/shard_map/ppermute | solution.py:477
  6.2 5.0 %copy-start = (bf16[512,512]{1,0:T(8,128)(2,1)S(1)}, bf16[512,512]{1,0:T(8,128)(2,1)}, u32[]{:S(2)}) copy-start(bf16[512,512]{1,0:T(8,128)(2,1)} %constant.32.clone.cl.refs_2_) | copy-start | bytes 1572868
  6.2 5.0 %copy-start.1 = (bf16[512,512]{1,0:T(8,128)(2,1)S(1)}, bf16[512,512]{1,0:T(8,128)(2,1)}, u32[]{:S(2)}) copy-start(bf16[512,512]{1,0:T(8,128)(2,1)} %constant.31.clone.ch.refs_1_) | copy-start | bytes 1572868
  6.2 5.0 %copy-start.2 = (f32[4,64,512]{2,1,0:T(8,128)S(1)}, f32[4,64,512]{2,1,0:T(8,128)}, u32[]{:S(2)}) copy-start(f32[4,64,512]{2,1,0:T(8,128)} %src.5) | copy-start | bytes 1572868
  13.3 36.4 %copy-start.6 = (bf16[128,128]{1,0:T(8,128)(2,1)S(1)}, bf16[128,128]{1,0:T(8,128)(2,1)}, u32[]{:S(2)}) copy-start(bf16[128,128]{1,0:T(8,128)(2,1)} %constant.34.clone.refs_4_) | copy-start | bytes 98308
  13.3 36.4 %copy-start.7 = (bf16[128,128]{1,0:T(8,128)(2,1)S(1)}, bf16[128,128]{1,0:T(8,128)(2,1)}, u32[]{:S(2)}) copy-start(bf16[128,128]{1,0:T(8,128)(2,1)} %constant.33.clone.refs_3_) | copy-start | bytes 98308
  52.6 24.4 %copy-start.3 = (bf16[128,256]{1,0:T(8,128)(2,1)S(1)}, bf16[128,256]{1,0:T(8,128)(2,1)}, u32[]{:S(2)}) copy-start(bf16[128,256]{1,0:T(8,128)(2,1)} %constant.37.clone.pick) | copy-start | bytes 196612
  52.6 24.4 %copy-start.4 = (bf16[128,128]{1,0:T(8,128)(2,1)S(1)}, bf16[128,128]{1,0:T(8,128)(2,1)}, u32[]{:S(2)}) copy-start(bf16[128,128]{1,0:T(8,128)(2,1)} %constant.36.clone.ql) | copy-start | bytes 98308
  52.6 24.4 %copy-start.5 = (bf16[128,128]{1,0:T(8,128)(2,1)S(1)}, bf16[128,128]{1,0:T(8,128)(2,1)}, u32[]{:S(2)}) copy-start(bf16[128,128]{1,0:T(8,128)(2,1)} %constant.35.clone.qh) | copy-start | bytes 98308
